TPU v7x, 1024 devices: a whole 4x4x32 slice. The times are simulated.
1024 devices in a mesh: curve: 128 (over x, z), group: 8 (over y, core).
Axes of the slice: x: 4, y: 4, z: 32, core: 2. Of those that a mesh axis runs over, the one named last changes fastest.
Arguments:
- positions: float32 [8, 2048, 3, 128], P('group', 'curve'), may hold values from 0 to 77.2, as said below
- velocities: float32 [8, 2048, 3, 128], P('group', 'curve'), may hold values from -3 to 3
- masses: float32 [8, 2048, 128], P('group', 'curve'), may hold values from 0.003 to 0.03
- counts: int32 [8, 2048], P('group', 'curve'), may hold values from 64 to 128
- neighbours_first: int32 [8, 2048, 6], P('group', 'curve'), may hold values from 0 to 23, as said below
- sends_first: int32 [8, 1024], P('group', 'curve'), may hold values from 0 to 15, as said below
- new_slot: int32 [8, 2048], P('group', 'curve'), may hold values from 0 to 127, as said below
- neighbours_second: int32 [8, 2048, 6], P('group', 'curve'), may hold values from 0 to 23, as said below
- sends_second: int32 [8, 1024], P('group', 'curve'), may hold values from 0 to 15, as said below
Outputs:
- positions_out: float32 [8, 2048, 3, 128], P('group', 'curve')
- velocities_out: float32 [8, 2048, 3, 128], P('group', 'curve')
- densities_out: float32 [8, 2048, 128], P('group', 'curve')
Inputs may be any that keep to these rules, and one draw needn't show every extreme that they name: `positions`: the particles of blocks c * 16 to c * 16 + 15 of every group have first component in [0.6 c, 0.6 c + 1) and other components in [0, 1). `neighbours_first`: A block's list holds 6 distinct candidate numbers, never the block's own slot. `neighbours_second`: A block's list holds 6 distinct candidate numbers, never the block's own slot. `sends_first`: each of a device's two lists of 4 holds distinct slots. `sends_second`: each of a device's two lists of 4 holds distinct slots. For each curve segment, new_slot over all groups' blocks of that segment is a permutation; from one device at most 2 blocks go to any one other group, and in every segment some device sends exactly 2 to some other group.
All inputs are finite; a program needn't handle non-finite values.
Results may differ from a plain program's by a relative error of at most 0.0003.
Values sent between devices are 32-bit elements; how exact they have to be, the bound alone decides.
No kernel may reach another device: no remote copies, remote signals or barrier semaphores. Data moves between devices by JAX's collectives and lax.ppermute only.
A program may use at most 32 MiB of HBM per device.

v0:
```python
import jax
import jax.numpy as jnp
from jax import lax
from jax.sharding import PartitionSpec as P

KERNEL_SCALE = 4.0
SMOOTHING = 0.5
SOFTENING = 0.0025
BACKGROUND = 0.5
TIME_STEP = 0.1


def with_halo(block, sides, width):
    for axis, dim in sides:
        count = lax.axis_size(axis)
        forward = [(i, i + 1) for i in range(count - 1)]
        forward.append((count - 1, 0))
        backward = [(target, source) for source, target in forward]
        low = lax.ppermute(
            lax.slice_in_dim(block, block.shape[dim] - width, None, axis=dim), axis, forward
        )
        high = lax.ppermute(lax.slice_in_dim(block, 0, width, axis=dim), axis, backward)
        block = jnp.concatenate([low, block, high], axis=dim)
    return block


def kernel_density(target_x, source_x, source_mass):
    offsets = [
        target_x[:, None, axis_id, :, None] - source_x[:, :, axis_id, None, :]
        for axis_id in range(3)
    ]
    square = offsets[0] * offsets[0] + offsets[1] * offsets[1] + offsets[2] * offsets[2]
    weight = jnp.exp(-KERNEL_SCALE * square)
    return BACKGROUND + jnp.sum(weight * source_mass[:, :, None, :], axis=(1, 3))


def kernel_force(target_x, target_v, target_rho, source_x, source_v, source_mass, source_rho):
    offsets = [
        target_x[:, None, axis_id, :, None] - source_x[:, :, axis_id, None, :]
        for axis_id in range(3)
    ]
    square = offsets[0] * offsets[0] + offsets[1] * offsets[1] + offsets[2] * offsets[2]
    approach = offsets[0] * (target_v[:, None, 0, :, None] - source_v[:, :, 0, None, :])
    approach = approach + offsets[1] * (target_v[:, None, 1, :, None] - source_v[:, :, 1, None, :])
    approach = approach + offsets[2] * (target_v[:, None, 2, :, None] - source_v[:, :, 2, None, :])
    weight = jnp.exp(-KERNEL_SCALE * square)
    closing = SMOOTHING * jnp.minimum(approach, 0.0) / (square + SOFTENING)
    mine = target_rho[:, None, :, None]
    theirs = source_rho[:, :, None, :]
    factor = source_mass[:, :, None, :] * (
        1.0 / mine + 1.0 / theirs - closing / (0.5 * (mine + theirs))
    )
    factor = factor * (2.0 * KERNEL_SCALE) * weight
    return jnp.stack(
        [jnp.sum(factor * offsets[axis_id], axis=(1, 3)) for axis_id in range(3)], axis=1
    )


def batched(function, arrays):
    shaped = tuple((item.reshape((item.shape[0] // 4, 4) + item.shape[1:]) for item in arrays))
    result = lax.map(lambda piece: function(*piece), shaped)
    return result.reshape((-1,) + result.shape[2:])


def send_positions(field, picks):
    outgoing = jnp.take(field, picks, axis=0)
    half = picks.shape[0] // 2
    arrived = with_halo(outgoing, (("curve", 0),), half)
    return jnp.concatenate([field, arrived[:half], arrived[3 * half :]], axis=0)


def send_returned(field, picks):
    outgoing = jnp.take(field, picks, axis=0)
    half = picks.shape[0] // 2
    arrived = with_halo(outgoing, (("curve", 0),), half)
    return jnp.concatenate([field, arrived[:half], arrived[3 * half :]], axis=0)


def sph_step(positions, velocities, mass_live, neighbours, picks):
    blocks = positions.shape[0]
    own = jnp.arange(blocks, dtype=jnp.int32)[:, None]
    index = jnp.concatenate([own, neighbours], axis=1)
    table = send_positions(
        jnp.concatenate([positions, velocities, mass_live[:, None, :]], axis=1), picks
    )
    table_x = table[:, 0:3]
    table_v = table[:, 3:6]
    table_m = table[:, 6]
    source_x = jnp.take(table_x, index, axis=0)
    source_m = jnp.take(table_m, index, axis=0)
    density = batched(kernel_density, (positions, source_x, source_m))
    table_r = send_returned(density, picks)
    source_v = jnp.take(table_v, index, axis=0)
    source_r = jnp.take(table_r, index, axis=0)
    accel = batched(
        kernel_force, (positions, velocities, density, source_x, source_v, source_m, source_r)
    )
    new_velocity = velocities + TIME_STEP * accel
    new_position = positions + TIME_STEP * new_velocity
    return (new_position, new_velocity, density)


def repartition(packed, new_slot):
    blocks = packed.shape[0]
    group_id = lax.axis_index("group")
    slots = jnp.arange(blocks, dtype=jnp.int32)
    everything, targets = (
        lax.all_gather(packed, "group", axis=0, tiled=True),
        lax.all_gather(new_slot, "group", axis=0, tiled=True),
    )
    wanted = group_id * blocks + slots
    hits = (targets[None, :] == wanted[:, None]).astype(jnp.int32)
    source = jnp.sum(hits * jnp.arange(targets.shape[0], dtype=jnp.int32)[None, :], axis=1)
    return jnp.take(everything, source, axis=0)


def body(
    positions,
    velocities,
    masses,
    counts,
    neighbours_first,
    sends_first,
    new_slot,
    neighbours_second,
    sends_second,
):
    positions = positions[0]
    velocities = velocities[0]
    masses = masses[0]
    counts = counts[0]
    particle_ids = jnp.arange(masses.shape[-1], dtype=jnp.int32)
    live = (particle_ids[None, :] < counts[:, None]).astype(jnp.float32)
    mass_live = masses * live
    first_x, first_v, first_rho = sph_step(
        positions, velocities, mass_live, neighbours_first[0], sends_first[0]
    )
    packed = jnp.concatenate([first_x, first_v, mass_live[:, None, :]], axis=1)
    moved = repartition(packed, new_slot[0])
    final_x, final_v, final_rho = sph_step(
        moved[:, 0:3], moved[:, 3:6], moved[:, 6], neighbours_second[0], sends_second[0]
    )
    return (final_x[None], final_v[None], final_rho[None])


def solution(mesh):
    in_specs = (
        P("group", "curve", None, None),
        P("group", "curve", None, None),
        P("group", "curve", None),
        P("group", "curve"),
        P("group", "curve", None),
        P("group", "curve"),
        P("group", "curve"),
        P("group", "curve", None),
        P("group", "curve"),
    )
    out_specs = (
        P("group", "curve", None, None),
        P("group", "curve", None, None),
        P("group", "curve", None),
    )
    return jax.shard_map(body, mesh=mesh, in_specs=in_specs, out_specs=out_specs, check_vma=False)
```

profile of v0, /device:TPU:1, one launch (start us, length us, event | category | flops | bytes accessed | tf_op | source)
XLA Modules:
  0.0 134.6 jit_solution(18130204171278829383)
XLA Ops:
  4.3 4.4 %collective-permute-start = (f32[4,7,128]{2,1,0:T(8,128)S(1)}, f32[4,7,128]{2,1,0:T(8,128)S(1)}, u32[]{:S(2)}, u32[]{:S(2)}) collective-permute-start(f32[4,7,128]{2,1,0:T(8,128)S(1)} %get-tuple-element.428), channel_id=1, source_target_pairs={{0,8},{8,16},{16,24},{24,32},{32,40},{40,48},{48,56},{56,64},{64,7... | collective-permute-start | bytes 43016 | tf_op jit(solution)/shard_map/ppermute | solution.py:19
  8.7 19.0 %collective-permute-start.1 = (f32[4,7,128]{2,1,0:T(8,128)S(1)}, f32[4,7,128]{2,1,0:T(8,128)S(1)}, u32[]{:S(2)}, u32[]{:S(2)}) collective-permute-start(f32[4,7,128]{2,1,0:T(8,128)S(1)} %get-tuple-element.429), channel_id=1, source_target_pairs={{8,0},{16,8},{24,16},{32,24},{40,32},{48,40},{56,48},{64,56},{72,6... | collective-permute-start | bytes 43016 | tf_op jit(solution)/shard_map/ppermute | solution.py:22
  27.6 1.3 dynamic-slice
  30.3 8.2 %all-reduce = s32[128]{0:T(128)S(1)} all-reduce(s32[128]{0:T(128)S(1)} %bitcast_dynamic-update-slice_fusion.2), channel_id=2, replica_groups=mesh['curve'=128,'group'=8] {'group'}, use_global_device_ids=true, to_apply=%add | all-reduce | flops 128 | bytes 1024
  42.5 4.6 %while.40 = (s32[]{:T(128)}, f32[4,4,128]{2,1,0:T(4,128)S(1)}, f32[4,4,3,128]{3,1,2,0:T(4,128)S(1)}, f32[4,4,7,3,128]{4,1,2,3,0:T(4,128)S(1)}, f32[4,4,7,128]{3,2,1,0:T(8,128)S(1)}, /*index=5*/s32[]{:T(128)}) while((s32[]{:T(128)}, f32[4,4,128]{2,1,0:T(4,128)S(1)}, f32[4,4,3,128]{3,1,2,0:T(4,128)S(1)}, f32[4,4,7,3,128]{4,1,2,3,0:T(4,128)S(1)}, ...), condition=%wide.region_3.7_spmd, body=%wide.region_1.6_spmd.sunk | while | flops 5046274 | bytes 381013 | solution.py:61
  42.6 1.0 multiply_reduce_fusion.4
  43.8 1.0 multiply_reduce_fusion.4
  44.9 1.0 multiply_reduce_fusion.4
  46.1 1.0 multiply_reduce_fusion.4
  47.8 1.9 %collective-permute-start.2 = (f32[4,128]{1,0:T(4,128)S(1)}, f32[4,128]{1,0:T(4,128)S(1)}, u32[]{:S(2)}, u32[]{:S(2)}) collective-permute-start(f32[4,128]{1,0:T(4,128)S(1)} %get-tuple-element.432), channel_id=1, source_target_pairs={{0,8},{8,16},{16,24},{24,32},{32,40},{40,48},{48,56},{56,64},{64,7... | collective-permute-start | bytes 6152 | tf_op jit(solution)/shard_map/ppermute | solution.py:19
  49.7 6.7 %collective-permute-start.3 = (f32[4,128]{1,0:T(4,128)S(1)}, f32[4,128]{1,0:T(4,128)S(1)}, u32[]{:S(2)}, u32[]{:S(2)}) collective-permute-start(f32[4,128]{1,0:T(4,128)S(1)} %get-tuple-element.433), channel_id=1, source_target_pairs={{8,0},{16,8},{24,16},{32,24},{40,32},{48,40},{56,48},{64,56},{72,6... | collective-permute-start | bytes 6152 | tf_op jit(solution)/shard_map/ppermute | solution.py:22
  57.8 14.7 %while.41 = (s32[]{:T(128)}, f32[4,4,3,128]{3,1,2,0:T(4,128)S(1)}, f32[4,4,7,128]{3,2,1,0:T(8,128)S(1)}, f32[4,4,128]{2,1,0:T(4,128)S(1)}, f32[4,4,7,128]{3,2,1,...) while((s32[]{:T(128)}, f32[4,4,3,128]{3,1,2,0:T(4,128)S(1)}, ...), condition=%wide.region_8.13_spmd, body=%wide.region_4.0_spmd.sunk | while | flops 16061954 | bytes 807041 | solution.py:61
  58.1 3.4 %fusion.50 = (f32[4,128]{1,0:T(4,128)S(1)}, f32[4,128]{1,0:T(4,128)S(1)}, f32[4,128]{1,0:T(4,128)S(1)}) fusion(f32[4,7,128]{2,1,0:T(8,128)S(1)} %copy.295, f32[4,128]{1,0:T(4,128)S(1)} %get-tuple-element.666, f32[4,7,128]{2,1,0:T(8,128)S(1)} %get-tuple-element.667, f32[4,128]{1,0:T(4,128)S(1)} %get-tuple-element.668, f32[4,7,128]{2,1,0:T(8,128)S(1)} %copy.296, ...), kind=kLoop, calls=%fused_computation.41.clone.1 | loop fusion | flops 16054784 | bytes 151552 | tf_op jit(solution)/shard_map/while/body/eval_jaxpr/reduce_sum | solution.py:55
  61.8 3.4 %fusion.50 = (f32[4,128]{1,0:T(4,128)S(1)}, f32[4,128]{1,0:T(4,128)S(1)}, f32[4,128]{1,0:T(4,128)S(1)}) fusion(f32[4,7,128]{2,1,0:T(8,128)S(1)} %copy.295, f32[4,128]{1,0:T(4,128)S(1)} %get-tuple-element.666, f32[4,7,128]{2,1,0:T(8,128)S(1)} %get-tuple-element.667, f32[4,128]{1,0:T(4,128)S(1)} %get-tuple-element.668, f32[4,7,128]{2,1,0:T(8,128)S(1)} %copy.296, ...), kind=kLoop, calls=%fused_computation.41.clone.1 | loop fusion | flops 16054784 | bytes 151552 | tf_op jit(solution)/shard_map/while/body/eval_jaxpr/reduce_sum | solution.py:55
  65.5 3.4 %fusion.50 = (f32[4,128]{1,0:T(4,128)S(1)}, f32[4,128]{1,0:T(4,128)S(1)}, f32[4,128]{1,0:T(4,128)S(1)}) fusion(f32[4,7,128]{2,1,0:T(8,128)S(1)} %copy.295, f32[4,128]{1,0:T(4,128)S(1)} %get-tuple-element.666, f32[4,7,128]{2,1,0:T(8,128)S(1)} %get-tuple-element.667, f32[4,128]{1,0:T(4,128)S(1)} %get-tuple-element.668, f32[4,7,128]{2,1,0:T(8,128)S(1)} %copy.296, ...), kind=kLoop, calls=%fused_computation.41.clone.1 | loop fusion | flops 16054784 | bytes 151552 | tf_op jit(solution)/shard_map/while/body/eval_jaxpr/reduce_sum | solution.py:55
  69.1 3.4 %fusion.50 = (f32[4,128]{1,0:T(4,128)S(1)}, f32[4,128]{1,0:T(4,128)S(1)}, f32[4,128]{1,0:T(4,128)S(1)}) fusion(f32[4,7,128]{2,1,0:T(8,128)S(1)} %copy.295, f32[4,128]{1,0:T(4,128)S(1)} %get-tuple-element.666, f32[4,7,128]{2,1,0:T(8,128)S(1)} %get-tuple-element.667, f32[4,128]{1,0:T(4,128)S(1)} %get-tuple-element.668, f32[4,7,128]{2,1,0:T(8,128)S(1)} %copy.296, ...), kind=kLoop, calls=%fused_computation.41.clone.1 | loop fusion | flops 16054784 | bytes 151552 | tf_op jit(solution)/shard_map/while/body/eval_jaxpr/reduce_sum | solution.py:55
  72.7 16.2 %all_gather.7 = f32[128,7,128]{2,0,1:T(8,128)S(1)} all-gather(f32[16,7,128]{2,0,1:T(8,128)S(1)} %copy.233), channel_id=1, replica_groups=mesh['curve'=128,'group'=8] {'group'}, dimensions={0}, use_global_device_ids=true | all-gather | bytes 516096 | tf_op jit(solution)/shard_map/all_gather | solution.py:108
  90.5 1.9 %collective-permute-start.4 = (f32[4,7,128]{2,1,0:T(8,128)S(1)}, f32[4,7,128]{2,1,0:T(8,128)S(1)}, u32[]{:S(2)}, u32[]{:S(2)}) collective-permute-start(f32[4,7,128]{2,1,0:T(8,128)S(1)} %get-tuple-element.426), channel_id=1, source_target_pairs={{0,8},{8,16},{16,24},{24,32},{32,40},{40,48},{48,56},{56,64},{64,7... | collective-permute-start | bytes 43016 | tf_op jit(solution)/shard_map/ppermute | solution.py:19
  92.5 7.2 %collective-permute-start.5 = (f32[4,7,128]{2,1,0:T(8,128)S(1)}, f32[4,7,128]{2,1,0:T(8,128)S(1)}, u32[]{:S(2)}, u32[]{:S(2)}) collective-permute-start(f32[4,7,128]{2,1,0:T(8,128)S(1)} %get-tuple-element.427), channel_id=1, source_target_pairs={{8,0},{16,8},{24,16},{32,24},{40,32},{48,40},{56,48},{64,56},{72,6... | collective-permute-start | bytes 43016 | tf_op jit(solution)/shard_map/ppermute | solution.py:22
  99.7 0.8 collective-permute-done.5
  103.0 4.6 %while.42 = (s32[]{:T(128)}, f32[4,4,128]{2,1,0:T(4,128)S(1)}, f32[4,4,3,128]{3,1,2,0:T(4,128)S(1)}, f32[4,4,7,3,128]{4,1,2,3,0:T(4,128)S(1)}, f32[4,4,7,128]{3,2,1,0:T(8,128)S(1)}, /*index=5*/s32[]{:T(128)}) while((s32[]{:T(128)}, f32[4,4,128]{2,1,0:T(4,128)S(1)}, f32[4,4,3,128]{3,1,2,0:T(4,128)S(1)}, f32[4,4,7,3,128]{4,1,2,3,0:T(4,128)S(1)}, ...), condition=%wide.region_11.16_spmd, body=%wide.region_9.15_spmd.sunk | while | flops 5046274 | bytes 381013 | solution.py:61
  103.1 1.0 multiply_reduce_fusion.5
  104.3 1.0 multiply_reduce_fusion.5
  105.4 1.0 multiply_reduce_fusion.5
  106.6 1.0 multiply_reduce_fusion.5
  108.3 1.9 %collective-permute-start.6 = (f32[4,128]{1,0:T(4,128)S(1)}, f32[4,128]{1,0:T(4,128)S(1)}, u32[]{:S(2)}, u32[]{:S(2)}) collective-permute-start(f32[4,128]{1,0:T(4,128)S(1)} %get-tuple-element.430), channel_id=1, source_target_pairs={{0,8},{8,16},{16,24},{24,32},{32,40},{40,48},{48,56},{56,64},{64,7... | collective-permute-start | bytes 6152 | tf_op jit(solution)/shard_map/ppermute | solution.py:19
  110.2 6.9 %collective-permute-start.7 = (f32[4,128]{1,0:T(4,128)S(1)}, f32[4,128]{1,0:T(4,128)S(1)}, u32[]{:S(2)}, u32[]{:S(2)}) collective-permute-start(f32[4,128]{1,0:T(4,128)S(1)} %get-tuple-element.431), channel_id=1, source_target_pairs={{8,0},{16,8},{24,16},{32,24},{40,32},{48,40},{56,48},{64,56},{72,6... | collective-permute-start | bytes 6152 | tf_op jit(solution)/shard_map/ppermute | solution.py:22
  118.6 14.7 %while.43 = (s32[]{:T(128)}, f32[4,4,3,128]{3,1,2,0:T(4,128)S(1)}, f32[4,4,7,128]{3,2,1,0:T(8,128)S(1)}, f32[4,4,128]{2,1,0:T(4,128)S(1)}, f32[4,4,7,128]{3,2,1,...) while((s32[]{:T(128)}, f32[4,4,3,128]{3,1,2,0:T(4,128)S(1)}, ...), condition=%wide.region_16.21_spmd, body=%wide.region_12.20_spmd.sunk | while | flops 16061954 | bytes 807037 | solution.py:61
  118.9 3.4 %fusion.52 = (f32[4,128]{1,0:T(4,128)S(1)}, f32[4,128]{1,0:T(4,128)S(1)}, f32[4,128]{1,0:T(4,128)S(1)}) fusion(f32[4,7,128]{2,1,0:T(8,128)S(1)} %copy.304, f32[4,128]{1,0:T(4,128)S(1)} %get-tuple-element.708, f32[4,7,128]{2,1,0:T(8,128)S(1)} %get-tuple-element.709, f32[4,128]{1,0:T(4,128)S(1)} %get-tuple-element.710, f32[4,7,128]{2,1,0:T(8,128)S(1)} %copy.305, ...), kind=kLoop, calls=%fused_computation.101.clone.1 | loop fusion | flops 16054784 | bytes 151552 | tf_op jit(solution)/shard_map/while/body/eval_jaxpr/reduce_sum | solution.py:55
  122.5 3.4 %fusion.52 = (f32[4,128]{1,0:T(4,128)S(1)}, f32[4,128]{1,0:T(4,128)S(1)}, f32[4,128]{1,0:T(4,128)S(1)}) fusion(f32[4,7,128]{2,1,0:T(8,128)S(1)} %copy.304, f32[4,128]{1,0:T(4,128)S(1)} %get-tuple-element.708, f32[4,7,128]{2,1,0:T(8,128)S(1)} %get-tuple-element.709, f32[4,128]{1,0:T(4,128)S(1)} %get-tuple-element.710, f32[4,7,128]{2,1,0:T(8,128)S(1)} %copy.305, ...), kind=kLoop, calls=%fused_computation.101.clone.1 | loop fusion | flops 16054784 | bytes 151552 | tf_op jit(solution)/shard_map/while/body/eval_jaxpr/reduce_sum | solution.py:55
  126.2 3.4 %fusion.52 = (f32[4,128]{1,0:T(4,128)S(1)}, f32[4,128]{1,0:T(4,128)S(1)}, f32[4,128]{1,0:T(4,128)S(1)}) fusion(f32[4,7,128]{2,1,0:T(8,128)S(1)} %copy.304, f32[4,128]{1,0:T(4,128)S(1)} %get-tuple-element.708, f32[4,7,128]{2,1,0:T(8,128)S(1)} %get-tuple-element.709, f32[4,128]{1,0:T(4,128)S(1)} %get-tuple-element.710, f32[4,7,128]{2,1,0:T(8,128)S(1)} %copy.305, ...), kind=kLoop, calls=%fused_computation.101.clone.1 | loop fusion | flops 16054784 | bytes 151552 | tf_op jit(solution)/shard_map/while/body/eval_jaxpr/reduce_sum | solution.py:55
  129.9 3.4 %fusion.52 = (f32[4,128]{1,0:T(4,128)S(1)}, f32[4,128]{1,0:T(4,128)S(1)}, f32[4,128]{1,0:T(4,128)S(1)}) fusion(f32[4,7,128]{2,1,0:T(8,128)S(1)} %copy.304, f32[4,128]{1,0:T(4,128)S(1)} %get-tuple-element.708, f32[4,7,128]{2,1,0:T(8,128)S(1)} %get-tuple-element.709, f32[4,128]{1,0:T(4,128)S(1)} %get-tuple-element.710, f32[4,7,128]{2,1,0:T(8,128)S(1)} %copy.305, ...), kind=kLoop, calls=%fused_computation.101.clone.1 | loop fusion | flops 16054784 | bytes 151552 | tf_op jit(solution)/shard_map/while/body/eval_jaxpr/reduce_sum | solution.py:55
  (309 shorter events, 19.1 us)
Async XLA Ops:
  0.6 39.2 %copy-start.2 = (f32[1,16,3,128]{3,1,2,0:T(8,128)S(1)}, f32[1,16,3,128]{3,1,2,0:T(8,128)}, u32[]{:S(2)}) copy-start(f32[1,16,3,128]{3,1,2,0:T(8,128)} %param.25) | copy-start | bytes 73732
  0.6 38.8 %copy-start.5 = (s32[1,8]{1,0:T(1,128)S(1)}, s32[1,8]{1,0:T(1,128)}, u32[]{:S(2)}) copy-start(s32[1,8]{1,0:T(1,128)} %param.33) | copy-start | bytes 100
  0.7 38.8 %copy-start.4 = (s32[1,16,6]{1,0,2:T(1,128)S(1)}, s32[1,16,6]{1,0,2:T(1,128)}, u32[]{:S(2)}) copy-start(s32[1,16,6]{1,0,2:T(1,128)} %param.29) | copy-start | bytes 1156
  0.7 38.8 %copy-start.3 = (s32[1,16,6]{1,0,2:T(1,128)S(1)}, s32[1,16,6]{1,0,2:T(1,128)}, u32[]{:S(2)}) copy-start(s32[1,16,6]{1,0,2:T(1,128)} %param.32) | copy-start | bytes 1156
  4.3 35.7 %collective-permute-start = (f32[4,7,128]{2,1,0:T(8,128)S(1)}, f32[4,7,128]{2,1,0:T(8,128)S(1)}, u32[]{:S(2)}, u32[]{:S(2)}) collective-permute-start(f32[4,7,128]{2,1,0:T(8,128)S(1)} %get-tuple-element.428), channel_id=1, source_target_pairs={{0,8},{8,16},{16,24},{24,32},{32,40},{40,48},{48,56},{56,64},{64,7... | collective-permute-start | bytes 43016 | tf_op jit(solution)/shard_map/ppermute | solution.py:19
  8.7 31.3 %collective-permute-start.1 = (f32[4,7,128]{2,1,0:T(8,128)S(1)}, f32[4,7,128]{2,1,0:T(8,128)S(1)}, u32[]{:S(2)}, u32[]{:S(2)}) collective-permute-start(f32[4,7,128]{2,1,0:T(8,128)S(1)} %get-tuple-element.429), channel_id=1, source_target_pairs={{8,0},{16,8},{24,16},{32,24},{40,32},{48,40},{56,48},{64,56},{72,6... | collective-permute-start | bytes 43016 | tf_op jit(solution)/shard_map/ppermute | solution.py:22
  47.8 8.8 %collective-permute-start.2 = (f32[4,128]{1,0:T(4,128)S(1)}, f32[4,128]{1,0:T(4,128)S(1)}, u32[]{:S(2)}, u32[]{:S(2)}) collective-permute-start(f32[4,128]{1,0:T(4,128)S(1)} %get-tuple-element.432), channel_id=1, source_target_pairs={{0,8},{8,16},{16,24},{24,32},{32,40},{40,48},{48,56},{56,64},{64,7... | collective-permute-start | bytes 6152 | tf_op jit(solution)/shard_map/ppermute | solution.py:19
  49.7 7.4 %collective-permute-start.3 = (f32[4,128]{1,0:T(4,128)S(1)}, f32[4,128]{1,0:T(4,128)S(1)}, u32[]{:S(2)}, u32[]{:S(2)}) collective-permute-start(f32[4,128]{1,0:T(4,128)S(1)} %get-tuple-element.433), channel_id=1, source_target_pairs={{8,0},{16,8},{24,16},{32,24},{40,32},{48,40},{56,48},{64,56},{72,6... | collective-permute-start | bytes 6152 | tf_op jit(solution)/shard_map/ppermute | solution.py:22
  56.5 1.3 copy-start.1
  90.5 9.2 %collective-permute-start.4 = (f32[4,7,128]{2,1,0:T(8,128)S(1)}, f32[4,7,128]{2,1,0:T(8,128)S(1)}, u32[]{:S(2)}, u32[]{:S(2)}) collective-permute-start(f32[4,7,128]{2,1,0:T(8,128)S(1)} %get-tuple-element.426), channel_id=1, source_target_pairs={{0,8},{8,16},{16,24},{24,32},{32,40},{40,48},{48,56},{56,64},{64,7... | collective-permute-start | bytes 43016 | tf_op jit(solution)/shard_map/ppermute | solution.py:19
  92.5 8.1 %collective-permute-start.5 = (f32[4,7,128]{2,1,0:T(8,128)S(1)}, f32[4,7,128]{2,1,0:T(8,128)S(1)}, u32[]{:S(2)}, u32[]{:S(2)}) collective-permute-start(f32[4,7,128]{2,1,0:T(8,128)S(1)} %get-tuple-element.427), channel_id=1, source_target_pairs={{8,0},{16,8},{24,16},{32,24},{40,32},{48,40},{56,48},{64,56},{72,6... | collective-permute-start | bytes 43016 | tf_op jit(solution)/shard_map/ppermute | solution.py:22
  108.3 8.9 %collective-permute-start.6 = (f32[4,128]{1,0:T(4,128)S(1)}, f32[4,128]{1,0:T(4,128)S(1)}, u32[]{:S(2)}, u32[]{:S(2)}) collective-permute-start(f32[4,128]{1,0:T(4,128)S(1)} %get-tuple-element.430), channel_id=1, source_target_pairs={{0,8},{8,16},{16,24},{24,32},{32,40},{40,48},{48,56},{56,64},{64,7... | collective-permute-start | bytes 6152 | tf_op jit(solution)/shard_map/ppermute | solution.py:19
  110.2 7.7 %collective-permute-start.7 = (f32[4,128]{1,0:T(4,128)S(1)}, f32[4,128]{1,0:T(4,128)S(1)}, u32[]{:S(2)}, u32[]{:S(2)}) collective-permute-start(f32[4,128]{1,0:T(4,128)S(1)} %get-tuple-element.431), channel_id=1, source_target_pairs={{8,0},{16,8},{24,16},{32,24},{40,32},{48,40},{56,48},{64,56},{72,6... | collective-permute-start | bytes 6152 | tf_op jit(solution)/shard_map/ppermute | solution.py:22
  133.3 1.3 copy-start
where the time goes:
time: 135 us
  starting transfers between devices  49.9 us (37%)
  other arithmetic  40 us (30%)
  blocking collectives  24.4 us (18%)
  local copies, waits for them, and re-layouts  14.6 us (11%)
  waiting for transfers between devices  1.97 us (1%)
  between operations  1.92 us (1%)
  loops' own time  1.78 us (1%)
    ppermute x4, starting transfers between devices, with_halo(): lax.ppermute(lax.slice_in_dim(block, 0, width, axis=dim), axis, backward)  39.8 us
    reduce_sum x8, other arithmetic, kernel_force(): jnp.sum(factor * offsets[axis_id], axis=(1, 3))  27.3 us
    all_gather x1, blocking collectives, repartition(): lax.all_gather(packed, 'group', axis=0, tiled=True)  16.2 us
    ppermute x4, starting transfers between devices, with_halo(): lax.ppermute(lax.slice_in_dim(block, block.shape[dim] - width, None, axis...  10.1 us
    unnamed x1, blocking collectives  8.21 us
    reduce_sum x8, other arithmetic, kernel_density(): jnp.sum(weight * source_mass[:, :, None, :], axis=(1, 3))  8.05 us
    unnamed x18, local copies, waits for them, and re-layouts  3.29 us
  transfers between devices with their start and end apart: 8, of which 3 were waited for; matrix products, arithmetic and copies ran while one was open for 3% of the time, Pallas kernels for 0%

commit v1 on v0

v1 whole, which is shorter than its diff:
```python
import math

import jax
import jax.numpy as jnp
from jax import lax
from jax.experimental import pallas as pl
from jax.experimental.pallas import tpu as pltpu
from jax.sharding import PartitionSpec as P

SOFTENING = 0.0025
BACKGROUND = 0.5
TIME_STEP = 0.1
SPACING = 0.6

BLOCKS = 16
HALO = 4
NBR = 6
CANDIDATES = BLOCKS + 2 * HALO
LANES = 128
FEATURES = 64
MOVES = 2
KAPPA = 4.0 * math.log2(math.e)
MASS_SCALE = 2.0 ** (KAPPA * SOFTENING)
FORCE_SCALE = 8.0 * MASS_SCALE

F32 = jnp.float32
BF16 = jnp.bfloat16
VMEM = pl.BlockSpec(memory_space=pltpu.VMEM)
SMEM = pl.BlockSpec(memory_space=pltpu.SMEM)


def rounded(value):
    return value.astype(BF16).astype(F32)


def split(value):
    high = rounded(value)
    rest = value - high
    middle = rounded(rest)
    return high, middle, rest - middle


def tile_rows():
    return lax.broadcasted_iota(jnp.int32, (8, LANES), 0)


def three_rows(rows, first, parts):
    return jnp.where(
        rows == first, parts[0], jnp.where(rows == first + 1, parts[1], jnp.where(rows == first + 2, parts[2], 0.0))
    )


def local_tile(tile, base, rows):
    shifted = jnp.where(rows == 0, tile - base, tile)
    return jnp.where(rows < 6, shifted, 0.0)


def swapped(local, rows):
    down = pltpu.roll(local, 5, axis=0)
    up = pltpu.roll(local, 3, axis=0)
    return jnp.where(rows < 3, down, jnp.where(rows < 6, up, 0.0))


def quadratics(local, other, rows):
    square = jnp.sum(jnp.where(rows < 3, local * local, 0.0), axis=0, keepdims=True)
    mixed = jnp.sum(jnp.where(rows < 3, local * other, 0.0), axis=0, keepdims=True)
    return square, mixed


def source_features(tile, base, rows):
    local = local_tile(tile, base, rows)
    other = swapped(local, rows)
    square, mixed = quadratics(local, other, rows)
    near = split(jnp.where(rows < 3, (2.0 * KAPPA) * local, 0.0))
    flow = split(-KAPPA * other)
    minus = jnp.where(rows < 3, -1.0, 0.0)
    plus = jnp.where((rows >= 3) & (rows < 6), 1.0, 0.0)
    last_near = three_rows(rows, 0, split(-KAPPA * (square + SOFTENING)))
    last_flow = three_rows(rows, 0, split(KAPPA * mixed))
    first = jnp.concatenate([near[0], near[1], near[2], near[0], near[1], near[0], minus, last_near], axis=0)
    second = jnp.concatenate([flow[0], flow[1], flow[2], flow[0], flow[1], flow[0], plus, last_flow], axis=0)
    mass = tile[6:7] * FORCE_SCALE
    weights = split(mass * jnp.where(rows < 3, local, jnp.where(rows == 3, 1.0, 0.0)))
    summed = jnp.concatenate([weights[0], weights[1], weights[2], jnp.zeros_like(local)], axis=0)
    return first.astype(BF16), second.astype(BF16), summed.astype(BF16)


def target_features(tile, base, rows):
    local = local_tile(tile, base, rows)
    other = swapped(local, rows)
    square, mixed = quadratics(local, other, rows)
    high, middle, low = split(local)
    quadratic = three_rows(rows, 0, split(KAPPA * square)) + three_rows(rows, 3, split(KAPPA * mixed))
    ones = jnp.where(rows < 3, 1.0, 0.0)
    stacked = jnp.concatenate([high, high, high, middle, middle, low, quadratic, ones], axis=0)
    return stacked.T.astype(BF16)


def base_of_segment():
    return SPACING * lax.axis_index("curve").astype(F32)


def list_blocks(table_ref, picks_ref, low_ref, high_ref):
    for h in range(HALO):
        low_ref[h] = table_ref[picks_ref[0, h]]
        high_ref[h] = table_ref[picks_ref[0, HALO + h]]


def gather_kernel(x_ref, v_ref, m_ref, counts_ref, picks_ref, table_ref, low_ref, high_ref, flat_ref):
    for axis_id in range(3):
        flat_ref[pl.ds(axis_id, BLOCKS, stride=8), :] = x_ref[axis_id]
        flat_ref[pl.ds(3 + axis_id, BLOCKS, stride=8), :] = v_ref[axis_id]
    lane = lax.broadcasted_iota(jnp.int32, (1, LANES), 1)
    for b in range(BLOCKS):
        live = jnp.where(lane < counts_ref[0, b], m_ref[pl.ds(b, 1), :], 0.0)
        flat_ref[pl.ds(8 * b + 6, 1), :] = live
        flat_ref[pl.ds(8 * b + 7, 1), :] = jnp.zeros_like(live)
    for b in range(BLOCKS):
        table_ref[b] = flat_ref[pl.ds(8 * b, 8), :]
    list_blocks(table_ref, picks_ref, low_ref, high_ref)


def density_kernel(
    table_ref, below_ref, above_ref, near_ref, picks_ref,
    rho_ref, low_ref, high_ref, pair_ref, target_ref, sum_ref, mass_ref,
):
    base = base_of_segment()
    rows = tile_rows()

    def put(tile, at):
        first, second, summed = source_features(tile, base, rows)
        pair_ref[at, :, 0:LANES] = first
        pair_ref[at, :, LANES : 2 * LANES] = second
        sum_ref[at] = summed
        mass_ref[at] = tile[6:7] * MASS_SCALE

    def own(b, carry):
        tile = table_ref[b]
        put(tile, b)
        target_ref[b] = target_features(tile, base, rows)
        return carry

    lax.fori_loop(0, BLOCKS, own, 0, unroll=4)
    for h in range(HALO):
        put(below_ref[h], BLOCKS + h)
        put(above_ref[h], BLOCKS + HALO + h)

    ones = jnp.ones((8, LANES), F32)

    def target(j, carry):
        left = target_ref[j]
        sources = [j] + [near_ref[n, 0, j] for n in range(NBR)]
        total = jnp.zeros((LANES, LANES), F32)
        for start in range(0, NBR + 1, 2):
            chosen = sources[start : start + 2]
            right = [pair_ref[s, :, 0:LANES] for s in chosen]
            right = right[0] if len(right) == 1 else jnp.concatenate(right, axis=1)
            weight = jnp.exp2(jnp.dot(left, right, preferred_element_type=F32))
            for n, s in enumerate(chosen):
                total = total + weight[:, n * LANES : (n + 1) * LANES] * mass_ref[s]
        row = lax.dot_general(
            ones, total, (((1,), (1,)), ((), ())), precision=lax.Precision.HIGHEST, preferred_element_type=F32
        )
        rho_ref[j] = BACKGROUND + row[0:1]
        return carry

    lax.fori_loop(0, BLOCKS, target, 0)
    for h in range(HALO):
        low_ref[pl.ds(h, 1), :] = rho_ref[picks_ref[0, h]]
        high_ref[pl.ds(h, 1), :] = rho_ref[picks_ref[0, HALO + h]]


def advance(table_ref, rho_ref, below_ref, above_ref, near_ref, pair_ref, target_ref, sum_ref, all_rho, columns, done):
    base = base_of_segment()
    rows = tile_rows()
    flat = jnp.concatenate([rho_ref[b] for b in range(BLOCKS)], axis=0)
    for b in range(BLOCKS):
        all_rho[b] = rho_ref[b]
    for h in range(HALO):
        all_rho[BLOCKS + h] = below_ref[pl.ds(h, 1), :]
        all_rho[BLOCKS + HALO + h] = above_ref[pl.ds(h, 1), :]
    columns[...] = jnp.concatenate([flat, jnp.ones((LANES - BLOCKS, LANES), F32)], axis=0).T
    lane = lax.broadcasted_iota(jnp.int32, (LANES, LANES), 1)

    def target(j, carry):
        left = target_ref[j]
        mine = jnp.sum(jnp.where(lane == j, columns[...], 0.0), axis=1, keepdims=True)
        mine_inverse = 1.0 / mine
        sources = [j] + [near_ref[n, 0, j] for n in range(NBR)]
        total = jnp.zeros((32, LANES), F32)
        for s in sources:
            product = jnp.dot(left, pair_ref[s], preferred_element_type=F32)
            distance = product[:, 0:LANES]
            approach = product[:, LANES : 2 * LANES]
            theirs = all_rho[s]
            closing = jnp.minimum(approach, 0.0) / (distance * (mine + theirs))
            factor = jnp.exp2(distance) * (closing + (mine_inverse + 1.0 / theirs))
            high = factor.astype(BF16)
            low = (factor - high.astype(F32)).astype(BF16)
            weights = sum_ref[s]
            for part in (high, low):
                total = total + lax.dot_general(
                    weights, part, (((1,), (1,)), ((), ())), preferred_element_type=F32
                )
        sums = total[0:8] + total[8:16] + total[16:24]
        tile = table_ref[j]
        local = local_tile(tile, base, rows)
        accel = jnp.where(rows < 3, local * sums[3:4] - sums, 0.0)
        kicked = tile + TIME_STEP * pltpu.roll(accel, 3, axis=0)
        drift = pltpu.roll(kicked, 5, axis=0)
        done(j, jnp.where(rows < 3, kicked + TIME_STEP * drift, kicked))
        return carry

    lax.fori_loop(0, BLOCKS, target, 0)


def force_move_kernel(
    table_ref, rho_ref, below_ref, above_ref, near_ref, pair_ref, target_ref, sum_ref, slot_ref,
    stay_ref, send_ref, all_rho, columns, filled,
):
    me = lax.axis_index("group")
    rows = tile_rows()
    groups = send_ref.shape[0]
    for g in range(groups):
        filled[g] = 0
        for k in range(MOVES):
            send_ref[g, k] = jnp.full((8, LANES), -1.0, F32)
    for b in range(BLOCKS):
        stay_ref[b] = jnp.zeros((8, LANES), F32)

    def done(b, tile):
        owner = slot_ref[0, b] // BLOCKS
        slot = slot_ref[0, b] % BLOCKS
        tagged = jnp.where(rows == 7, jnp.full((8, LANES), slot, jnp.int32).astype(F32), tile)

        @pl.when(owner == me)
        def _():
            stay_ref[slot] = tagged

        @pl.when(owner != me)
        def _():
            place = jnp.minimum(filled[owner], MOVES - 1)
            send_ref[owner, place] = tagged
            filled[owner] = place + 1

    advance(
        table_ref, rho_ref, below_ref, above_ref, near_ref, pair_ref, target_ref, sum_ref, all_rho, columns, done
    )


def arrive_kernel(stay_ref, arrived_ref, picks_ref, table_ref, low_ref, high_ref):
    groups = arrived_ref.shape[0]
    tiles = [arrived_ref[g, k] for g in range(groups) for k in range(MOVES)]
    tags = [jnp.broadcast_to(tile[7:8], (8, LANES)) for tile in tiles]
    for s in range(BLOCKS):
        value = stay_ref[s]
        for tile, tag in zip(tiles, tags):
            value = jnp.where(tag == float(s), tile, value)
        table_ref[s] = value
    list_blocks(table_ref, picks_ref, low_ref, high_ref)


def force_out_kernel(
    table_ref, rho_ref, below_ref, above_ref, near_ref, pair_ref, target_ref, sum_ref,
    x_ref, v_ref, all_rho, columns, flat_ref,
):
    def done(b, tile):
        flat_ref[pl.ds(pl.multiple_of(8 * b, 8), 8), :] = tile

    advance(
        table_ref, rho_ref, below_ref, above_ref, near_ref, pair_ref, target_ref, sum_ref, all_rho, columns, done
    )
    for axis_id in range(3):
        x_ref[axis_id] = flat_ref[pl.ds(axis_id, BLOCKS, stride=8), :]
        v_ref[axis_id] = flat_ref[pl.ds(3 + axis_id, BLOCKS, stride=8), :]


def shape(*dims, dtype=F32):
    return jax.ShapeDtypeStruct(dims, dtype)


TABLE = shape(BLOCKS, 8, LANES)
LISTED = shape(HALO, 8, LANES)


def call(kernel, name, out_shape, in_specs, scratch=(), flops=0):
    return pl.pallas_call(
        kernel,
        name=name,
        out_shape=out_shape,
        in_specs=in_specs,
        out_specs=[VMEM] * len(out_shape),
        scratch_shapes=list(scratch),
        cost_estimate=pl.CostEstimate(flops=flops, bytes_accessed=200000, transcendentals=0),
    )


def exchange(low, high):
    count = lax.axis_size("curve")
    forward = [(i, (i + 1) % count) for i in range(count)]
    backward = [(target, source) for source, target in forward]
    return lax.ppermute(high, "curve", forward), lax.ppermute(low, "curve", backward)


def half_step(table, below, above, near, picks):
    rho, low, high, pairs, targets, sums = call(
        density_kernel,
        "density",
        (
            shape(BLOCKS, 1, LANES),
            shape(HALO, LANES),
            shape(HALO, LANES),
            shape(CANDIDATES, FEATURES, 2 * LANES, dtype=BF16),
            shape(BLOCKS, LANES, FEATURES, dtype=BF16),
            shape(CANDIDATES, 32, LANES, dtype=BF16),
        ),
        [VMEM, VMEM, VMEM, SMEM, SMEM],
        [pltpu.VMEM((CANDIDATES, 1, LANES), F32)],
    )(table, below, above, near, picks)
    rho_below, rho_above = exchange(low, high)
    return (table, rho, rho_below, rho_above, near, pairs, targets, sums)


FORCE_SPECS = [VMEM, VMEM, VMEM, VMEM, SMEM, VMEM, VMEM, VMEM]
FORCE_SCRATCH = [pltpu.VMEM((CANDIDATES, 1, LANES), F32), pltpu.VMEM((LANES, LANES), F32)]


def body(x, v, masses, counts, near_first, picks_first, new_slot, near_second, picks_second):
    groups = lax.axis_size("group")
    near_first = jnp.transpose(near_first, (2, 0, 1))
    near_second = jnp.transpose(near_second, (2, 0, 1))
    table, low, high = call(
        gather_kernel,
        "gather",
        (TABLE, LISTED, LISTED),
        [VMEM, VMEM, VMEM, SMEM, SMEM],
        [pltpu.VMEM((8 * BLOCKS, LANES), F32)],
    )(jnp.transpose(x[0], (1, 0, 2)), jnp.transpose(v[0], (1, 0, 2)), masses[0], counts, picks_first)
    below, above = exchange(low, high)
    stay, send = call(
        force_move_kernel,
        "force_move",
        (TABLE, shape(groups, MOVES, 8, LANES)),
        FORCE_SPECS + [SMEM],
        FORCE_SCRATCH + [pltpu.SMEM((groups,), jnp.int32)],
    )(*half_step(table, below, above, near_first, picks_first), new_slot)
    arrived = lax.all_to_all(send, "group", 0, 0)
    table, low, high = call(
        arrive_kernel, "arrive", (TABLE, LISTED, LISTED), [VMEM, VMEM, SMEM]
    )(stay, arrived, picks_second)
    below, above = exchange(low, high)
    state = half_step(table, below, above, near_second, picks_second)
    x_out, v_out = call(
        force_out_kernel,
        "force_out",
        (shape(3, BLOCKS, LANES), shape(3, BLOCKS, LANES)),
        FORCE_SPECS,
        FORCE_SCRATCH + [pltpu.VMEM((8 * BLOCKS, LANES), F32)],
    )(*state)
    rho = state[1].reshape(1, BLOCKS, LANES)
    return jnp.transpose(x_out, (1, 0, 2))[None], jnp.transpose(v_out, (1, 0, 2))[None], rho


def solution(mesh):
    in_specs = (
        P("group", "curve", None, None),
        P("group", "curve", None, None),
        P("group", "curve", None),
        P("group", "curve"),
        P("group", "curve", None),
        P("group", "curve"),
        P("group", "curve"),
        P("group", "curve", None),
        P("group", "curve"),
    )
    out_specs = (
        P("group", "curve", None, None),
        P("group", "curve", None, None),
        P("group", "curve", None),
    )
    return jax.shard_map(body, mesh=mesh, in_specs=in_specs, out_specs=out_specs, check_vma=False)
```

time: 135 us -> 138 us (1.022)
  Pallas kernels: 0 us -> 67.7 us
  other arithmetic: 40 us -> 0 us
  blocking collectives: 24.4 us -> 12.1 us
  local copies, waits for them, and re-layouts: 14.6 us -> 2.38 us
  loops' own time: 1.78 us -> 0 us
  waiting for transfers between devices: 1.97 us -> 3.47 us
    pallas_call x0 -> x6, Pallas kernels: none -> 67.7 us  [the longest x1 23.3 us: body(): call(force_move_kernel, 'force_move', (TABLE, shape(groups, MOVES, 8, LAN...]
    reduce_sum x17 -> x0, other arithmetic: 35.5 us -> none  [the longest x8 27.3 us: kernel_force(): jnp.sum(factor * offsets[axis_id], axis=(1, 3))]
    all_gather x1 -> x0, blocking collectives: 16.2 us -> none  [repartition(): lax.all_gather(packed, 'group', axis=0, tiled=True)]
    all_to_all x0 -> x1, blocking collectives: none -> 12.1 us  [body(): arrived = lax.all_to_all(send, 'group', 0, 0)]
    gather x17 -> x0, local copies, waits for them, and re-layouts: 8.26 us -> none  [the longest x2 1.46 us: sph_step(): source_v = jnp.take(table_v, index, axis=0)]
    unnamed x1 -> x0, blocking collectives: 8.21 us -> none
    select_n x14 -> x0, other arithmetic: 2.27 us -> none  [the longest x4 1.49 us: send_positions(): outgoing = jnp.take(field, picks, axis=0)]
    another operation x4 -> x0, loops' own time: 1.78 us -> none  [batched(): result = lax.map(lambda piece: function(*piece), shaped)]
  transfers between devices with their start and end apart: 8 -> 8, of which waited for: 3 -> 4; matrix products, arithmetic and copies ran while one was open for 3% -> 0% of each run, Pallas kernels for 0% -> 0%
where the time goes in v1:
time: 138 us; the launch traced here: 137 us
  Pallas kernels  67.7 us (49%)
  starting transfers between devices  50.4 us (37%)
  blocking collectives  12.1 us (9%)
  waiting for transfers between devices  3.47 us (3%)
  local copies, waits for them, and re-layouts  2.38 us (2%)
    ppermute x4, starting transfers between devices, exchange(): lax.ppermute(low, 'curve', backward)  40.1 us
    pallas_call x1, Pallas kernels, body(): call(force_move_kernel, 'force_move', (TABLE, shape(groups, MOVES, 8, LAN...  23.3 us
    pallas_call x1, Pallas kernels, body(): call(force_out_kernel, 'force_out', (shape(3, BLOCKS, LANES), shape(3, BL...  23.3 us
    pallas_call x2, Pallas kernels, half_step(): call(density_kernel, 'density', (shape(BLOCKS, 1, LANES), shape(HALO, LAN...  18.1 us
    all_to_all x1, blocking collectives, body(): arrived = lax.all_to_all(send, 'group', 0, 0)  12.1 us
    ppermute x4, starting transfers between devices, exchange(): lax.ppermute(high, 'curve', forward)  10.3 us
    ppermute x4, waiting for transfers between devices, exchange(): lax.ppermute(low, 'curve', backward)  3.45 us
  transfers between devices with their start and end apart: 8, of which 4 were waited for; matrix products, arithmetic and copies ran while one was open for 0% of the time, Pallas kernels for 0%

profile of v1, /device:TPU:1, one launch (start us, length us, event | category | flops | bytes accessed | tf_op | source)
XLA Modules:
  0.0 136.9 jit_solution(5027411278611460951)
XLA Ops:
  0.6 1.5 %gather.1 = (f32[16,8,128]{2,1,0:T(8,128)}, f32[4,8,128]{2,1,0:T(8,128)}, f32[4,8,128]{2,1,0:T(8,128)}) custom-call(f32[3,16,128]{2,1,0:T(8,128)} %bitcast.16, f32[3,16,128]{2,1,0:T(8,128)} %bitcast.17, f32[16,128]{1,0:T(8,128)} %bitcast.23, s32[1,16]{1,0:T(1,128)} %counts_ref.1, s32[1,8]{1,0:T(1,128)} %picks_ref.5), custom_call_target="tpu_custom_call" | custom-call | bytes 200000 | tf_op jit(solution)/shard_map/gather/pallas_call | solution.py:332
  2.1 4.4 %collective-permute-start = (f32[4,8,128]{2,1,0:T(8,128)}, f32[4,8,128]{2,1,0:T(8,128)S(1)}, u32[]{:S(2)}, u32[]{:S(2)}) collective-permute-start(f32[4,8,128]{2,1,0:T(8,128)} %get-tuple-element.26), channel_id=1, source_target_pairs={{0,8},{8,16},{16,24},{24,32},{32,40},{40,48},{48,56},{56,64},{64,7... | collective-permute-start | bytes 49160 | tf_op jit(solution)/shard_map/ppermute | solution.py:302
  6.5 19.0 %collective-permute-start.1 = (f32[4,8,128]{2,1,0:T(8,128)}, f32[4,8,128]{2,1,0:T(8,128)S(1)}, u32[]{:S(2)}, u32[]{:S(2)}) collective-permute-start(f32[4,8,128]{2,1,0:T(8,128)} %get-tuple-element.27), channel_id=1, source_target_pairs={{8,0},{16,8},{24,16},{32,24},{40,32},{48,40},{56,48},{64,56},{72,6... | collective-permute-start | bytes 49160 | tf_op jit(solution)/shard_map/ppermute | solution.py:302
  25.4 0.0 collective-permute-done.below_ref
  25.4 0.0 copy-start
  25.5 1.0 collective-permute-done.1.above_ref
  26.5 0.0 copy-done
  26.5 0.6 copy-done.2
  27.1 9.0 %density.2 = (f32[16,1,128]{2,1,0:T(1,128)}, f32[4,128]{1,0:T(4,128)}, f32[4,128]{1,0:T(4,128)}, bf16[24,64,256]{2,1,0:T(8,128)(2,1)}, bf16[16,128,64]{2,1,0:T(8,128)(2,1)}, /*index=5*/bf16[24,32,128]{2,1,0:T(8,128)(2,1)}) custom-call(f32[16,8,128]{2,1,0:T(8,128)} %get-tuple-element.25.table_ref, f32[4,8,128]{2,1,0:T(8,128)} %copy-done, ...), custom_call_target="tpu_custom_call" | custom-call | bytes 200000 | tf_op jit(solution)/shard_map/density/pallas_call | solution.py:306
  36.1 2.0 %collective-permute-start.2 = (f32[4,128]{1,0:T(4,128)}, f32[4,128]{1,0:T(4,128)S(1)}, u32[]{:S(2)}, u32[]{:S(2)}) collective-permute-start(f32[4,128]{1,0:T(4,128)} %get-tuple-element.29), channel_id=1, source_target_pairs={{0,8},{8,16},{16,24},{24,32},{32,40},{40,48},{48,56},{56,64},{64,7... | collective-permute-start | bytes 6152 | tf_op jit(solution)/shard_map/ppermute | solution.py:302
  38.2 7.0 %collective-permute-start.3 = (f32[4,128]{1,0:T(4,128)S(1)}, f32[4,128]{1,0:T(4,128)S(1)}, u32[]{:S(2)}, u32[]{:S(2)}) collective-permute-start(f32[4,128]{1,0:T(4,128)S(1)} %copy-done.8), channel_id=1, source_target_pairs={{8,0},{16,8},{24,16},{32,24},{40,32},{48,40},{56,48},{64,56},{72,6... | collective-permute-start | bytes 6152 | tf_op jit(solution)/shard_map/ppermute | solution.py:302
  45.1 0.0 collective-permute-done.2.below_ref
  45.2 0.0 copy-start.4
  45.2 0.7 collective-permute-done.3.above_ref
  45.9 0.0 copy-done.4
  45.9 0.6 copy-done.6
  46.4 23.3 %force_move.1 = (f32[16,8,128]{2,1,0:T(8,128)}, f32[8,2,8,128]{3,2,1,0:T(8,128)}) custom-call(f32[16,8,128]{2,1,0:T(8,128)} %get-tuple-element.25.table_ref, f32[16,1,128]{2,1,0:T(1,128)} %get-tuple-element.28.rho_ref, f32[4,128]{1,0:T(4,128)} %copy-done.4, f32[4,128]{1,0:T(4,128)} %copy-done.6, s32[6,1,16]{2,1,0:T(1,128)} %bitcast.19, ...), custom_call_target="tpu_custom_call" | custom-call | bytes 200000 | tf_op jit(solution)/shard_map/force_move/pallas_call | solution.py:340
  69.8 12.1 %all_to_all.5.arrived_ref = f32[8,2,8,128]{3,2,1,0:T(8,128)} all-to-all(f32[8,2,8,128]{3,2,1,0:T(8,128)} %get-tuple-element.35), channel_id=1, replica_groups=mesh['curve'=128,'group'=8] {'group'}, dimensions={0} | all-to-all | bytes 131072 | tf_op jit(solution)/shard_map/all_to_all | solution.py:347
  81.9 1.6 %arrive.1 = (f32[16,8,128]{2,1,0:T(8,128)}, f32[4,8,128]{2,1,0:T(8,128)}, f32[4,8,128]{2,1,0:T(8,128)}) custom-call(f32[16,8,128]{2,1,0:T(8,128)} %get-tuple-element.34.stay_ref, f32[8,2,8,128]{3,2,1,0:T(8,128)} %all_to_all.5.arrived_ref, s32[1,8]{1,0:T(1,128)} %picks_ref.7), custom_call_target="tpu_custom_call" | custom-call | bytes 200000 | tf_op jit(solution)/shard_map/arrive/pallas_call | solution.py:348
  83.4 1.9 %collective-permute-start.4 = (f32[4,8,128]{2,1,0:T(8,128)}, f32[4,8,128]{2,1,0:T(8,128)S(1)}, u32[]{:S(2)}, u32[]{:S(2)}) collective-permute-start(f32[4,8,128]{2,1,0:T(8,128)} %get-tuple-element.37), channel_id=1, source_target_pairs={{0,8},{8,16},{16,24},{24,32},{32,40},{40,48},{48,56},{56,64},{64,7... | collective-permute-start | bytes 49160 | tf_op jit(solution)/shard_map/ppermute | solution.py:302
  85.4 7.2 %collective-permute-start.5 = (f32[4,8,128]{2,1,0:T(8,128)}, f32[4,8,128]{2,1,0:T(8,128)S(1)}, u32[]{:S(2)}, u32[]{:S(2)}) collective-permute-start(f32[4,8,128]{2,1,0:T(8,128)} %get-tuple-element.38), channel_id=1, source_target_pairs={{8,0},{16,8},{24,16},{32,24},{40,32},{48,40},{56,48},{64,56},{72,6... | collective-permute-start | bytes 49160 | tf_op jit(solution)/shard_map/ppermute | solution.py:302
  92.6 0.0 collective-permute-done.4.below_ref
  92.6 0.0 copy-start.1
  92.6 1.0 collective-permute-done.5.above_ref
  93.6 0.6 copy-done.3
  94.2 9.0 %density.3 = (f32[16,1,128]{2,1,0:T(1,128)}, f32[4,128]{1,0:T(4,128)}, f32[4,128]{1,0:T(4,128)}, bf16[24,64,256]{2,1,0:T(8,128)(2,1)}, bf16[16,128,64]{2,1,0:T(8,128)(2,1)}, /*index=5*/bf16[24,32,128]{2,1,0:T(8,128)(2,1)}) custom-call(f32[16,8,128]{2,1,0:T(8,128)} %get-tuple-element.36.table_ref, f32[4,8,128]{2,1,0:T(8,128)} %copy-done.1, ...), custom_call_target="tpu_custom_call" | custom-call | bytes 200000 | tf_op jit(solution)/shard_map/density/pallas_call | solution.py:306
  103.3 2.0 %collective-permute-start.6 = (f32[4,128]{1,0:T(4,128)}, f32[4,128]{1,0:T(4,128)S(1)}, u32[]{:S(2)}, u32[]{:S(2)}) collective-permute-start(f32[4,128]{1,0:T(4,128)} %get-tuple-element.40), channel_id=1, source_target_pairs={{0,8},{8,16},{16,24},{24,32},{32,40},{40,48},{48,56},{56,64},{64,7... | collective-permute-start | bytes 6152 | tf_op jit(solution)/shard_map/ppermute | solution.py:302
  105.3 7.0 %collective-permute-start.7 = (f32[4,128]{1,0:T(4,128)S(1)}, f32[4,128]{1,0:T(4,128)S(1)}, u32[]{:S(2)}, u32[]{:S(2)}) collective-permute-start(f32[4,128]{1,0:T(4,128)S(1)} %copy-done.9), channel_id=1, source_target_pairs={{8,0},{16,8},{24,16},{32,24},{40,32},{48,40},{56,48},{64,56},{72,6... | collective-permute-start | bytes 6152 | tf_op jit(solution)/shard_map/ppermute | solution.py:302
  112.3 0.0 collective-permute-done.6.below_ref
  112.3 0.7 collective-permute-done.7.above_ref
  113.0 0.6 copy-done.7
  113.6 23.3 %force_out.1 = (f32[3,16,128]{2,1,0:T(8,128)}, f32[3,16,128]{2,1,0:T(8,128)}) custom-call(f32[16,8,128]{2,1,0:T(8,128)} %get-tuple-element.36.table_ref, f32[16,1,128]{2,1,0:T(1,128)} %get-tuple-element.39.rho_ref, f32[4,128]{1,0:T(4,128)} %copy-done.5, f32[4,128]{1,0:T(4,128)} %copy-done.7, s32[6,1,16]{2,1,0:T(1,128)} %bitcast.21, ...), custom_call_target="tpu_custom_call" | custom-call | bytes 200000 | tf_op jit(solution)/shard_map/force_out/pallas_call | solution.py:353
  (11 shorter events, 0.0 us)
Async XLA Ops:
  2.1 23.3 %collective-permute-start = (f32[4,8,128]{2,1,0:T(8,128)}, f32[4,8,128]{2,1,0:T(8,128)S(1)}, u32[]{:S(2)}, u32[]{:S(2)}) collective-permute-start(f32[4,8,128]{2,1,0:T(8,128)} %get-tuple-element.26), channel_id=1, source_target_pairs={{0,8},{8,16},{16,24},{24,32},{32,40},{40,48},{48,56},{56,64},{64,7... | collective-permute-start | bytes 49160 | tf_op jit(solution)/shard_map/ppermute | solution.py:302
  6.5 20.0 %collective-permute-start.1 = (f32[4,8,128]{2,1,0:T(8,128)}, f32[4,8,128]{2,1,0:T(8,128)S(1)}, u32[]{:S(2)}, u32[]{:S(2)}) collective-permute-start(f32[4,8,128]{2,1,0:T(8,128)} %get-tuple-element.27), channel_id=1, source_target_pairs={{8,0},{16,8},{24,16},{32,24},{40,32},{48,40},{56,48},{64,56},{72,6... | collective-permute-start | bytes 49160 | tf_op jit(solution)/shard_map/ppermute | solution.py:302
  25.4 1.1 copy-start
  26.5 0.6 copy-start.2
  36.1 2.1 %copy-start.8 = (f32[4,128]{1,0:T(4,128)S(1)}, f32[4,128]{1,0:T(4,128)}, u32[]{:S(2)}) copy-start(f32[4,128]{1,0:T(4,128)} %get-tuple-element.30) | copy-start | bytes 6148
  36.1 9.0 %collective-permute-start.2 = (f32[4,128]{1,0:T(4,128)}, f32[4,128]{1,0:T(4,128)S(1)}, u32[]{:S(2)}, u32[]{:S(2)}) collective-permute-start(f32[4,128]{1,0:T(4,128)} %get-tuple-element.29), channel_id=1, source_target_pairs={{0,8},{8,16},{16,24},{24,32},{32,40},{40,48},{48,56},{56,64},{64,7... | collective-permute-start | bytes 6152 | tf_op jit(solution)/shard_map/ppermute | solution.py:302
  38.2 7.7 %collective-permute-start.3 = (f32[4,128]{1,0:T(4,128)S(1)}, f32[4,128]{1,0:T(4,128)S(1)}, u32[]{:S(2)}, u32[]{:S(2)}) collective-permute-start(f32[4,128]{1,0:T(4,128)S(1)} %copy-done.8), channel_id=1, source_target_pairs={{8,0},{16,8},{24,16},{32,24},{40,32},{48,40},{56,48},{64,56},{72,6... | collective-permute-start | bytes 6152 | tf_op jit(solution)/shard_map/ppermute | solution.py:302
  45.2 0.7 copy-start.4
  45.9 0.6 copy-start.6
  83.4 9.1 %collective-permute-start.4 = (f32[4,8,128]{2,1,0:T(8,128)}, f32[4,8,128]{2,1,0:T(8,128)S(1)}, u32[]{:S(2)}, u32[]{:S(2)}) collective-permute-start(f32[4,8,128]{2,1,0:T(8,128)} %get-tuple-element.37), channel_id=1, source_target_pairs={{0,8},{8,16},{16,24},{24,32},{32,40},{40,48},{48,56},{56,64},{64,7... | collective-permute-start | bytes 49160 | tf_op jit(solution)/shard_map/ppermute | solution.py:302
  85.4 8.3 %collective-permute-start.5 = (f32[4,8,128]{2,1,0:T(8,128)}, f32[4,8,128]{2,1,0:T(8,128)S(1)}, u32[]{:S(2)}, u32[]{:S(2)}) collective-permute-start(f32[4,8,128]{2,1,0:T(8,128)} %get-tuple-element.38), channel_id=1, source_target_pairs={{8,0},{16,8},{24,16},{32,24},{40,32},{48,40},{56,48},{64,56},{72,6... | collective-permute-start | bytes 49160 | tf_op jit(solution)/shard_map/ppermute | solution.py:302
  92.6 1.1 copy-start.1
  93.6 0.6 copy-start.3
  103.3 2.1 %copy-start.9 = (f32[4,128]{1,0:T(4,128)S(1)}, f32[4,128]{1,0:T(4,128)}, u32[]{:S(2)}) copy-start(f32[4,128]{1,0:T(4,128)} %get-tuple-element.41) | copy-start | bytes 6148
  103.3 9.0 %collective-permute-start.6 = (f32[4,128]{1,0:T(4,128)}, f32[4,128]{1,0:T(4,128)S(1)}, u32[]{:S(2)}, u32[]{:S(2)}) collective-permute-start(f32[4,128]{1,0:T(4,128)} %get-tuple-element.40), channel_id=1, source_target_pairs={{0,8},{8,16},{16,24},{24,32},{32,40},{40,48},{48,56},{56,64},{64,7... | collective-permute-start | bytes 6152 | tf_op jit(solution)/shard_map/ppermute | solution.py:302
  105.3 7.7 %collective-permute-start.7 = (f32[4,128]{1,0:T(4,128)S(1)}, f32[4,128]{1,0:T(4,128)S(1)}, u32[]{:S(2)}, u32[]{:S(2)}) collective-permute-start(f32[4,128]{1,0:T(4,128)S(1)} %copy-done.9), channel_id=1, source_target_pairs={{8,0},{16,8},{24,16},{32,24},{40,32},{48,40},{56,48},{64,56},{72,6... | collective-permute-start | bytes 6152 | tf_op jit(solution)/shard_map/ppermute | solution.py:302
  112.3 0.7 copy-start.5
  113.0 0.6 copy-start.7

commit v2 on v1

--- a/solution.py
+++ b/solution.py
@@ -22,6 +22,7 @@
 KAPPA = 4.0 * math.log2(math.e)
 MASS_SCALE = 2.0 ** (KAPPA * SOFTENING)
 FORCE_SCALE = 8.0 * MASS_SCALE
+NO_MASS = -4096.0
 
 F32 = jnp.float32
 BF16 = jnp.bfloat16
@@ -67,7 +68,7 @@
     return square, mixed
 
 
-def source_features(tile, base, rows):
+def target_features(tile, base, rows):
     local = local_tile(tile, base, rows)
     other = swapped(local, rows)
     square, mixed = quadratics(local, other, rows)
@@ -77,23 +78,32 @@
     plus = jnp.where((rows >= 3) & (rows < 6), 1.0, 0.0)
     last_near = three_rows(rows, 0, split(-KAPPA * (square + SOFTENING)))
     last_flow = three_rows(rows, 0, split(KAPPA * mixed))
-    first = jnp.concatenate([near[0], near[1], near[2], near[0], near[1], near[0], minus, last_near], axis=0)
-    second = jnp.concatenate([flow[0], flow[1], flow[2], flow[0], flow[1], flow[0], plus, last_flow], axis=0)
-    mass = tile[6:7] * FORCE_SCALE
-    weights = split(mass * jnp.where(rows < 3, local, jnp.where(rows == 3, 1.0, 0.0)))
-    summed = jnp.concatenate([weights[0], weights[1], weights[2], jnp.zeros_like(local)], axis=0)
-    return first.astype(BF16), second.astype(BF16), summed.astype(BF16)
-
-
-def target_features(tile, base, rows):
+    near = [near[0], near[1], near[2], near[0], near[1], near[0]]
+    flow = [flow[0], flow[1], flow[2], flow[0], flow[1], flow[0]]
+    distance = jnp.concatenate(near + [minus, last_near], axis=0)
+    approach = jnp.concatenate(flow + [plus, last_flow], axis=0)
+    weighted = jnp.concatenate(
+        near + [jnp.where(rows >= 6, 1.0, minus), jnp.where(rows == 3, 1.0, last_near)], axis=0
+    )
+    return distance.astype(BF16), approach.astype(BF16), weighted.astype(BF16)
+
+
+def source_features(tile, base, rows):
     local = local_tile(tile, base, rows)
     other = swapped(local, rows)
     square, mixed = quadratics(local, other, rows)
     high, middle, low = split(local)
+    mass = tile[6:7]
+    alive = mass > 0.0
+    exponent = jnp.where(alive, jnp.log2(jnp.where(alive, mass, 1.0)) + KAPPA * SOFTENING, NO_MASS)
+    exponents = split(exponent)
     quadratic = three_rows(rows, 0, split(KAPPA * square)) + three_rows(rows, 3, split(KAPPA * mixed))
-    ones = jnp.where(rows < 3, 1.0, 0.0)
+    quadratic = jnp.where(rows == 6, exponents[0], jnp.where(rows == 7, exponents[1], quadratic))
+    ones = jnp.where(rows < 3, 1.0, jnp.where(rows == 3, exponents[2], 0.0))
     stacked = jnp.concatenate([high, high, high, middle, middle, low, quadratic, ones], axis=0)
-    return stacked.T.astype(BF16)
+    weights = split((mass * FORCE_SCALE) * jnp.where(rows < 3, local, jnp.where(rows == 3, 1.0, 0.0)))
+    summed = jnp.concatenate([weights[0], weights[1], weights[2], jnp.zeros_like(local)], axis=0).astype(BF16)
+    return stacked.T.astype(BF16), jnp.concatenate([summed, summed], axis=1)
 
 
 def base_of_segment():
@@ -122,22 +132,22 @@
 
 def density_kernel(
     table_ref, below_ref, above_ref, near_ref, picks_ref,
-    rho_ref, low_ref, high_ref, pair_ref, target_ref, sum_ref, mass_ref,
+    rho_ref, low_ref, high_ref, target_ref, source_ref, sum_ref,
 ):
     base = base_of_segment()
     rows = tile_rows()
 
     def put(tile, at):
-        first, second, summed = source_features(tile, base, rows)
-        pair_ref[at, :, 0:LANES] = first
-        pair_ref[at, :, LANES : 2 * LANES] = second
+        features, summed = source_features(tile, base, rows)
+        source_ref[at] = features
         sum_ref[at] = summed
-        mass_ref[at] = tile[6:7] * MASS_SCALE
 
     def own(b, carry):
         tile = table_ref[b]
         put(tile, b)
-        target_ref[b] = target_features(tile, base, rows)
+        parts = target_features(tile, base, rows)
+        for n in range(3):
+            target_ref[b, :, n * LANES : (n + 1) * LANES] = parts[n]
         return carry
 
     lax.fori_loop(0, BLOCKS, own, 0, unroll=4)
@@ -145,63 +155,50 @@
         put(below_ref[h], BLOCKS + h)
         put(above_ref[h], BLOCKS + HALO + h)
 
-    ones = jnp.ones((8, LANES), F32)
-
     def target(j, carry):
-        left = target_ref[j]
+        right = target_ref[j, :, 2 * LANES : 3 * LANES]
         sources = [j] + [near_ref[n, 0, j] for n in range(NBR)]
-        total = jnp.zeros((LANES, LANES), F32)
-        for start in range(0, NBR + 1, 2):
-            chosen = sources[start : start + 2]
-            right = [pair_ref[s, :, 0:LANES] for s in chosen]
-            right = right[0] if len(right) == 1 else jnp.concatenate(right, axis=1)
-            weight = jnp.exp2(jnp.dot(left, right, preferred_element_type=F32))
-            for n, s in enumerate(chosen):
-                total = total + weight[:, n * LANES : (n + 1) * LANES] * mass_ref[s]
-        row = lax.dot_general(
-            ones, total, (((1,), (1,)), ((), ())), precision=lax.Precision.HIGHEST, preferred_element_type=F32
-        )
-        rho_ref[j] = BACKGROUND + row[0:1]
+        left = jnp.concatenate([source_ref[s] for s in sources], axis=0)
+        weight = jnp.exp2(jnp.dot(left, right, preferred_element_type=F32))
+        rho_ref[j] = BACKGROUND + jnp.sum(weight, axis=0, keepdims=True)
         return carry
 
-    lax.fori_loop(0, BLOCKS, target, 0)
+    lax.fori_loop(0, BLOCKS, target, 0, unroll=2)
     for h in range(HALO):
         low_ref[pl.ds(h, 1), :] = rho_ref[picks_ref[0, h]]
         high_ref[pl.ds(h, 1), :] = rho_ref[picks_ref[0, HALO + h]]
 
 
-def advance(table_ref, rho_ref, below_ref, above_ref, near_ref, pair_ref, target_ref, sum_ref, all_rho, columns, done):
+def advance(
+    table_ref, rho_ref, below_ref, above_ref, near_ref, target_ref, source_ref, sum_ref, rho_of, inverse_of, done
+):
     base = base_of_segment()
     rows = tile_rows()
-    flat = jnp.concatenate([rho_ref[b] for b in range(BLOCKS)], axis=0)
-    for b in range(BLOCKS):
-        all_rho[b] = rho_ref[b]
-    for h in range(HALO):
-        all_rho[BLOCKS + h] = below_ref[pl.ds(h, 1), :]
-        all_rho[BLOCKS + HALO + h] = above_ref[pl.ds(h, 1), :]
-    columns[...] = jnp.concatenate([flat, jnp.ones((LANES - BLOCKS, LANES), F32)], axis=0).T
-    lane = lax.broadcasted_iota(jnp.int32, (LANES, LANES), 1)
+    flat = [rho_ref[b] for b in range(BLOCKS)] + [below_ref[...], above_ref[...], jnp.ones((8, LANES), F32)]
+    flat = jnp.concatenate(flat, axis=0)
+    across = flat.T
+    for s in range(CANDIDATES):
+        column = jnp.broadcast_to(across[:, s : s + 1], (LANES, LANES))
+        rho_of[s] = column
+        inverse_of[s] = 1.0 / column
 
     def target(j, carry):
-        left = target_ref[j]
-        mine = jnp.sum(jnp.where(lane == j, columns[...], 0.0), axis=1, keepdims=True)
+        right = target_ref[j, :, 0 : 2 * LANES]
+        mine = rho_ref[j]
         mine_inverse = 1.0 / mine
         sources = [j] + [near_ref[n, 0, j] for n in range(NBR)]
-        total = jnp.zeros((32, LANES), F32)
+        wholes, lefts = [], []
         for s in sources:
-            product = jnp.dot(left, pair_ref[s], preferred_element_type=F32)
+            product = jnp.dot(source_ref[s], right, preferred_element_type=F32)
             distance = product[:, 0:LANES]
             approach = product[:, LANES : 2 * LANES]
-            theirs = all_rho[s]
-            closing = jnp.minimum(approach, 0.0) / (distance * (mine + theirs))
-            factor = jnp.exp2(distance) * (closing + (mine_inverse + 1.0 / theirs))
+            closing = jnp.minimum(approach, 0.0) / (distance * (mine + rho_of[s]))
+            factor = jnp.exp2(distance) * (closing + (mine_inverse + inverse_of[s]))
             high = factor.astype(BF16)
             low = (factor - high.astype(F32)).astype(BF16)
-            weights = sum_ref[s]
-            for part in (high, low):
-                total = total + lax.dot_general(
-                    weights, part, (((1,), (1,)), ((), ())), preferred_element_type=F32
-                )
+            wholes += [high, low]
+            lefts.append(sum_ref[s])
+        total = jnp.dot(jnp.concatenate(lefts, axis=1), jnp.concatenate(wholes, axis=0), preferred_element_type=F32)
         sums = total[0:8] + total[8:16] + total[16:24]
         tile = table_ref[j]
         local = local_tile(tile, base, rows)
@@ -211,12 +208,12 @@
         done(j, jnp.where(rows < 3, kicked + TIME_STEP * drift, kicked))
         return carry
 
-    lax.fori_loop(0, BLOCKS, target, 0)
+    lax.fori_loop(0, BLOCKS, target, 0, unroll=2)
 
 
 def force_move_kernel(
-    table_ref, rho_ref, below_ref, above_ref, near_ref, pair_ref, target_ref, sum_ref, slot_ref,
-    stay_ref, send_ref, all_rho, columns, filled,
+    table_ref, rho_ref, below_ref, above_ref, near_ref, target_ref, source_ref, sum_ref, slot_ref,
+    stay_ref, send_ref, rho_of, inverse_of, filled,
 ):
     me = lax.axis_index("group")
     rows = tile_rows()
@@ -244,7 +241,7 @@
             filled[owner] = place + 1
 
     advance(
-        table_ref, rho_ref, below_ref, above_ref, near_ref, pair_ref, target_ref, sum_ref, all_rho, columns, done
+        table_ref, rho_ref, below_ref, above_ref, near_ref, target_ref, source_ref, sum_ref, rho_of, inverse_of, done
     )
 
 
@@ -261,14 +258,14 @@
 
 
 def force_out_kernel(
-    table_ref, rho_ref, below_ref, above_ref, near_ref, pair_ref, target_ref, sum_ref,
-    x_ref, v_ref, all_rho, columns, flat_ref,
+    table_ref, rho_ref, below_ref, above_ref, near_ref, target_ref, source_ref, sum_ref,
+    x_ref, v_ref, rho_of, inverse_of, flat_ref,
 ):
     def done(b, tile):
         flat_ref[pl.ds(pl.multiple_of(8 * b, 8), 8), :] = tile
 
     advance(
-        table_ref, rho_ref, below_ref, above_ref, near_ref, pair_ref, target_ref, sum_ref, all_rho, columns, done
+        table_ref, rho_ref, below_ref, above_ref, near_ref, target_ref, source_ref, sum_ref, rho_of, inverse_of, done
     )
     for axis_id in range(3):
         x_ref[axis_id] = flat_ref[pl.ds(axis_id, BLOCKS, stride=8), :]
@@ -292,6 +289,7 @@
         out_specs=[VMEM] * len(out_shape),
         scratch_shapes=list(scratch),
         cost_estimate=pl.CostEstimate(flops=flops, bytes_accessed=200000, transcendentals=0),
+        compiler_params=pltpu.CompilerParams(vmem_limit_bytes=16 << 20),
     )
 
 
@@ -303,26 +301,25 @@
 
 
 def half_step(table, below, above, near, picks):
-    rho, low, high, pairs, targets, sums = call(
+    rho, low, high, targets, sources, sums = call(
         density_kernel,
         "density",
         (
             shape(BLOCKS, 1, LANES),
             shape(HALO, LANES),
             shape(HALO, LANES),
-            shape(CANDIDATES, FEATURES, 2 * LANES, dtype=BF16),
-            shape(BLOCKS, LANES, FEATURES, dtype=BF16),
-            shape(CANDIDATES, 32, LANES, dtype=BF16),
+            shape(BLOCKS, FEATURES, 3 * LANES, dtype=BF16),
+            shape(CANDIDATES, LANES, FEATURES, dtype=BF16),
+            shape(CANDIDATES, 32, 2 * LANES, dtype=BF16),
         ),
         [VMEM, VMEM, VMEM, SMEM, SMEM],
-        [pltpu.VMEM((CANDIDATES, 1, LANES), F32)],
     )(table, below, above, near, picks)
     rho_below, rho_above = exchange(low, high)
-    return (table, rho, rho_below, rho_above, near, pairs, targets, sums)
+    return (table, rho, rho_below, rho_above, near, targets, sources, sums)
 
 
 FORCE_SPECS = [VMEM, VMEM, VMEM, VMEM, SMEM, VMEM, VMEM, VMEM]
-FORCE_SCRATCH = [pltpu.VMEM((CANDIDATES, 1, LANES), F32), pltpu.VMEM((LANES, LANES), F32)]
+FORCE_SCRATCH = [pltpu.VMEM((CANDIDATES, LANES, LANES), F32)] * 2
 
 
 def body(x, v, masses, counts, near_first, picks_first, new_slot, near_second, picks_second):

time: 138 us -> 96.7 us (0.70)
  Pallas kernels: 67.7 us -> 25.7 us
  local copies, waits for them, and re-layouts: 2.38 us -> 4.15 us
    pallas_call x1, Pallas kernels: 23.3 us -> 8.09 us  [body(): call(force_out_kernel, 'force_out', (shape(3, BLOCKS, LANES), shape(3, BL...]
    pallas_call x1, Pallas kernels: 23.3 us -> 8.68 us  [body(): call(force_move_kernel, 'force_move', (TABLE, shape(groups, MOVES, 8, LAN...]
    pallas_call x2, Pallas kernels: 18.1 us -> 7.71 us  [half_step(): call(density_kernel, 'density', (shape(BLOCKS, 1, LANES), shape(HALO, LAN...]
    unnamed x20, local copies, waits for them, and re-layouts: 2.38 us -> 4.15 us
where the time goes in v2:
time: 96.7 us; the launch traced here: 95.8 us
  starting transfers between devices  50.3 us (52%)
  Pallas kernels  25.7 us (27%)
  blocking collectives  11.8 us (12%)
  local copies, waits for them, and re-layouts  4.15 us (4%)
  waiting for transfers between devices  3.09 us (3%)
    ppermute x4, starting transfers between devices, exchange(): lax.ppermute(low, 'curve', backward)  40.1 us
    all_to_all x1, blocking collectives, body(): arrived = lax.all_to_all(send, 'group', 0, 0)  11.8 us
    ppermute x4, starting transfers between devices, exchange(): lax.ppermute(high, 'curve', forward)  10.2 us
    pallas_call x1, Pallas kernels, body(): call(force_move_kernel, 'force_move', (TABLE, shape(groups, MOVES, 8, LAN...  8.68 us
    pallas_call x1, Pallas kernels, body(): call(force_out_kernel, 'force_out', (shape(3, BLOCKS, LANES), shape(3, BL...  8.09 us
    pallas_call x2, Pallas kernels, half_step(): call(density_kernel, 'density', (shape(BLOCKS, 1, LANES), shape(HALO, LAN...  7.71 us
    unnamed x20, local copies, waits for them, and re-layouts  4.15 us
    ppermute x4, waiting for transfers between devices, exchange(): lax.ppermute(low, 'curve', backward)  3.08 us
  transfers between devices with their start and end apart: 8, of which 4 were waited for; matrix products, arithmetic and copies ran while one was open for 0% of the time, Pallas kernels for 0%

profile of v2, /device:TPU:1, one launch (start us, length us, event | category | flops | bytes accessed | tf_op | source)
XLA Modules:
  0.0 95.8 jit_solution(10714327638248546331)
XLA Ops:
  0.7 0.6 copy-done.6
  1.3 0.0 copy-done.8
  1.3 0.7 copy-done
  2.0 0.7 copy-done.1
  2.8 0.7 copy-done.5
  3.5 0.6 gather.1
  4.1 0.0 copy-start.2
  4.1 4.4 %collective-permute-start = (f32[4,8,128]{2,1,0:T(8,128)S(1)}, f32[4,8,128]{2,1,0:T(8,128)S(1)}, u32[]{:S(2)}, u32[]{:S(2)}) collective-permute-start(f32[4,8,128]{2,1,0:T(8,128)S(1)} %get-tuple-element.26), channel_id=1, source_target_pairs={{0,8},{8,16},{16,24},{24,32},{32,40},{40,48},{48,56},{56,64},{64,7... | collective-permute-start | bytes 49160 | tf_op jit(solution)/shard_map/ppermute | solution.py:300
  8.4 19.0 %collective-permute-start.1 = (f32[4,8,128]{2,1,0:T(8,128)S(1)}, f32[4,8,128]{2,1,0:T(8,128)S(1)}, u32[]{:S(2)}, u32[]{:S(2)}) collective-permute-start(f32[4,8,128]{2,1,0:T(8,128)S(1)} %get-tuple-element.27), channel_id=1, source_target_pairs={{8,0},{16,8},{24,16},{32,24},{40,32},{48,40},{56,48},{64,56},{72,6... | collective-permute-start | bytes 49160 | tf_op jit(solution)/shard_map/ppermute | solution.py:300
  27.4 0.0 collective-permute-done.below_ref
  27.4 0.8 collective-permute-done.1.above_ref
  28.3 3.6 %density.2 = (f32[16,1,128]{2,1,0:T(1,128)S(1)}, f32[4,128]{1,0:T(4,128)S(1)}, f32[4,128]{1,0:T(4,128)S(1)}, bf16[16,64,384]{2,1,0:T(8,128)(2,1)S(1)}, bf16[24,1...) custom-call(f32[16,8,128]{2,1,0:T(8,128)S(1)} %get-tuple-element.25.table_ref, ...), custom_call_target="tpu_custom_call" | custom-call | bytes 200000 | tf_op jit(solution)/shard_map/density/pallas_call | solution.py:304
  31.8 1.9 %collective-permute-start.2 = (f32[4,128]{1,0:T(4,128)S(1)}, f32[4,128]{1,0:T(4,128)S(1)}, u32[]{:S(2)}, u32[]{:S(2)}) collective-permute-start(f32[4,128]{1,0:T(4,128)S(1)} %get-tuple-element.29), channel_id=1, source_target_pairs={{0,8},{8,16},{16,24},{24,32},{32,40},{40,48},{48,56},{56,64},{64,7... | collective-permute-start | bytes 6152 | tf_op jit(solution)/shard_map/ppermute | solution.py:300
  33.8 6.9 %collective-permute-start.3 = (f32[4,128]{1,0:T(4,128)S(1)}, f32[4,128]{1,0:T(4,128)S(1)}, u32[]{:S(2)}, u32[]{:S(2)}) collective-permute-start(f32[4,128]{1,0:T(4,128)S(1)} %get-tuple-element.30), channel_id=1, source_target_pairs={{8,0},{16,8},{24,16},{32,24},{40,32},{48,40},{56,48},{64,56},{72,6... | collective-permute-start | bytes 6152 | tf_op jit(solution)/shard_map/ppermute | solution.py:300
  40.7 0.0 collective-permute-done.2.below_ref
  40.7 0.7 collective-permute-done.3.above_ref
  41.4 0.7 copy-done.9
  42.1 8.7 %force_move.1 = (f32[16,8,128]{2,1,0:T(8,128)S(1)}, f32[8,2,8,128]{3,2,1,0:T(8,128)S(1)}) custom-call(f32[16,8,128]{2,1,0:T(8,128)S(1)} %get-tuple-element.25.table_ref, f32[16,1,128]{2,1,0:T(1,128)S(1)} %get-tuple-element.28.rho_ref, f32[4,128]{1,0:T(4,128)S(1)} %collective-permute-done.2.below_ref, f32[4,128]{1,0:T(4,128)S(1)} %collective-permute-done.3.above_ref, ...), custom_call_target="tpu_custom_call" | custom-call | bytes 200000 | tf_op jit(solution)/shard_map/force_move/pallas_call | solution.py:337
  50.8 11.8 %all_to_all.5.arrived_ref = f32[8,2,8,128]{3,2,1,0:T(8,128)S(1)} all-to-all(f32[8,2,8,128]{3,2,1,0:T(8,128)S(1)} %get-tuple-element.35), channel_id=1, replica_groups=mesh['curve'=128,'group'=8] {'group'}, dimensions={0} | all-to-all | bytes 131072 | tf_op jit(solution)/shard_map/all_to_all | solution.py:344
  62.5 0.7 copy-done.7
  63.2 0.6 arrive.1
  63.8 0.0 copy-start.3
  63.8 1.9 %collective-permute-start.4 = (f32[4,8,128]{2,1,0:T(8,128)S(1)}, f32[4,8,128]{2,1,0:T(8,128)S(1)}, u32[]{:S(2)}, u32[]{:S(2)}) collective-permute-start(f32[4,8,128]{2,1,0:T(8,128)S(1)} %get-tuple-element.37), channel_id=1, source_target_pairs={{0,8},{8,16},{16,24},{24,32},{32,40},{40,48},{48,56},{56,64},{64,7... | collective-permute-start | bytes 49160 | tf_op jit(solution)/shard_map/ppermute | solution.py:300
  65.8 7.2 %collective-permute-start.5 = (f32[4,8,128]{2,1,0:T(8,128)S(1)}, f32[4,8,128]{2,1,0:T(8,128)S(1)}, u32[]{:S(2)}, u32[]{:S(2)}) collective-permute-start(f32[4,8,128]{2,1,0:T(8,128)S(1)} %get-tuple-element.38), channel_id=1, source_target_pairs={{8,0},{16,8},{24,16},{32,24},{40,32},{48,40},{56,48},{64,56},{72,6... | collective-permute-start | bytes 49160 | tf_op jit(solution)/shard_map/ppermute | solution.py:300
  73.0 0.0 collective-permute-done.4.below_ref
  73.0 0.8 collective-permute-done.5.above_ref
  73.9 4.2 %density.3 = (f32[16,1,128]{2,1,0:T(1,128)}, f32[4,128]{1,0:T(4,128)S(1)}, f32[4,128]{1,0:T(4,128)S(1)}, bf16[16,64,384]{2,1,0:T(8,128)(2,1)S(1)}, bf16[24,128,6...) custom-call(f32[16,8,128]{2,1,0:T(8,128)S(1)} %get-tuple-element.36.table_ref, ...), custom_call_target="tpu_custom_call" | custom-call | bytes 200000 | tf_op jit(solution)/shard_map/density/pallas_call | solution.py:304
  78.0 2.0 %collective-permute-start.6 = (f32[4,128]{1,0:T(4,128)S(1)}, f32[4,128]{1,0:T(4,128)S(1)}, u32[]{:S(2)}, u32[]{:S(2)}) collective-permute-start(f32[4,128]{1,0:T(4,128)S(1)} %get-tuple-element.40), channel_id=1, source_target_pairs={{0,8},{8,16},{16,24},{24,32},{32,40},{40,48},{48,56},{56,64},{64,7... | collective-permute-start | bytes 6152 | tf_op jit(solution)/shard_map/ppermute | solution.py:300
  80.1 6.9 %collective-permute-start.7 = (f32[4,128]{1,0:T(4,128)S(1)}, f32[4,128]{1,0:T(4,128)S(1)}, u32[]{:S(2)}, u32[]{:S(2)}) collective-permute-start(f32[4,128]{1,0:T(4,128)S(1)} %get-tuple-element.41), channel_id=1, source_target_pairs={{8,0},{16,8},{24,16},{32,24},{40,32},{48,40},{56,48},{64,56},{72,6... | collective-permute-start | bytes 6152 | tf_op jit(solution)/shard_map/ppermute | solution.py:300
  87.0 0.0 collective-permute-done.6.below_ref
  87.0 0.7 collective-permute-done.7.above_ref
  87.7 8.1 %force_out.1 = (f32[3,16,128]{2,1,0:T(8,128)}, f32[3,16,128]{2,1,0:T(8,128)}) custom-call(f32[16,8,128]{2,1,0:T(8,128)S(1)} %get-tuple-element.36.table_ref, f32[16,1,128]{2,1,0:T(1,128)S(1)} %copy-done.4, f32[4,128]{1,0:T(4,128)S(1)} %collective-permute-done.6.below_ref, f32[4,128]{1,0:T(4,128)S(1)} %collective-permute-done.7.above_ref, ...), custom_call_target="tpu_custom_call" | custom-call | bytes 200000 | tf_op jit(solution)/shard_map/force_out/pallas_call | solution.py:350
  (11 shorter events, 0.0 us)
Async XLA Ops:
  0.6 0.7 copy-start.6
  0.6 0.7 copy-start.8
  1.3 0.7 copy-start
  2.0 0.7 copy-start.1
  2.8 0.7 copy-start.5
  4.1 24.2 %copy-start.2 = (s32[1,16,6]{1,0,2:T(1,128)S(1)}, s32[1,16,6]{1,0,2:T(1,128)}, u32[]{:S(2)}) copy-start(s32[1,16,6]{1,0,2:T(1,128)} %param.13) | copy-start | bytes 1156
  4.1 23.4 %collective-permute-start = (f32[4,8,128]{2,1,0:T(8,128)S(1)}, f32[4,8,128]{2,1,0:T(8,128)S(1)}, u32[]{:S(2)}, u32[]{:S(2)}) collective-permute-start(f32[4,8,128]{2,1,0:T(8,128)S(1)} %get-tuple-element.26), channel_id=1, source_target_pairs={{0,8},{8,16},{16,24},{24,32},{32,40},{40,48},{48,56},{56,64},{64,7... | collective-permute-start | bytes 49160 | tf_op jit(solution)/shard_map/ppermute | solution.py:300
  8.4 19.8 %collective-permute-start.1 = (f32[4,8,128]{2,1,0:T(8,128)S(1)}, f32[4,8,128]{2,1,0:T(8,128)S(1)}, u32[]{:S(2)}, u32[]{:S(2)}) collective-permute-start(f32[4,8,128]{2,1,0:T(8,128)S(1)} %get-tuple-element.27), channel_id=1, source_target_pairs={{8,0},{16,8},{24,16},{32,24},{40,32},{48,40},{56,48},{64,56},{72,6... | collective-permute-start | bytes 49160 | tf_op jit(solution)/shard_map/ppermute | solution.py:300
  31.8 8.9 %collective-permute-start.2 = (f32[4,128]{1,0:T(4,128)S(1)}, f32[4,128]{1,0:T(4,128)S(1)}, u32[]{:S(2)}, u32[]{:S(2)}) collective-permute-start(f32[4,128]{1,0:T(4,128)S(1)} %get-tuple-element.29), channel_id=1, source_target_pairs={{0,8},{8,16},{16,24},{24,32},{32,40},{40,48},{48,56},{56,64},{64,7... | collective-permute-start | bytes 6152 | tf_op jit(solution)/shard_map/ppermute | solution.py:300
  33.8 7.7 %collective-permute-start.3 = (f32[4,128]{1,0:T(4,128)S(1)}, f32[4,128]{1,0:T(4,128)S(1)}, u32[]{:S(2)}, u32[]{:S(2)}) collective-permute-start(f32[4,128]{1,0:T(4,128)S(1)} %get-tuple-element.30), channel_id=1, source_target_pairs={{8,0},{16,8},{24,16},{32,24},{40,32},{48,40},{56,48},{64,56},{72,6... | collective-permute-start | bytes 6152 | tf_op jit(solution)/shard_map/ppermute | solution.py:300
  41.4 0.7 copy-start.9
  62.5 0.7 copy-start.7
  63.8 10.0 %copy-start.3 = (s32[1,16,6]{1,0,2:T(1,128)S(1)}, s32[1,16,6]{1,0,2:T(1,128)}, u32[]{:S(2)}) copy-start(s32[1,16,6]{1,0,2:T(1,128)} %param.16) | copy-start | bytes 1156
  63.8 9.2 %collective-permute-start.4 = (f32[4,8,128]{2,1,0:T(8,128)S(1)}, f32[4,8,128]{2,1,0:T(8,128)S(1)}, u32[]{:S(2)}, u32[]{:S(2)}) collective-permute-start(f32[4,8,128]{2,1,0:T(8,128)S(1)} %get-tuple-element.37), channel_id=1, source_target_pairs={{0,8},{8,16},{16,24},{24,32},{32,40},{40,48},{48,56},{56,64},{64,7... | collective-permute-start | bytes 49160 | tf_op jit(solution)/shard_map/ppermute | solution.py:300
  65.8 8.1 %collective-permute-start.5 = (f32[4,8,128]{2,1,0:T(8,128)S(1)}, f32[4,8,128]{2,1,0:T(8,128)S(1)}, u32[]{:S(2)}, u32[]{:S(2)}) collective-permute-start(f32[4,8,128]{2,1,0:T(8,128)S(1)} %get-tuple-element.38), channel_id=1, source_target_pairs={{8,0},{16,8},{24,16},{32,24},{40,32},{48,40},{56,48},{64,56},{72,6... | collective-permute-start | bytes 49160 | tf_op jit(solution)/shard_map/ppermute | solution.py:300
  78.0 9.7 %copy-start.4 = (f32[16,1,128]{2,1,0:T(1,128)S(1)}, f32[16,1,128]{2,1,0:T(1,128)}, u32[]{:S(2)}) copy-start(f32[16,1,128]{2,1,0:T(1,128)} %get-tuple-element.39.rho_ref) | copy-start | bytes 24580
  78.0 9.0 %collective-permute-start.6 = (f32[4,128]{1,0:T(4,128)S(1)}, f32[4,128]{1,0:T(4,128)S(1)}, u32[]{:S(2)}, u32[]{:S(2)}) collective-permute-start(f32[4,128]{1,0:T(4,128)S(1)} %get-tuple-element.40), channel_id=1, source_target_pairs={{0,8},{8,16},{16,24},{24,32},{32,40},{40,48},{48,56},{56,64},{64,7... | collective-permute-start | bytes 6152 | tf_op jit(solution)/shard_map/ppermute | solution.py:300
  80.1 7.7 %collective-permute-start.7 = (f32[4,128]{1,0:T(4,128)S(1)}, f32[4,128]{1,0:T(4,128)S(1)}, u32[]{:S(2)}, u32[]{:S(2)}) collective-permute-start(f32[4,128]{1,0:T(4,128)S(1)} %get-tuple-element.41), channel_id=1, source_target_pairs={{8,0},{16,8},{24,16},{32,24},{40,32},{48,40},{56,48},{64,56},{72,6... | collective-permute-start | bytes 6152 | tf_op jit(solution)/shard_map/ppermute | solution.py:300

commit v3 on v2

--- a/solution.py
+++ b/solution.py
@@ -19,6 +19,7 @@
 LANES = 128
 FEATURES = 64
 MOVES = 2
+GATHER_GRANT = 63_000_000
 KAPPA = 4.0 * math.log2(math.e)
 MASS_SCALE = 2.0 ** (KAPPA * SOFTENING)
 FORCE_SCALE = 8.0 * MASS_SCALE
@@ -28,6 +29,7 @@
 BF16 = jnp.bfloat16
 VMEM = pl.BlockSpec(memory_space=pltpu.VMEM)
 SMEM = pl.BlockSpec(memory_space=pltpu.SMEM)
+HBM = pl.BlockSpec(memory_space=pltpu.HBM)
 
 
 def rounded(value):
@@ -110,13 +112,28 @@
     return SPACING * lax.axis_index("curve").astype(F32)
 
 
-def list_blocks(table_ref, picks_ref, low_ref, high_ref):
+def parity():
+    return lax.rem(lax.axis_index("curve"), 2)
+
+
+def list_blocks(table_ref, picks_ref, outer_ref, inner_ref):
+    odd = parity()
     for h in range(HALO):
-        low_ref[h] = table_ref[picks_ref[0, h]]
-        high_ref[h] = table_ref[picks_ref[0, HALO + h]]
-
-
-def gather_kernel(x_ref, v_ref, m_ref, counts_ref, picks_ref, table_ref, low_ref, high_ref, flat_ref):
+        outer_ref[h] = table_ref[picks_ref[0, odd * HALO + h]]
+        inner_ref[h] = table_ref[picks_ref[0, (1 - odd) * HALO + h]]
+
+
+def gather_kernel(
+    x_hbm, v_hbm, m_hbm, counts_hbm, picks_hbm,
+    table_ref, outer_ref, inner_ref,
+    x_ref, v_ref, m_ref, flat_ref, counts_ref, picks_ref, sems,
+):
+    pairs = ((x_hbm, x_ref), (v_hbm, v_ref), (m_hbm, m_ref), (counts_hbm, counts_ref), (picks_hbm, picks_ref))
+    copies = [pltpu.make_async_copy(source, target, sems.at[n]) for n, (source, target) in enumerate(pairs)]
+    for copy in copies:
+        copy.start()
+    for copy in copies:
+        copy.wait()
     for axis_id in range(3):
         flat_ref[pl.ds(axis_id, BLOCKS, stride=8), :] = x_ref[axis_id]
         flat_ref[pl.ds(3 + axis_id, BLOCKS, stride=8), :] = v_ref[axis_id]
@@ -127,14 +144,16 @@
         flat_ref[pl.ds(8 * b + 7, 1), :] = jnp.zeros_like(live)
     for b in range(BLOCKS):
         table_ref[b] = flat_ref[pl.ds(8 * b, 8), :]
-    list_blocks(table_ref, picks_ref, low_ref, high_ref)
-
-
-def density_kernel(
-    table_ref, below_ref, above_ref, near_ref, picks_ref,
-    rho_ref, low_ref, high_ref, target_ref, source_ref, sum_ref,
-):
+    list_blocks(table_ref, picks_ref, outer_ref, inner_ref)
+
+
+def density_kernel(table_ref, outer_ref, inner_ref, near_ref, picks_ref, *refs):
+    rho_ref, outer_out_ref, inner_out_ref, target_ref, source_ref, sum_ref = refs[-6:]
+    passed = (len(refs) - 6) // 2
+    for n in range(passed):
+        refs[passed + n][...] = refs[n][...]
     base = base_of_segment()
+    odd = parity()
     rows = tile_rows()
 
     def put(tile, at):
@@ -152,8 +171,8 @@
 
     lax.fori_loop(0, BLOCKS, own, 0, unroll=4)
     for h in range(HALO):
-        put(below_ref[h], BLOCKS + h)
-        put(above_ref[h], BLOCKS + HALO + h)
+        put(outer_ref[h], BLOCKS + odd * HALO + h)
+        put(inner_ref[h], BLOCKS + (1 - odd) * HALO + h)
 
     def target(j, carry):
         right = target_ref[j, :, 2 * LANES : 3 * LANES]
@@ -165,16 +184,20 @@
 
     lax.fori_loop(0, BLOCKS, target, 0, unroll=2)
     for h in range(HALO):
-        low_ref[pl.ds(h, 1), :] = rho_ref[picks_ref[0, h]]
-        high_ref[pl.ds(h, 1), :] = rho_ref[picks_ref[0, HALO + h]]
+        outer_out_ref[pl.ds(h, 1), :] = rho_ref[picks_ref[0, odd * HALO + h]]
+        inner_out_ref[pl.ds(h, 1), :] = rho_ref[picks_ref[0, (1 - odd) * HALO + h]]
 
 
 def advance(
-    table_ref, rho_ref, below_ref, above_ref, near_ref, target_ref, source_ref, sum_ref, rho_of, inverse_of, done
+    table_ref, rho_ref, outer_ref, inner_ref, near_ref, target_ref, source_ref, sum_ref, rho_of, inverse_of, done
 ):
     base = base_of_segment()
     rows = tile_rows()
-    flat = [rho_ref[b] for b in range(BLOCKS)] + [below_ref[...], above_ref[...], jnp.ones((8, LANES), F32)]
+    even = parity() == 0
+    outer, inner = outer_ref[...], inner_ref[...]
+    below = jnp.where(even, outer, inner)
+    above = jnp.where(even, inner, outer)
+    flat = [rho_ref[b] for b in range(BLOCKS)] + [below, above, jnp.ones((8, LANES), F32)]
     flat = jnp.concatenate(flat, axis=0)
     across = flat.T
     for s in range(CANDIDATES):
@@ -212,9 +235,11 @@
 
 
 def force_move_kernel(
-    table_ref, rho_ref, below_ref, above_ref, near_ref, target_ref, source_ref, sum_ref, slot_ref,
-    stay_ref, send_ref, rho_of, inverse_of, filled,
+    table_ref, rho_ref, outer_ref, inner_ref, near_ref, target_ref, source_ref, sum_ref, slot_hbm,
+    stay_ref, send_ref, rho_of, inverse_of, filled, slot_ref, sem,
 ):
+    copy = pltpu.make_async_copy(slot_hbm, slot_ref, sem)
+    copy.start()
     me = lax.axis_index("group")
     rows = tile_rows()
     groups = send_ref.shape[0]
@@ -224,6 +249,7 @@
             send_ref[g, k] = jnp.full((8, LANES), -1.0, F32)
     for b in range(BLOCKS):
         stay_ref[b] = jnp.zeros((8, LANES), F32)
+    copy.wait()
 
     def done(b, tile):
         owner = slot_ref[0, b] // BLOCKS
@@ -241,11 +267,13 @@
             filled[owner] = place + 1
 
     advance(
-        table_ref, rho_ref, below_ref, above_ref, near_ref, target_ref, source_ref, sum_ref, rho_of, inverse_of, done
-    )
-
-
-def arrive_kernel(stay_ref, arrived_ref, picks_ref, table_ref, low_ref, high_ref):
+        table_ref, rho_ref, outer_ref, inner_ref, near_ref, target_ref, source_ref, sum_ref, rho_of, inverse_of, done
+    )
+
+
+def arrive_kernel(stay_ref, arrived_ref, picks_hbm, table_ref, outer_ref, inner_ref, picks_ref, sem):
+    copy = pltpu.make_async_copy(picks_hbm, picks_ref, sem)
+    copy.start()
     groups = arrived_ref.shape[0]
     tiles = [arrived_ref[g, k] for g in range(groups) for k in range(MOVES)]
     tags = [jnp.broadcast_to(tile[7:8], (8, LANES)) for tile in tiles]
@@ -254,18 +282,19 @@
         for tile, tag in zip(tiles, tags):
             value = jnp.where(tag == float(s), tile, value)
         table_ref[s] = value
-    list_blocks(table_ref, picks_ref, low_ref, high_ref)
+    copy.wait()
+    list_blocks(table_ref, picks_ref, outer_ref, inner_ref)
 
 
 def force_out_kernel(
-    table_ref, rho_ref, below_ref, above_ref, near_ref, target_ref, source_ref, sum_ref,
+    table_ref, rho_ref, outer_ref, inner_ref, near_ref, target_ref, source_ref, sum_ref,
     x_ref, v_ref, rho_of, inverse_of, flat_ref,
 ):
     def done(b, tile):
         flat_ref[pl.ds(pl.multiple_of(8 * b, 8), 8), :] = tile
 
     advance(
-        table_ref, rho_ref, below_ref, above_ref, near_ref, target_ref, source_ref, sum_ref, rho_of, inverse_of, done
+        table_ref, rho_ref, outer_ref, inner_ref, near_ref, target_ref, source_ref, sum_ref, rho_of, inverse_of, done
     )
     for axis_id in range(3):
         x_ref[axis_id] = flat_ref[pl.ds(axis_id, BLOCKS, stride=8), :]
@@ -280,7 +309,7 @@
 LISTED = shape(HALO, 8, LANES)
 
 
-def call(kernel, name, out_shape, in_specs, scratch=(), flops=0):
+def call(kernel, name, out_shape, in_specs, scratch=(), flops=0, grant=16 << 20):
     return pl.pallas_call(
         kernel,
         name=name,
@@ -289,22 +318,24 @@
         out_specs=[VMEM] * len(out_shape),
         scratch_shapes=list(scratch),
         cost_estimate=pl.CostEstimate(flops=flops, bytes_accessed=200000, transcendentals=0),
-        compiler_params=pltpu.CompilerParams(vmem_limit_bytes=16 << 20),
-    )
-
-
-def exchange(low, high):
+        compiler_params=pltpu.CompilerParams(vmem_limit_bytes=grant),
+    )
+
+
+def exchange(outer, inner):
     count = lax.axis_size("curve")
-    forward = [(i, (i + 1) % count) for i in range(count)]
-    backward = [(target, source) for source, target in forward]
-    return lax.ppermute(high, "curve", forward), lax.ppermute(low, "curve", backward)
-
-
-def half_step(table, below, above, near, picks):
-    rho, low, high, targets, sources, sums = call(
+    odd_first = [(i, (i + 1) % count) for i in range(1, count, 2)]
+    even_first = [(i, i + 1) for i in range(0, count, 2)]
+    both = lambda pairs: pairs + [(target, source) for source, target in pairs]
+    return lax.ppermute(outer, "curve", both(odd_first)), lax.ppermute(inner, "curve", both(even_first))
+
+
+def half_step(table, outer, inner, near, picks, passed=()):
+    *passed, rho, outer_rho, inner_rho, targets, sources, sums = call(
         density_kernel,
         "density",
-        (
+        tuple(shape(*item.shape, dtype=item.dtype) for item in passed)
+        + (
             shape(BLOCKS, 1, LANES),
             shape(HALO, LANES),
             shape(HALO, LANES),
@@ -312,10 +343,10 @@
             shape(CANDIDATES, LANES, FEATURES, dtype=BF16),
             shape(CANDIDATES, 32, 2 * LANES, dtype=BF16),
         ),
-        [VMEM, VMEM, VMEM, SMEM, SMEM],
-    )(table, below, above, near, picks)
-    rho_below, rho_above = exchange(low, high)
-    return (table, rho, rho_below, rho_above, near, targets, sources, sums)
+        [VMEM, VMEM, VMEM, SMEM, SMEM] + [VMEM] * len(passed),
+    )(table, outer, inner, near, picks, *passed)
+    outer_rho, inner_rho = exchange(outer_rho, inner_rho)
+    return (table, rho, outer_rho, inner_rho, near, targets, sources, sums), passed
 
 
 FORCE_SPECS = [VMEM, VMEM, VMEM, VMEM, SMEM, VMEM, VMEM, VMEM]
@@ -326,27 +357,44 @@
     groups = lax.axis_size("group")
     near_first = jnp.transpose(near_first, (2, 0, 1))
     near_second = jnp.transpose(near_second, (2, 0, 1))
-    table, low, high = call(
+    table, outer, inner = call(
         gather_kernel,
         "gather",
         (TABLE, LISTED, LISTED),
-        [VMEM, VMEM, VMEM, SMEM, SMEM],
-        [pltpu.VMEM((8 * BLOCKS, LANES), F32)],
+        [HBM] * 5,
+        [
+            pltpu.VMEM((3, BLOCKS, LANES), F32),
+            pltpu.VMEM((3, BLOCKS, LANES), F32),
+            pltpu.VMEM((BLOCKS, LANES), F32),
+            pltpu.VMEM((8 * BLOCKS, LANES), F32),
+            pltpu.SMEM((1, BLOCKS), jnp.int32),
+            pltpu.SMEM((1, 2 * HALO), jnp.int32),
+            pltpu.SemaphoreType.DMA((5,)),
+        ],
+        grant=GATHER_GRANT,
     )(jnp.transpose(x[0], (1, 0, 2)), jnp.transpose(v[0], (1, 0, 2)), masses[0], counts, picks_first)
-    below, above = exchange(low, high)
+    outer, inner = exchange(outer, inner)
+    state, (new_slot, picks_second) = half_step(
+        table, outer, inner, near_first, picks_first, (new_slot, picks_second)
+    )
     stay, send = call(
         force_move_kernel,
         "force_move",
         (TABLE, shape(groups, MOVES, 8, LANES)),
-        FORCE_SPECS + [SMEM],
-        FORCE_SCRATCH + [pltpu.SMEM((groups,), jnp.int32)],
-    )(*half_step(table, below, above, near_first, picks_first), new_slot)
+        FORCE_SPECS + [HBM],
+        FORCE_SCRATCH
+        + [pltpu.SMEM((groups,), jnp.int32), pltpu.SMEM((1, BLOCKS), jnp.int32), pltpu.SemaphoreType.DMA],
+    )(*state, new_slot)
     arrived = lax.all_to_all(send, "group", 0, 0)
-    table, low, high = call(
-        arrive_kernel, "arrive", (TABLE, LISTED, LISTED), [VMEM, VMEM, SMEM]
+    table, outer, inner = call(
+        arrive_kernel,
+        "arrive",
+        (TABLE, LISTED, LISTED),
+        [VMEM, VMEM, HBM],
+        [pltpu.SMEM((1, 2 * HALO), jnp.int32), pltpu.SemaphoreType.DMA],
     )(stay, arrived, picks_second)
-    below, above = exchange(low, high)
-    state = half_step(table, below, above, near_second, picks_second)
+    outer, inner = exchange(outer, inner)
+    state, _ = half_step(table, outer, inner, near_second, picks_second)
     x_out, v_out = call(
         force_out_kernel,
         "force_out",

time: 96.7 us -> 94.7 us (0.979)
  starting transfers between devices: 50.3 us -> 41.4 us
  waiting for transfers between devices: 3.09 us -> 10.1 us
  local copies, waits for them, and re-layouts: 4.15 us -> 1.54 us
  Pallas kernels: 25.7 us -> 27.1 us
    ppermute x8, starting transfers between devices: 50.3 us -> 41.4 us  [the longest x4 33.7 us: exchange(): lax.ppermute(outer, 'curve', both(odd_first))]
    ppermute x8, waiting for transfers between devices: 3.09 us -> 10.1 us  [the longest x4 5.09 us: exchange(): lax.ppermute(outer, 'curve', both(odd_first))]
    unnamed x20 -> x16, local copies, waits for them, and re-layouts: 4.15 us -> 1.54 us
  transfers between devices with their start and end apart: 8 -> 8, of which waited for: 4 -> 5; matrix products, arithmetic and copies ran while one was open for 0% -> 0% of each run, Pallas kernels for 0% -> 0%
where the time goes in v3:
time: 94.7 us; the launch traced here: 93.3 us
  starting transfers between devices  41.4 us (44%)
  Pallas kernels  27.1 us (29%)
  blocking collectives  12.3 us (13%)
  waiting for transfers between devices  10.1 us (11%)
  local copies, waits for them, and re-layouts  1.54 us (2%)
    ppermute x4, starting transfers between devices, exchange(): lax.ppermute(outer, 'curve', both(odd_first))  33.7 us
    all_to_all x1, blocking collectives, body(): arrived = lax.all_to_all(send, 'group', 0, 0)  12.3 us
    pallas_call x1, Pallas kernels, body(): call(force_move_kernel, 'force_move', (TABLE, shape(groups, MOVES, 8, LAN...  9.19 us
    pallas_call x1, Pallas kernels, body(): call(force_out_kernel, 'force_out', (shape(3, BLOCKS, LANES), shape(3, BL...  8.11 us
    pallas_call x2, Pallas kernels, half_step(): call(density_kernel, 'density', tuple((shape(*item.shape, dtype=item.dtyp...  7.72 us
    ppermute x4, starting transfers between devices, exchange(): lax.ppermute(inner, 'curve', both(even_first))  7.68 us
    ppermute x4, waiting for transfers between devices, exchange(): lax.ppermute(outer, 'curve', both(odd_first))  5.09 us
    ppermute x4, waiting for transfers between devices, exchange(): lax.ppermute(inner, 'curve', both(even_first))  5.03 us
  transfers between devices with their start and end apart: 8, of which 5 were waited for; matrix products, arithmetic and copies ran while one was open for 0% of the time, Pallas kernels for 0%

profile of v3, /device:TPU:1, one launch (start us, length us, event | category | flops | bytes accessed | tf_op | source)
XLA Modules:
  0.0 93.3 jit_solution(8062955163155137608)
XLA Ops:
  0.6 1.5 %gather.1 = (f32[16,8,128]{2,1,0:T(8,128)}, f32[4,8,128]{2,1,0:T(8,128)}, f32[4,8,128]{2,1,0:T(8,128)}) custom-call(f32[3,16,128]{2,1,0:T(8,128)} %bitcast.21, f32[3,16,128]{2,1,0:T(8,128)} %bitcast.22, f32[16,128]{1,0:T(8,128)} %bitcast.23, s32[1,16]{1,0:T(1,128)} %counts_hbm.1, s32[1,8]{1,0:T(1,128)} %picks_ref.1), custom_call_target="tpu_custom_call" | custom-call | bytes 200000 | tf_op jit(solution)/shard_map/gather/pallas_call | solution.py:360
  2.1 0.0 copy-start.2
  2.2 21.4 %collective-permute-start = (f32[4,8,128]{2,1,0:T(8,128)}, f32[4,8,128]{2,1,0:T(8,128)S(1)}, u32[]{:S(2)}, u32[]{:S(2)}) collective-permute-start(f32[4,8,128]{2,1,0:T(8,128)} %get-tuple-element.28), channel_id=1, source_target_pairs={{8,16},{24,32},{40,48},{56,64},{72,80},{88,96},{104,112},{120,128}... | collective-permute-start | bytes 49160 | tf_op jit(solution)/shard_map/ppermute | solution.py:330
  23.6 1.9 %collective-permute-start.1 = (f32[4,8,128]{2,1,0:T(8,128)}, f32[4,8,128]{2,1,0:T(8,128)S(1)}, u32[]{:S(2)}, u32[]{:S(2)}) collective-permute-start(f32[4,8,128]{2,1,0:T(8,128)} %get-tuple-element.29), channel_id=1, source_target_pairs={{0,8},{16,24},{32,40},{48,56},{64,72},{80,88},{96,104},{112,120},{... | collective-permute-start | bytes 49160 | tf_op jit(solution)/shard_map/ppermute | solution.py:330
  25.5 0.0 collective-permute-done.outer_ref
  25.5 2.8 %collective-permute-done.1.inner_ref = f32[4,8,128]{2,1,0:T(8,128)S(1)} collective-permute-done((f32[4,8,128]{2,1,0:T(8,128)}, f32[4,8,128]{2,1,0:T(8,128)S(1)}, u32[]{:S(2)}, u32[]{:S(2)}) %collective-permute-start.1) | collective-permute-done | bytes 16416 | tf_op jit(solution)/shard_map/ppermute | solution.py:330
  28.3 0.0 copy-done.2
  28.3 0.6 copy-done.5
  28.9 0.0 copy-done.6
  28.9 0.0 copy-done.7
  29.0 0.8 copy-done
  29.8 3.6 %density.2 = (s32[1,16]{1,0:T(1,128)S(1)}, s32[1,8]{1,0:T(1,128)S(1)}, f32[16,1,128]{2,1,0:T(1,128)S(1)}, f32[4,128]{1,0:T(4,128)S(1)}, f32[4,128]{1,0:T(4,128)S...) custom-call(f32[16,8,128]{2,1,0:T(8,128)S(1)} %copy-done, ...), custom_call_target="tpu_custom_call" | custom-call | bytes 200000 | tf_op jit(solution)/shard_map/density/pallas_call | solution.py:334
  33.4 3.3 %collective-permute-start.2 = (f32[4,128]{1,0:T(4,128)S(1)}, f32[4,128]{1,0:T(4,128)S(1)}, u32[]{:S(2)}, u32[]{:S(2)}) collective-permute-start(f32[4,128]{1,0:T(4,128)S(1)} %get-tuple-element.31), channel_id=1, source_target_pairs={{8,16},{24,32},{40,48},{56,64},{72,80},{88,96},{104,112},{120,128}... | collective-permute-start | bytes 6152 | tf_op jit(solution)/shard_map/ppermute | solution.py:330
  36.7 1.9 %collective-permute-start.3 = (f32[4,128]{1,0:T(4,128)S(1)}, f32[4,128]{1,0:T(4,128)S(1)}, u32[]{:S(2)}, u32[]{:S(2)}) collective-permute-start(f32[4,128]{1,0:T(4,128)S(1)} %get-tuple-element.32), channel_id=1, source_target_pairs={{0,8},{16,24},{32,40},{48,56},{64,72},{80,88},{96,104},{112,120},{... | collective-permute-start | bytes 6152 | tf_op jit(solution)/shard_map/ppermute | solution.py:330
  38.6 2.4 %collective-permute-done.2.outer_ref = f32[4,128]{1,0:T(4,128)S(1)} collective-permute-done((f32[4,128]{1,0:T(4,128)S(1)}, f32[4,128]{1,0:T(4,128)S(1)}, u32[]{:S(2)}, u32[]{:S(2)}) %collective-permute-start.2) | collective-permute-done | bytes 2080 | tf_op jit(solution)/shard_map/ppermute | solution.py:330
  41.0 0.0 collective-permute-done.3.inner_ref
  41.0 0.0 copy-done.1
  41.0 9.2 %force_move.1 = (f32[16,8,128]{2,1,0:T(8,128)S(1)}, f32[8,2,8,128]{3,2,1,0:T(8,128)S(1)}) custom-call(f32[16,8,128]{2,1,0:T(8,128)S(1)} %copy-done.1, f32[16,1,128]{2,1,0:T(1,128)S(1)} %get-tuple-element.30.rho_ref, f32[4,128]{1,0:T(4,128)S(1)} %collective-permute-done.2.outer_ref, f32[4,128]{1,0:T(4,128)S(1)} %collective-permute-done.3.inner_ref, ...), custom_call_target="tpu_custom_call" | custom-call | bytes 200000 | tf_op jit(solution)/shard_map/force_move/pallas_call | solution.py:380
  50.2 12.3 %all_to_all.5.arrived_ref = f32[8,2,8,128]{3,2,1,0:T(8,128)S(1)} all-to-all(f32[8,2,8,128]{3,2,1,0:T(8,128)S(1)} %get-tuple-element.38), channel_id=1, replica_groups=mesh['curve'=128,'group'=8] {'group'}, dimensions={0} | all-to-all | bytes 131072 | tf_op jit(solution)/shard_map/all_to_all | solution.py:388
  62.6 0.6 arrive.1
  63.2 0.0 copy-start.3
  63.2 5.5 %collective-permute-start.4 = (f32[4,8,128]{2,1,0:T(8,128)S(1)}, f32[4,8,128]{2,1,0:T(8,128)S(1)}, u32[]{:S(2)}, u32[]{:S(2)}) collective-permute-start(f32[4,8,128]{2,1,0:T(8,128)S(1)} %get-tuple-element.41), channel_id=1, source_target_pairs={{8,16},{24,32},{40,48},{56,64},{72,80},{88,96},{104,112},{120,128}... | collective-permute-start | bytes 49160 | tf_op jit(solution)/shard_map/ppermute | solution.py:330
  68.7 1.9 %collective-permute-start.5 = (f32[4,8,128]{2,1,0:T(8,128)S(1)}, f32[4,8,128]{2,1,0:T(8,128)S(1)}, u32[]{:S(2)}, u32[]{:S(2)}) collective-permute-start(f32[4,8,128]{2,1,0:T(8,128)S(1)} %get-tuple-element.42), channel_id=1, source_target_pairs={{0,8},{16,24},{32,40},{48,56},{64,72},{80,88},{96,104},{112,120},{... | collective-permute-start | bytes 49160 | tf_op jit(solution)/shard_map/ppermute | solution.py:330
  70.7 0.3 collective-permute-done.4.outer_ref
  71.0 2.2 %collective-permute-done.5.inner_ref = f32[4,8,128]{2,1,0:T(8,128)S(1)} collective-permute-done((f32[4,8,128]{2,1,0:T(8,128)S(1)}, f32[4,8,128]{2,1,0:T(8,128)S(1)}, u32[]{:S(2)}, u32[]{:S(2)}) %collective-permute-start.5) | collective-permute-done | bytes 16416 | tf_op jit(solution)/shard_map/ppermute | solution.py:330
  73.2 0.0 copy-done.3
  73.2 4.2 %density.3 = (f32[16,1,128]{2,1,0:T(1,128)}, f32[4,128]{1,0:T(4,128)S(1)}, f32[4,128]{1,0:T(4,128)S(1)}, bf16[16,64,384]{2,1,0:T(8,128)(2,1)S(1)}, bf16[24,128,6...) custom-call(f32[16,8,128]{2,1,0:T(8,128)S(1)} %get-tuple-element.40.table_ref, ...), custom_call_target="tpu_custom_call" | custom-call | bytes 200000 | tf_op jit(solution)/shard_map/density/pallas_call | solution.py:334
  77.4 3.5 %collective-permute-start.6 = (f32[4,128]{1,0:T(4,128)S(1)}, f32[4,128]{1,0:T(4,128)S(1)}, u32[]{:S(2)}, u32[]{:S(2)}) collective-permute-start(f32[4,128]{1,0:T(4,128)S(1)} %get-tuple-element.44), channel_id=1, source_target_pairs={{8,16},{24,32},{40,48},{56,64},{72,80},{88,96},{104,112},{120,128}... | collective-permute-start | bytes 6152 | tf_op jit(solution)/shard_map/ppermute | solution.py:330
  80.8 1.9 %collective-permute-start.7 = (f32[4,128]{1,0:T(4,128)S(1)}, f32[4,128]{1,0:T(4,128)S(1)}, u32[]{:S(2)}, u32[]{:S(2)}) collective-permute-start(f32[4,128]{1,0:T(4,128)S(1)} %get-tuple-element.45), channel_id=1, source_target_pairs={{0,8},{16,24},{32,40},{48,56},{64,72},{80,88},{96,104},{112,120},{... | collective-permute-start | bytes 6152 | tf_op jit(solution)/shard_map/ppermute | solution.py:330
  82.8 2.4 %collective-permute-done.6.outer_ref = f32[4,128]{1,0:T(4,128)S(1)} collective-permute-done((f32[4,128]{1,0:T(4,128)S(1)}, f32[4,128]{1,0:T(4,128)S(1)}, u32[]{:S(2)}, u32[]{:S(2)}) %collective-permute-start.6) | collective-permute-done | bytes 2080 | tf_op jit(solution)/shard_map/ppermute | solution.py:330
  85.1 0.0 collective-permute-done.7.inner_ref
  85.2 8.1 %force_out.1 = (f32[3,16,128]{2,1,0:T(8,128)}, f32[3,16,128]{2,1,0:T(8,128)}) custom-call(f32[16,8,128]{2,1,0:T(8,128)S(1)} %get-tuple-element.40.table_ref, f32[16,1,128]{2,1,0:T(1,128)S(1)} %copy-done.4, f32[4,128]{1,0:T(4,128)S(1)} %collective-permute-done.6.outer_ref, f32[4,128]{1,0:T(4,128)S(1)} %collective-permute-done.7.inner_ref, ...), custom_call_target="tpu_custom_call" | custom-call | bytes 200000 | tf_op jit(solution)/shard_map/force_out/pallas_call | solution.py:398
  (7 shorter events, 0.0 us)
Async XLA Ops:
  2.1 26.1 %copy-start.2 = (s32[1,16,6]{1,0,2:T(1,128)S(1)}, s32[1,16,6]{1,0,2:T(1,128)}, u32[]{:S(2)}) copy-start(s32[1,16,6]{1,0,2:T(1,128)} %param.13) | copy-start | bytes 1156
  2.2 23.3 %collective-permute-start = (f32[4,8,128]{2,1,0:T(8,128)}, f32[4,8,128]{2,1,0:T(8,128)S(1)}, u32[]{:S(2)}, u32[]{:S(2)}) collective-permute-start(f32[4,8,128]{2,1,0:T(8,128)} %get-tuple-element.28), channel_id=1, source_target_pairs={{8,16},{24,32},{40,48},{56,64},{72,80},{88,96},{104,112},{120,128}... | collective-permute-start | bytes 49160 | tf_op jit(solution)/shard_map/ppermute | solution.py:330
  23.6 4.7 %collective-permute-start.1 = (f32[4,8,128]{2,1,0:T(8,128)}, f32[4,8,128]{2,1,0:T(8,128)S(1)}, u32[]{:S(2)}, u32[]{:S(2)}) collective-permute-start(f32[4,8,128]{2,1,0:T(8,128)} %get-tuple-element.29), channel_id=1, source_target_pairs={{0,8},{16,24},{32,40},{48,56},{64,72},{80,88},{96,104},{112,120},{... | collective-permute-start | bytes 49160 | tf_op jit(solution)/shard_map/ppermute | solution.py:330
  28.3 0.7 copy-start.5
  28.3 0.7 copy-start.6
  28.3 0.7 copy-start.7
  29.0 0.8 copy-start
  29.8 11.2 %copy-start.1 = (f32[16,8,128]{2,1,0:T(8,128)S(1)}, f32[16,8,128]{2,1,0:T(8,128)}, u32[]{:S(2)}) copy-start(f32[16,8,128]{2,1,0:T(8,128)} %get-tuple-element.27.table_ref) | copy-start | bytes 196612
  33.4 7.6 %collective-permute-start.2 = (f32[4,128]{1,0:T(4,128)S(1)}, f32[4,128]{1,0:T(4,128)S(1)}, u32[]{:S(2)}, u32[]{:S(2)}) collective-permute-start(f32[4,128]{1,0:T(4,128)S(1)} %get-tuple-element.31), channel_id=1, source_target_pairs={{8,16},{24,32},{40,48},{56,64},{72,80},{88,96},{104,112},{120,128}... | collective-permute-start | bytes 6152 | tf_op jit(solution)/shard_map/ppermute | solution.py:330
  36.7 4.3 %collective-permute-start.3 = (f32[4,128]{1,0:T(4,128)S(1)}, f32[4,128]{1,0:T(4,128)S(1)}, u32[]{:S(2)}, u32[]{:S(2)}) collective-permute-start(f32[4,128]{1,0:T(4,128)S(1)} %get-tuple-element.32), channel_id=1, source_target_pairs={{0,8},{16,24},{32,40},{48,56},{64,72},{80,88},{96,104},{112,120},{... | collective-permute-start | bytes 6152 | tf_op jit(solution)/shard_map/ppermute | solution.py:330
  63.2 10.1 %copy-start.3 = (s32[1,16,6]{1,0,2:T(1,128)S(1)}, s32[1,16,6]{1,0,2:T(1,128)}, u32[]{:S(2)}) copy-start(s32[1,16,6]{1,0,2:T(1,128)} %param.16) | copy-start | bytes 1156
  63.2 7.8 %collective-permute-start.4 = (f32[4,8,128]{2,1,0:T(8,128)S(1)}, f32[4,8,128]{2,1,0:T(8,128)S(1)}, u32[]{:S(2)}, u32[]{:S(2)}) collective-permute-start(f32[4,8,128]{2,1,0:T(8,128)S(1)} %get-tuple-element.41), channel_id=1, source_target_pairs={{8,16},{24,32},{40,48},{56,64},{72,80},{88,96},{104,112},{120,128}... | collective-permute-start | bytes 49160 | tf_op jit(solution)/shard_map/ppermute | solution.py:330
  68.7 4.5 %collective-permute-start.5 = (f32[4,8,128]{2,1,0:T(8,128)S(1)}, f32[4,8,128]{2,1,0:T(8,128)S(1)}, u32[]{:S(2)}, u32[]{:S(2)}) collective-permute-start(f32[4,8,128]{2,1,0:T(8,128)S(1)} %get-tuple-element.42), channel_id=1, source_target_pairs={{0,8},{16,24},{32,40},{48,56},{64,72},{80,88},{96,104},{112,120},{... | collective-permute-start | bytes 49160 | tf_op jit(solution)/shard_map/ppermute | solution.py:330
  77.4 7.8 %copy-start.4 = (f32[16,1,128]{2,1,0:T(1,128)S(1)}, f32[16,1,128]{2,1,0:T(1,128)}, u32[]{:S(2)}) copy-start(f32[16,1,128]{2,1,0:T(1,128)} %get-tuple-element.43.rho_ref) | copy-start | bytes 24580
  77.4 7.8 %collective-permute-start.6 = (f32[4,128]{1,0:T(4,128)S(1)}, f32[4,128]{1,0:T(4,128)S(1)}, u32[]{:S(2)}, u32[]{:S(2)}) collective-permute-start(f32[4,128]{1,0:T(4,128)S(1)} %get-tuple-element.44), channel_id=1, source_target_pairs={{8,16},{24,32},{40,48},{56,64},{72,80},{88,96},{104,112},{120,128}... | collective-permute-start | bytes 6152 | tf_op jit(solution)/shard_map/ppermute | solution.py:330
  80.8 4.3 %collective-permute-start.7 = (f32[4,128]{1,0:T(4,128)S(1)}, f32[4,128]{1,0:T(4,128)S(1)}, u32[]{:S(2)}, u32[]{:S(2)}) collective-permute-start(f32[4,128]{1,0:T(4,128)S(1)} %get-tuple-element.45), channel_id=1, source_target_pairs={{0,8},{16,24},{32,40},{48,56},{64,72},{80,88},{96,104},{112,120},{... | collective-permute-start | bytes 6152 | tf_op jit(solution)/shard_map/ppermute | solution.py:330

commit v4 on v3

--- a/solution.py
+++ b/solution.py
@@ -6,6 +6,7 @@
 from jax.experimental import pallas as pl
 from jax.experimental.pallas import tpu as pltpu
 from jax.sharding import PartitionSpec as P
+
 
 SOFTENING = 0.0025
 BACKGROUND = 0.5
@@ -147,44 +148,62 @@
     list_blocks(table_ref, picks_ref, outer_ref, inner_ref)
 
 
-def density_kernel(table_ref, outer_ref, inner_ref, near_ref, picks_ref, *refs):
-    rho_ref, outer_out_ref, inner_out_ref, target_ref, source_ref, sum_ref = refs[-6:]
-    passed = (len(refs) - 6) // 2
+def features_kernel(table_ref, *refs):
+    target_ref, source_ref, sum_ref = refs[-3:]
+    passed = (len(refs) - 3) // 2
     for n in range(passed):
         refs[passed + n][...] = refs[n][...]
     base = base_of_segment()
-    odd = parity()
     rows = tile_rows()
-
-    def put(tile, at):
-        features, summed = source_features(tile, base, rows)
-        source_ref[at] = features
-        sum_ref[at] = summed
 
     def own(b, carry):
         tile = table_ref[b]
-        put(tile, b)
+        source_ref[b], sum_ref[b] = source_features(tile, base, rows)
         parts = target_features(tile, base, rows)
         for n in range(3):
             target_ref[b, :, n * LANES : (n + 1) * LANES] = parts[n]
         return carry
 
     lax.fori_loop(0, BLOCKS, own, 0, unroll=4)
+
+
+def density_of(j, target_ref, source_ref, near_ref):
+    right = target_ref[j, :, 2 * LANES : 3 * LANES]
+    sources = [j] + [near_ref[n, 0, j] for n in range(NBR)]
+    left = jnp.concatenate([source_ref[s] for s in sources], axis=0)
+    weight = jnp.exp2(jnp.dot(left, right, preferred_element_type=F32))
+    return BACKGROUND + jnp.sum(weight, axis=0, keepdims=True)
+
+
+def listed_density_kernel(
+    outer_ref, inner_ref, near_ref, picks_ref, target_ref, own_source_ref, own_sum_ref,
+    outer_out_ref, source_ref, sum_ref,
+):
+    base = base_of_segment()
+    odd = parity()
+    rows = tile_rows()
+    for b in range(BLOCKS):
+        source_ref[b] = own_source_ref[b]
+        sum_ref[b] = own_sum_ref[b]
     for h in range(HALO):
-        put(outer_ref[h], BLOCKS + odd * HALO + h)
-        put(inner_ref[h], BLOCKS + (1 - odd) * HALO + h)
+        for block_ref, side in ((outer_ref, odd), (inner_ref, 1 - odd)):
+            at = BLOCKS + side * HALO + h
+            source_ref[at], sum_ref[at] = source_features(block_ref[h], base, rows)
+
+    for h in range(HALO):
+        j = picks_ref[0, odd * HALO + h]
+        outer_out_ref[pl.ds(h, 1), :] = density_of(j, target_ref, source_ref, near_ref)
+
+
+def density_kernel(near_ref, picks_ref, target_ref, source_ref, rho_ref, inner_out_ref):
+    odd = parity()
 
     def target(j, carry):
-        right = target_ref[j, :, 2 * LANES : 3 * LANES]
-        sources = [j] + [near_ref[n, 0, j] for n in range(NBR)]
-        left = jnp.concatenate([source_ref[s] for s in sources], axis=0)
-        weight = jnp.exp2(jnp.dot(left, right, preferred_element_type=F32))
-        rho_ref[j] = BACKGROUND + jnp.sum(weight, axis=0, keepdims=True)
+        rho_ref[j] = density_of(j, target_ref, source_ref, near_ref)
         return carry
 
     lax.fori_loop(0, BLOCKS, target, 0, unroll=2)
     for h in range(HALO):
-        outer_out_ref[pl.ds(h, 1), :] = rho_ref[picks_ref[0, odd * HALO + h]]
         inner_out_ref[pl.ds(h, 1), :] = rho_ref[picks_ref[0, (1 - odd) * HALO + h]]
 
 
@@ -236,7 +255,7 @@
 
 def force_move_kernel(
     table_ref, rho_ref, outer_ref, inner_ref, near_ref, target_ref, source_ref, sum_ref, slot_hbm,
-    stay_ref, send_ref, rho_of, inverse_of, filled, slot_ref, sem,
+    stay_ref, send_ref, rho_of, inverse_of, filled, slot_ref, sem, moved_ref,
 ):
     copy = pltpu.make_async_copy(slot_hbm, slot_ref, sem)
     copy.start()
@@ -252,9 +271,16 @@
     copy.wait()
 
     def done(b, tile):
+        moved_ref[b] = tile
+
+    advance(
+        table_ref, rho_ref, outer_ref, inner_ref, near_ref, target_ref, source_ref, sum_ref, rho_of, inverse_of, done
+    )
+
+    def route(b, carry):
         owner = slot_ref[0, b] // BLOCKS
         slot = slot_ref[0, b] % BLOCKS
-        tagged = jnp.where(rows == 7, jnp.full((8, LANES), slot, jnp.int32).astype(F32), tile)
+        tagged = jnp.where(rows == 7, jnp.full((8, LANES), slot, jnp.int32).astype(F32), moved_ref[b])
 
         @pl.when(owner == me)
         def _():
@@ -266,9 +292,9 @@
             send_ref[owner, place] = tagged
             filled[owner] = place + 1
 
-    advance(
-        table_ref, rho_ref, outer_ref, inner_ref, near_ref, target_ref, source_ref, sum_ref, rho_of, inverse_of, done
-    )
+        return carry
+
+    lax.fori_loop(0, BLOCKS, route, 0)
 
 
 def arrive_kernel(stay_ref, arrived_ref, picks_hbm, table_ref, outer_ref, inner_ref, picks_ref, sem):
@@ -288,7 +314,7 @@
 
 def force_out_kernel(
     table_ref, rho_ref, outer_ref, inner_ref, near_ref, target_ref, source_ref, sum_ref,
-    x_ref, v_ref, rho_of, inverse_of, flat_ref,
+    x_ref, v_ref, rho_out_ref, rho_of, inverse_of, flat_ref,
 ):
     def done(b, tile):
         flat_ref[pl.ds(pl.multiple_of(8 * b, 8), 8), :] = tile
@@ -296,6 +322,8 @@
     advance(
         table_ref, rho_ref, outer_ref, inner_ref, near_ref, target_ref, source_ref, sum_ref, rho_of, inverse_of, done
     )
+    for b in range(BLOCKS):
+        rho_out_ref[pl.ds(b, 1), :] = rho_ref[b]
     for axis_id in range(3):
         x_ref[axis_id] = flat_ref[pl.ds(axis_id, BLOCKS, stride=8), :]
         v_ref[axis_id] = flat_ref[pl.ds(3 + axis_id, BLOCKS, stride=8), :]
@@ -309,10 +337,9 @@
 LISTED = shape(HALO, 8, LANES)
 
 
-def call(kernel, name, out_shape, in_specs, scratch=(), flops=0, grant=16 << 20):
+def call(kernel, out_shape, in_specs, scratch=(), flops=0, grant=16 << 20):
     return pl.pallas_call(
         kernel,
-        name=name,
         out_shape=out_shape,
         in_specs=in_specs,
         out_specs=[VMEM] * len(out_shape),
@@ -322,30 +349,46 @@
     )
 
 
-def exchange(outer, inner):
+def swap_outer(item):
     count = lax.axis_size("curve")
-    odd_first = [(i, (i + 1) % count) for i in range(1, count, 2)]
-    even_first = [(i, i + 1) for i in range(0, count, 2)]
-    both = lambda pairs: pairs + [(target, source) for source, target in pairs]
-    return lax.ppermute(outer, "curve", both(odd_first)), lax.ppermute(inner, "curve", both(even_first))
+    pairs = [(i, (i + 1) % count) for i in range(1, count, 2)]
+    return lax.ppermute(item, "curve", pairs + [(target, source) for source, target in pairs])
+
+
+def swap_inner(item):
+    pairs = [(i, i + 1) for i in range(0, lax.axis_size("curve"), 2)]
+    return lax.ppermute(item, "curve", pairs + [(target, source) for source, target in pairs])
+
+
+SOURCES = (
+    shape(CANDIDATES, LANES, FEATURES, dtype=BF16),
+    shape(CANDIDATES, 32, 2 * LANES, dtype=BF16),
+)
+OWN_SOURCES = (
+    shape(BLOCKS, LANES, FEATURES, dtype=BF16),
+    shape(BLOCKS, 32, 2 * LANES, dtype=BF16),
+)
 
 
 def half_step(table, outer, inner, near, picks, passed=()):
-    *passed, rho, outer_rho, inner_rho, targets, sources, sums = call(
-        density_kernel,
-        "density",
+    outer = swap_outer(outer)
+    inner = swap_inner(inner)
+    passed = (near, picks) + tuple(passed)
+    near, picks, *passed, targets, own_source, own_sum = call(
+        features_kernel,
         tuple(shape(*item.shape, dtype=item.dtype) for item in passed)
-        + (
-            shape(BLOCKS, 1, LANES),
-            shape(HALO, LANES),
-            shape(HALO, LANES),
-            shape(BLOCKS, FEATURES, 3 * LANES, dtype=BF16),
-            shape(CANDIDATES, LANES, FEATURES, dtype=BF16),
-            shape(CANDIDATES, 32, 2 * LANES, dtype=BF16),
-        ),
-        [VMEM, VMEM, VMEM, SMEM, SMEM] + [VMEM] * len(passed),
-    )(table, outer, inner, near, picks, *passed)
-    outer_rho, inner_rho = exchange(outer_rho, inner_rho)
+        + (shape(BLOCKS, FEATURES, 3 * LANES, dtype=BF16),)
+        + OWN_SOURCES,
+        [VMEM] * (1 + len(passed)),
+    )(table, *passed)
+    outer_rho, sources, sums = call(
+        listed_density_kernel, (shape(HALO, LANES),) + SOURCES, [VMEM, VMEM, SMEM, SMEM, VMEM, VMEM, VMEM]
+    )(outer, inner, near, picks, targets, own_source, own_sum)
+    outer_rho = swap_outer(outer_rho)
+    rho, inner_rho = call(
+        density_kernel, (shape(BLOCKS, 1, LANES), shape(HALO, LANES)), [SMEM, SMEM, VMEM, VMEM]
+    )(near, picks, targets, sources)
+    inner_rho = swap_inner(inner_rho)
     return (table, rho, outer_rho, inner_rho, near, targets, sources, sums), passed
 
 
@@ -359,7 +402,6 @@
     near_second = jnp.transpose(near_second, (2, 0, 1))
     table, outer, inner = call(
         gather_kernel,
-        "gather",
         (TABLE, LISTED, LISTED),
         [HBM] * 5,
         [
@@ -373,37 +415,30 @@
         ],
         grant=GATHER_GRANT,
     )(jnp.transpose(x[0], (1, 0, 2)), jnp.transpose(v[0], (1, 0, 2)), masses[0], counts, picks_first)
-    outer, inner = exchange(outer, inner)
-    state, (new_slot, picks_second) = half_step(
-        table, outer, inner, near_first, picks_first, (new_slot, picks_second)
-    )
+    state, (new_slot, picks_second) = half_step(table, outer, inner, near_first, picks_first, (new_slot, picks_second))
     stay, send = call(
         force_move_kernel,
-        "force_move",
         (TABLE, shape(groups, MOVES, 8, LANES)),
         FORCE_SPECS + [HBM],
         FORCE_SCRATCH
-        + [pltpu.SMEM((groups,), jnp.int32), pltpu.SMEM((1, BLOCKS), jnp.int32), pltpu.SemaphoreType.DMA],
+        + [pltpu.SMEM((groups,), jnp.int32), pltpu.SMEM((1, BLOCKS), jnp.int32), pltpu.SemaphoreType.DMA]
+        + [pltpu.VMEM((BLOCKS, 8, LANES), F32)],
     )(*state, new_slot)
     arrived = lax.all_to_all(send, "group", 0, 0)
     table, outer, inner = call(
         arrive_kernel,
-        "arrive",
         (TABLE, LISTED, LISTED),
         [VMEM, VMEM, HBM],
         [pltpu.SMEM((1, 2 * HALO), jnp.int32), pltpu.SemaphoreType.DMA],
     )(stay, arrived, picks_second)
-    outer, inner = exchange(outer, inner)
     state, _ = half_step(table, outer, inner, near_second, picks_second)
-    x_out, v_out = call(
+    x_out, v_out, rho = call(
         force_out_kernel,
-        "force_out",
-        (shape(3, BLOCKS, LANES), shape(3, BLOCKS, LANES)),
+        (shape(3, BLOCKS, LANES), shape(3, BLOCKS, LANES), shape(BLOCKS, LANES)),
         FORCE_SPECS,
         FORCE_SCRATCH + [pltpu.VMEM((8 * BLOCKS, LANES), F32)],
     )(*state)
-    rho = state[1].reshape(1, BLOCKS, LANES)
-    return jnp.transpose(x_out, (1, 0, 2))[None], jnp.transpose(v_out, (1, 0, 2))[None], rho
+    return jnp.transpose(x_out, (1, 0, 2))[None], jnp.transpose(v_out, (1, 0, 2))[None], rho[None]
 
 
 def solution(mesh):

time: 94.7 us -> 94.4 us (level)
    pallas_call x6 -> x10, Pallas kernels: 27.1 us -> 27.8 us  [the longest x1 8.42 us: body(): call(force_move_kernel, (TABLE, shape(groups, MOVES, 8, LANES)), FORCE_SP...]
  transfers between devices with their start and end apart: 8 -> 8, of which waited for: 5 -> 5; matrix products, arithmetic and copies ran while one was open for 0% -> 0% of each run, Pallas kernels for 0% -> 1%
where the time goes in v4:
time: 94.4 us; the launch traced here: 93.3 us
  starting transfers between devices  40.8 us (43%)
  Pallas kernels  27.8 us (29%)
  blocking collectives  11.8 us (12%)
  waiting for transfers between devices  10.6 us (11%)
  local copies, waits for them, and re-layouts  1.51 us (2%)
    ppermute x4, starting transfers between devices, swap_outer(): lax.ppermute(item, 'curve', pairs + [(target, source) for source, target...  32.2 us
    all_to_all x1, blocking collectives, body(): arrived = lax.all_to_all(send, 'group', 0, 0)  11.8 us
    ppermute x4, waiting for transfers between devices, swap_outer(): lax.ppermute(item, 'curve', pairs + [(target, source) for source, target...  9.69 us
    ppermute x4, starting transfers between devices, swap_inner(): lax.ppermute(item, 'curve', pairs + [(target, source) for source, target...  8.55 us
    pallas_call x1, Pallas kernels, body(): call(force_move_kernel, (TABLE, shape(groups, MOVES, 8, LANES)), FORCE_SP...  8.42 us
    pallas_call x1, Pallas kernels, body(): call(force_out_kernel, (shape(3, BLOCKS, LANES), shape(3, BLOCKS, LANES),...  8.13 us
    pallas_call x2, Pallas kernels, half_step(): call(density_kernel, (shape(BLOCKS, 1, LANES), shape(HALO, LANES)), [SMEM...  5.52 us
    pallas_call x2, Pallas kernels, half_step(): call(listed_density_kernel, (shape(HALO, LANES),) + SOURCES, [VMEM, VMEM,...  2.37 us
  transfers between devices with their start and end apart: 8, of which 5 were waited for; matrix products, arithmetic and copies ran while one was open for 0% of the time, Pallas kernels for 1%

profile of v4, /device:TPU:1, one launch (start us, length us, event | category | flops | bytes accessed | tf_op | source)
XLA Modules:
  0.0 93.3 jit_solution(9714658766322705732)
XLA Ops:
  0.6 1.5 %shard_map.112 = (f32[16,8,128]{2,1,0:T(8,128)}, f32[4,8,128]{2,1,0:T(8,128)}, f32[4,8,128]{2,1,0:T(8,128)}) custom-call(f32[3,16,128]{2,1,0:T(8,128)} %bitcast.18, f32[3,16,128]{2,1,0:T(8,128)} %bitcast.19, f32[16,128]{1,0:T(8,128)} %bitcast.20, s32[1,16]{1,0:T(1,128)} %counts_hbm.1, s32[1,8]{1,0:T(1,128)} %refs_1_.1), custom_call_target="tpu_custom_call" | custom-call | bytes 200000 | tf_op jit(solution)/shard_map/pallas_call | solution.py:403
  2.1 0.0 copy-start.2
  2.2 21.4 %collective-permute-start = (f32[4,8,128]{2,1,0:T(8,128)}, f32[4,8,128]{2,1,0:T(8,128)S(1)}, u32[]{:S(2)}, u32[]{:S(2)}) collective-permute-start(f32[4,8,128]{2,1,0:T(8,128)} %get-tuple-element.40), channel_id=1, source_target_pairs={{8,16},{24,32},{40,48},{56,64},{72,80},{88,96},{104,112},{120,128}... | collective-permute-start | bytes 49160 | tf_op jit(solution)/shard_map/ppermute | solution.py:355
  23.6 1.9 %collective-permute-start.1 = (f32[4,8,128]{2,1,0:T(8,128)}, f32[4,8,128]{2,1,0:T(8,128)S(1)}, u32[]{:S(2)}, u32[]{:S(2)}) collective-permute-start(f32[4,8,128]{2,1,0:T(8,128)} %get-tuple-element.41), channel_id=1, source_target_pairs={{0,8},{16,24},{32,40},{48,56},{64,72},{80,88},{96,104},{112,120},{... | collective-permute-start | bytes 49160 | tf_op jit(solution)/shard_map/ppermute | solution.py:360
  25.5 0.0 copy-start.4
  25.5 0.0 copy-start.5
  25.5 0.0 copy-start.6
  25.6 0.6 copy-done.4
  26.2 0.0 copy-done.5
  26.2 0.0 copy-done.6
  26.2 0.8 copy-done
  27.0 0.6 shard_map.113
  27.7 0.6 collective-permute-done.1.inner_ref
  28.3 1.2 %shard_map.114 = (f32[4,128]{1,0:T(4,128)S(1)}, bf16[24,128,64]{2,1,0:T(8,128)(2,1)S(1)}, bf16[24,32,256]{2,1,0:T(8,128)(2,1)S(1)}) custom-call(f32[4,8,128]{2,1,0:T(8,128)S(1)} %collective-permute-done.outer_ref, f32[4,8,128]{2,1,0:T(8,128)S(1)} %collective-permute-done.1.inner_ref, s32[6,1,16]{2,1,0:T(1,128)S(1)} %get-tuple-element.37.near_ref, ...), custom_call_target="tpu_custom_call" | custom-call | bytes 200000 | tf_op jit(solution)/shard_map/pallas_call | solution.py:384
  29.5 2.8 %shard_map.115 = (f32[16,1,128]{2,1,0:T(1,128)S(1)}, f32[4,128]{1,0:T(4,128)S(1)}) custom-call(s32[6,1,16]{2,1,0:T(1,128)S(1)} %get-tuple-element.37.near_ref, s32[1,8]{1,0:T(1,128)S(1)} %get-tuple-element.38.picks_ref, bf16[16,64,384]{2,1,0:T(8,128)(2,1)S(1)} %get-tuple-element.39.target_ref, bf16[24,128,64]{2,1,0:T(8,128)(2,1)S(1)} %get-tuple-element.44.source_ref), custom_call_target="tpu_custom_call" | custom-call | bytes 200000 | tf_op jit(solution)/shard_map/pallas_call | solution.py:388
  32.2 2.8 %collective-permute-start.3 = (f32[4,128]{1,0:T(4,128)S(1)}, f32[4,128]{1,0:T(4,128)S(1)}, u32[]{:S(2)}, u32[]{:S(2)}) collective-permute-start(f32[4,128]{1,0:T(4,128)S(1)} %get-tuple-element.47), channel_id=1, source_target_pairs={{0,8},{16,24},{32,40},{48,56},{64,72},{80,88},{96,104},{112,120},{... | collective-permute-start | bytes 6152 | tf_op jit(solution)/shard_map/ppermute | solution.py:360
  35.0 2.5 %collective-permute-start.2 = (f32[4,128]{1,0:T(4,128)S(1)}, f32[4,128]{1,0:T(4,128)S(1)}, u32[]{:S(2)}, u32[]{:S(2)}) collective-permute-start(f32[4,128]{1,0:T(4,128)S(1)} %get-tuple-element.46), channel_id=1, source_target_pairs={{8,16},{24,32},{40,48},{56,64},{72,80},{88,96},{104,112},{120,128}... | collective-permute-start | bytes 6152 | tf_op jit(solution)/shard_map/ppermute | solution.py:355
  37.5 5.1 %collective-permute-done.2.outer_ref = f32[4,128]{1,0:T(4,128)S(1)} collective-permute-done((f32[4,128]{1,0:T(4,128)S(1)}, f32[4,128]{1,0:T(4,128)S(1)}, u32[]{:S(2)}, u32[]{:S(2)}) %collective-permute-start.2) | collective-permute-done | bytes 2080 | tf_op jit(solution)/shard_map/ppermute | solution.py:355
  42.7 8.4 %shard_map.116 = (f32[16,8,128]{2,1,0:T(8,128)S(1)}, f32[8,2,8,128]{3,2,1,0:T(8,128)S(1)}) custom-call(f32[16,8,128]{2,1,0:T(8,128)S(1)} %copy-done.1, f32[16,1,128]{2,1,0:T(1,128)S(1)} %get-tuple-element.45.rho_ref, f32[4,128]{1,0:T(4,128)S(1)} %collective-permute-done.2.outer_ref, f32[4,128]{1,0:T(4,128)S(1)} %collective-permute-done.3.inner_ref, ...), custom_call_target="tpu_custom_call" | custom-call | bytes 200000 | tf_op jit(solution)/shard_map/pallas_call | solution.py:419
  51.1 11.8 %all_to_all.5.arrived_ref = f32[8,2,8,128]{3,2,1,0:T(8,128)S(1)} all-to-all(f32[8,2,8,128]{3,2,1,0:T(8,128)S(1)} %get-tuple-element.51), channel_id=1, replica_groups=mesh['curve'=128,'group'=8] {'group'}, dimensions={0} | all-to-all | bytes 131072 | tf_op jit(solution)/shard_map/all_to_all | solution.py:427
  62.9 0.6 shard_map.117
  63.5 3.3 %collective-permute-start.4 = (f32[4,8,128]{2,1,0:T(8,128)S(1)}, f32[4,8,128]{2,1,0:T(8,128)S(1)}, u32[]{:S(2)}, u32[]{:S(2)}) collective-permute-start(f32[4,8,128]{2,1,0:T(8,128)S(1)} %get-tuple-element.57), channel_id=1, source_target_pairs={{8,16},{24,32},{40,48},{56,64},{72,80},{88,96},{104,112},{120,128}... | collective-permute-start | bytes 49160 | tf_op jit(solution)/shard_map/ppermute | solution.py:355
  66.9 1.9 %collective-permute-start.5 = (f32[4,8,128]{2,1,0:T(8,128)S(1)}, f32[4,8,128]{2,1,0:T(8,128)S(1)}, u32[]{:S(2)}, u32[]{:S(2)}) collective-permute-start(f32[4,8,128]{2,1,0:T(8,128)S(1)} %get-tuple-element.58), channel_id=1, source_target_pairs={{0,8},{16,24},{32,40},{48,56},{64,72},{80,88},{96,104},{112,120},{... | collective-permute-start | bytes 49160 | tf_op jit(solution)/shard_map/ppermute | solution.py:360
  68.8 0.6 shard_map.118
  69.4 1.9 %collective-permute-done.4.outer_ref = f32[4,8,128]{2,1,0:T(8,128)S(1)} collective-permute-done((f32[4,8,128]{2,1,0:T(8,128)S(1)}, f32[4,8,128]{2,1,0:T(8,128)S(1)}, u32[]{:S(2)}, u32[]{:S(2)}) %collective-permute-start.4) | collective-permute-done | bytes 16416 | tf_op jit(solution)/shard_map/ppermute | solution.py:355
  71.3 0.3 collective-permute-done.5.inner_ref
  71.6 1.2 %shard_map.119 = (f32[4,128]{1,0:T(4,128)S(1)}, bf16[24,128,64]{2,1,0:T(8,128)(2,1)S(1)}, bf16[24,32,256]{2,1,0:T(8,128)(2,1)S(1)}) custom-call(f32[4,8,128]{2,1,0:T(8,128)S(1)} %collective-permute-done.4.outer_ref, f32[4,8,128]{2,1,0:T(8,128)S(1)} %collective-permute-done.5.inner_ref, s32[6,1,16]{2,1,0:T(1,128)S(1)} %get-tuple-element.54.near_ref, ...), custom_call_target="tpu_custom_call" | custom-call | bytes 200000 | tf_op jit(solution)/shard_map/pallas_call | solution.py:384
  72.8 2.8 %shard_map.120 = (f32[16,1,128]{2,1,0:T(1,128)S(1)}, f32[4,128]{1,0:T(4,128)S(1)}) custom-call(s32[6,1,16]{2,1,0:T(1,128)S(1)} %get-tuple-element.54.near_ref, s32[1,8]{1,0:T(1,128)S(1)} %get-tuple-element.55.picks_ref, bf16[16,64,384]{2,1,0:T(8,128)(2,1)S(1)} %get-tuple-element.56.target_ref, bf16[24,128,64]{2,1,0:T(8,128)(2,1)S(1)} %get-tuple-element.61.source_ref), custom_call_target="tpu_custom_call" | custom-call | bytes 200000 | tf_op jit(solution)/shard_map/pallas_call | solution.py:388
  75.6 1.9 %collective-permute-start.7 = (f32[4,128]{1,0:T(4,128)S(1)}, f32[4,128]{1,0:T(4,128)S(1)}, u32[]{:S(2)}, u32[]{:S(2)}) collective-permute-start(f32[4,128]{1,0:T(4,128)S(1)} %get-tuple-element.64), channel_id=1, source_target_pairs={{0,8},{16,24},{32,40},{48,56},{64,72},{80,88},{96,104},{112,120},{... | collective-permute-start | bytes 6152 | tf_op jit(solution)/shard_map/ppermute | solution.py:360
  77.5 5.0 %collective-permute-start.6 = (f32[4,128]{1,0:T(4,128)S(1)}, f32[4,128]{1,0:T(4,128)S(1)}, u32[]{:S(2)}, u32[]{:S(2)}) collective-permute-start(f32[4,128]{1,0:T(4,128)S(1)} %get-tuple-element.63), channel_id=1, source_target_pairs={{8,16},{24,32},{40,48},{56,64},{72,80},{88,96},{104,112},{120,128}... | collective-permute-start | bytes 6152 | tf_op jit(solution)/shard_map/ppermute | solution.py:355
  82.5 2.6 %collective-permute-done.6.outer_ref = f32[4,128]{1,0:T(4,128)S(1)} collective-permute-done((f32[4,128]{1,0:T(4,128)S(1)}, f32[4,128]{1,0:T(4,128)S(1)}, u32[]{:S(2)}, u32[]{:S(2)}) %collective-permute-start.6) | collective-permute-done | bytes 2080 | tf_op jit(solution)/shard_map/ppermute | solution.py:355
  85.2 8.1 %shard_map.121 = (f32[3,16,128]{2,1,0:T(8,128)}, f32[3,16,128]{2,1,0:T(8,128)}, f32[16,128]{1,0:T(8,128)}) custom-call(f32[16,8,128]{2,1,0:T(8,128)S(1)} %get-tuple-element.53.table_ref, f32[16,1,128]{2,1,0:T(1,128)S(1)} %get-tuple-element.62.rho_ref, f32[4,128]{1,0:T(4,128)S(1)} %collective-permute-done.6.outer_ref, ...), custom_call_target="tpu_custom_call" | custom-call | bytes 200000 | tf_op jit(solution)/shard_map/pallas_call | solution.py:435
  (9 shorter events, 0.0 us)
Async XLA Ops:
  2.1 23.4 %copy-start.2 = (s32[1,16,6]{1,0,2:T(1,128)S(1)}, s32[1,16,6]{1,0,2:T(1,128)}, u32[]{:S(2)}) copy-start(s32[1,16,6]{1,0,2:T(1,128)} %param.13) | copy-start | bytes 1156
  2.2 25.5 %collective-permute-start = (f32[4,8,128]{2,1,0:T(8,128)}, f32[4,8,128]{2,1,0:T(8,128)S(1)}, u32[]{:S(2)}, u32[]{:S(2)}) collective-permute-start(f32[4,8,128]{2,1,0:T(8,128)} %get-tuple-element.40), channel_id=1, source_target_pairs={{8,16},{24,32},{40,48},{56,64},{72,80},{88,96},{104,112},{120,128}... | collective-permute-start | bytes 49160 | tf_op jit(solution)/shard_map/ppermute | solution.py:355
  23.6 4.7 %collective-permute-start.1 = (f32[4,8,128]{2,1,0:T(8,128)}, f32[4,8,128]{2,1,0:T(8,128)S(1)}, u32[]{:S(2)}, u32[]{:S(2)}) collective-permute-start(f32[4,8,128]{2,1,0:T(8,128)} %get-tuple-element.41), channel_id=1, source_target_pairs={{0,8},{16,24},{32,40},{48,56},{64,72},{80,88},{96,104},{112,120},{... | collective-permute-start | bytes 49160 | tf_op jit(solution)/shard_map/ppermute | solution.py:360
  25.5 0.7 copy-start.4
  25.5 0.7 copy-start.5
  25.5 0.7 copy-start.6
  26.2 0.8 copy-start
  29.5 13.2 %copy-start.1 = (f32[16,8,128]{2,1,0:T(8,128)S(1)}, f32[16,8,128]{2,1,0:T(8,128)}, u32[]{:S(2)}) copy-start(f32[16,8,128]{2,1,0:T(8,128)} %get-tuple-element.36.table_ref) | copy-start | bytes 196612
  32.2 5.3 %collective-permute-start.3 = (f32[4,128]{1,0:T(4,128)S(1)}, f32[4,128]{1,0:T(4,128)S(1)}, u32[]{:S(2)}, u32[]{:S(2)}) collective-permute-start(f32[4,128]{1,0:T(4,128)S(1)} %get-tuple-element.47), channel_id=1, source_target_pairs={{0,8},{16,24},{32,40},{48,56},{64,72},{80,88},{96,104},{112,120},{... | collective-permute-start | bytes 6152 | tf_op jit(solution)/shard_map/ppermute | solution.py:360
  35.0 7.6 %collective-permute-start.2 = (f32[4,128]{1,0:T(4,128)S(1)}, f32[4,128]{1,0:T(4,128)S(1)}, u32[]{:S(2)}, u32[]{:S(2)}) collective-permute-start(f32[4,128]{1,0:T(4,128)S(1)} %get-tuple-element.46), channel_id=1, source_target_pairs={{8,16},{24,32},{40,48},{56,64},{72,80},{88,96},{104,112},{120,128}... | collective-permute-start | bytes 6152 | tf_op jit(solution)/shard_map/ppermute | solution.py:355
  63.5 5.3 %copy-start.3 = (s32[1,16,6]{1,0,2:T(1,128)S(1)}, s32[1,16,6]{1,0,2:T(1,128)}, u32[]{:S(2)}) copy-start(s32[1,16,6]{1,0,2:T(1,128)} %param.16) | copy-start | bytes 1156
  63.5 7.8 %collective-permute-start.4 = (f32[4,8,128]{2,1,0:T(8,128)S(1)}, f32[4,8,128]{2,1,0:T(8,128)S(1)}, u32[]{:S(2)}, u32[]{:S(2)}) collective-permute-start(f32[4,8,128]{2,1,0:T(8,128)S(1)} %get-tuple-element.57), channel_id=1, source_target_pairs={{8,16},{24,32},{40,48},{56,64},{72,80},{88,96},{104,112},{120,128}... | collective-permute-start | bytes 49160 | tf_op jit(solution)/shard_map/ppermute | solution.py:355
  66.9 4.8 %collective-permute-start.5 = (f32[4,8,128]{2,1,0:T(8,128)S(1)}, f32[4,8,128]{2,1,0:T(8,128)S(1)}, u32[]{:S(2)}, u32[]{:S(2)}) collective-permute-start(f32[4,8,128]{2,1,0:T(8,128)S(1)} %get-tuple-element.58), channel_id=1, source_target_pairs={{0,8},{16,24},{32,40},{48,56},{64,72},{80,88},{96,104},{112,120},{... | collective-permute-start | bytes 49160 | tf_op jit(solution)/shard_map/ppermute | solution.py:360
  75.6 6.9 %collective-permute-start.7 = (f32[4,128]{1,0:T(4,128)S(1)}, f32[4,128]{1,0:T(4,128)S(1)}, u32[]{:S(2)}, u32[]{:S(2)}) collective-permute-start(f32[4,128]{1,0:T(4,128)S(1)} %get-tuple-element.64), channel_id=1, source_target_pairs={{0,8},{16,24},{32,40},{48,56},{64,72},{80,88},{96,104},{112,120},{... | collective-permute-start | bytes 6152 | tf_op jit(solution)/shard_map/ppermute | solution.py:360
  77.5 7.6 %collective-permute-start.6 = (f32[4,128]{1,0:T(4,128)S(1)}, f32[4,128]{1,0:T(4,128)S(1)}, u32[]{:S(2)}, u32[]{:S(2)}) collective-permute-start(f32[4,128]{1,0:T(4,128)S(1)} %get-tuple-element.63), channel_id=1, source_target_pairs={{8,16},{24,32},{40,48},{56,64},{72,80},{88,96},{104,112},{120,128}... | collective-permute-start | bytes 6152 | tf_op jit(solution)/shard_map/ppermute | solution.py:355

commit v5 on v4

--- a/solution.py
+++ b/solution.py
@@ -177,7 +177,7 @@
 
 def listed_density_kernel(
     outer_ref, inner_ref, near_ref, picks_ref, target_ref, own_source_ref, own_sum_ref,
-    outer_out_ref, source_ref, sum_ref,
+    outer_out_ref, inner_out_ref, source_ref, sum_ref,
 ):
     base = base_of_segment()
     odd = parity()
@@ -190,21 +190,18 @@
             at = BLOCKS + side * HALO + h
             source_ref[at], sum_ref[at] = source_features(block_ref[h], base, rows)
 
-    for h in range(HALO):
-        j = picks_ref[0, odd * HALO + h]
-        outer_out_ref[pl.ds(h, 1), :] = density_of(j, target_ref, source_ref, near_ref)
-
-
-def density_kernel(near_ref, picks_ref, target_ref, source_ref, rho_ref, inner_out_ref):
-    odd = parity()
-
+    for out_ref, side in ((outer_out_ref, odd), (inner_out_ref, 1 - odd)):
+        for h in range(HALO):
+            j = picks_ref[0, side * HALO + h]
+            out_ref[pl.ds(h, 1), :] = density_of(j, target_ref, source_ref, near_ref)
+
+
+def density_kernel(near_ref, target_ref, source_ref, rho_ref):
     def target(j, carry):
         rho_ref[j] = density_of(j, target_ref, source_ref, near_ref)
         return carry
 
     lax.fori_loop(0, BLOCKS, target, 0, unroll=2)
-    for h in range(HALO):
-        inner_out_ref[pl.ds(h, 1), :] = rho_ref[picks_ref[0, (1 - odd) * HALO + h]]
 
 
 def advance(
@@ -381,14 +378,14 @@
         + OWN_SOURCES,
         [VMEM] * (1 + len(passed)),
     )(table, *passed)
-    outer_rho, sources, sums = call(
-        listed_density_kernel, (shape(HALO, LANES),) + SOURCES, [VMEM, VMEM, SMEM, SMEM, VMEM, VMEM, VMEM]
+    outer_rho, inner_rho, sources, sums = call(
+        listed_density_kernel,
+        (shape(HALO, LANES), shape(HALO, LANES)) + SOURCES,
+        [VMEM, VMEM, SMEM, SMEM, VMEM, VMEM, VMEM],
     )(outer, inner, near, picks, targets, own_source, own_sum)
     outer_rho = swap_outer(outer_rho)
-    rho, inner_rho = call(
-        density_kernel, (shape(BLOCKS, 1, LANES), shape(HALO, LANES)), [SMEM, SMEM, VMEM, VMEM]
-    )(near, picks, targets, sources)
     inner_rho = swap_inner(inner_rho)
+    (rho,) = call(density_kernel, (shape(BLOCKS, 1, LANES),), [SMEM, VMEM, VMEM])(near, targets, sources)
     return (table, rho, outer_rho, inner_rho, near, targets, sources, sums), passed
 
 

time: 94.4 us -> 87.6 us (0.928)
  waiting for transfers between devices: 10.6 us -> 2.5 us
    ppermute x4, waiting for transfers between devices: 9.69 us -> 0.01 us  [swap_outer(): lax.ppermute(item, 'curve', pairs + [(target, source) for source, target...]
    ppermute x4, waiting for transfers between devices: 0.89 us -> 2.49 us  [swap_inner(): lax.ppermute(item, 'curve', pairs + [(target, source) for source, target...]
    ppermute x4, starting transfers between devices: 32.2 us -> 33.6 us  [swap_outer(): lax.ppermute(item, 'curve', pairs + [(target, source) for source, target...]
  transfers between devices with their start and end apart: 8 -> 8, of which waited for: 5 -> 2; matrix products, arithmetic and copies ran while one was open for 0% -> 0% of each run, Pallas kernels for 1% -> 8%
where the time goes in v5:
time: 87.6 us; the launch traced here: 86.3 us
  starting transfers between devices  41.3 us (47%)
  Pallas kernels  28.1 us (32%)
  blocking collectives  12 us (14%)
  waiting for transfers between devices  2.5 us (3%)
  local copies, waits for them, and re-layouts  1.51 us (2%)
  between operations  0.88 us (1%)
    ppermute x4, starting transfers between devices, swap_outer(): lax.ppermute(item, 'curve', pairs + [(target, source) for source, target...  33.6 us
    all_to_all x1, blocking collectives, body(): arrived = lax.all_to_all(send, 'group', 0, 0)  12 us
    pallas_call x1, Pallas kernels, body(): call(force_move_kernel, (TABLE, shape(groups, MOVES, 8, LANES)), FORCE_SP...  8.37 us
    pallas_call x1, Pallas kernels, body(): call(force_out_kernel, (shape(3, BLOCKS, LANES), shape(3, BLOCKS, LANES),...  8.11 us
    ppermute x4, starting transfers between devices, swap_inner(): lax.ppermute(item, 'curve', pairs + [(target, source) for source, target...  7.68 us
    pallas_call x2, Pallas kernels, half_step(): call(density_kernel, (shape(BLOCKS, 1, LANES),), [SMEM, VMEM, VMEM])  5.48 us
    pallas_call x2, Pallas kernels, half_step(): call(listed_density_kernel, (shape(HALO, LANES), shape(HALO, LANES)) + SO...  2.84 us
    ppermute x4, waiting for transfers between devices, swap_inner(): lax.ppermute(item, 'curve', pairs + [(target, source) for source, target...  2.49 us
  transfers between devices with their start and end apart: 8, of which 2 were waited for; matrix products, arithmetic and copies ran while one was open for 0% of the time, Pallas kernels for 8%

profile of v5, /device:TPU:1, one launch (start us, length us, event | category | flops | bytes accessed | tf_op | source)
XLA Modules:
  0.0 86.3 jit_solution(3140068007719159973)
XLA Ops:
  0.6 1.5 %shard_map.112 = (f32[16,8,128]{2,1,0:T(8,128)}, f32[4,8,128]{2,1,0:T(8,128)}, f32[4,8,128]{2,1,0:T(8,128)}) custom-call(f32[3,16,128]{2,1,0:T(8,128)} %bitcast.18, f32[3,16,128]{2,1,0:T(8,128)} %bitcast.19, f32[16,128]{1,0:T(8,128)} %bitcast.20, s32[1,16]{1,0:T(1,128)} %counts_hbm.1, s32[1,8]{1,0:T(1,128)} %refs_1_.1), custom_call_target="tpu_custom_call" | custom-call | bytes 200000 | tf_op jit(solution)/shard_map/pallas_call | solution.py:400
  2.1 0.0 copy-start.2
  2.2 21.4 %collective-permute-start = (f32[4,8,128]{2,1,0:T(8,128)}, f32[4,8,128]{2,1,0:T(8,128)S(1)}, u32[]{:S(2)}, u32[]{:S(2)}) collective-permute-start(f32[4,8,128]{2,1,0:T(8,128)} %get-tuple-element.37), channel_id=1, source_target_pairs={{8,16},{24,32},{40,48},{56,64},{72,80},{88,96},{104,112},{120,128}... | collective-permute-start | bytes 49160 | tf_op jit(solution)/shard_map/ppermute | solution.py:352
  23.6 1.9 %collective-permute-start.1 = (f32[4,8,128]{2,1,0:T(8,128)}, f32[4,8,128]{2,1,0:T(8,128)S(1)}, u32[]{:S(2)}, u32[]{:S(2)}) collective-permute-start(f32[4,8,128]{2,1,0:T(8,128)} %get-tuple-element.38), channel_id=1, source_target_pairs={{0,8},{16,24},{32,40},{48,56},{64,72},{80,88},{96,104},{112,120},{... | collective-permute-start | bytes 49160 | tf_op jit(solution)/shard_map/ppermute | solution.py:357
  25.5 0.0 copy-start.4
  25.5 0.0 copy-start.5
  25.5 0.0 copy-start.6
  25.6 0.6 copy-done.4
  26.2 0.0 copy-done.5
  26.2 0.0 copy-done.6
  26.2 0.8 copy-done
  27.0 0.6 shard_map.113
  27.7 0.6 collective-permute-done.1.inner_ref
  28.3 1.4 %shard_map.114 = (f32[4,128]{1,0:T(4,128)S(1)}, f32[4,128]{1,0:T(4,128)S(1)}, bf16[24,128,64]{2,1,0:T(8,128)(2,1)S(1)}, bf16[24,32,256]{2,1,0:T(8,128)(2,1)S(1)}) custom-call(f32[4,8,128]{2,1,0:T(8,128)S(1)} %collective-permute-done.outer_ref, f32[4,8,128]{2,1,0:T(8,128)S(1)} %collective-permute-done.1.inner_ref, ...), custom_call_target="tpu_custom_call" | custom-call | bytes 200000 | tf_op jit(solution)/shard_map/pallas_call | solution.py:381
  29.7 3.3 %collective-permute-start.2 = (f32[4,128]{1,0:T(4,128)S(1)}, f32[4,128]{1,0:T(4,128)S(1)}, u32[]{:S(2)}, u32[]{:S(2)}) collective-permute-start(f32[4,128]{1,0:T(4,128)S(1)} %get-tuple-element.43), channel_id=1, source_target_pairs={{8,16},{24,32},{40,48},{56,64},{72,80},{88,96},{104,112},{120,128}... | collective-permute-start | bytes 6152 | tf_op jit(solution)/shard_map/ppermute | solution.py:352
  33.0 1.9 %collective-permute-start.3 = (f32[4,128]{1,0:T(4,128)S(1)}, f32[4,128]{1,0:T(4,128)S(1)}, u32[]{:S(2)}, u32[]{:S(2)}) collective-permute-start(f32[4,128]{1,0:T(4,128)S(1)} %get-tuple-element.44), channel_id=1, source_target_pairs={{0,8},{16,24},{32,40},{48,56},{64,72},{80,88},{96,104},{112,120},{... | collective-permute-start | bytes 6152 | tf_op jit(solution)/shard_map/ppermute | solution.py:357
  35.0 2.7 %shard_map.115.rho_ref = f32[16,1,128]{2,1,0:T(1,128)S(1)} custom-call(s32[6,1,16]{2,1,0:T(1,128)S(1)} %get-tuple-element.35.near_ref, bf16[16,64,384]{2,1,0:T(8,128)(2,1)S(1)} %get-tuple-element.36.target_ref, bf16[24,128,64]{2,1,0:T(8,128)(2,1)S(1)} %get-tuple-element.42.source_ref), custom_call_target="tpu_custom_call" | custom-call | bytes 200000 | tf_op jit(solution)/shard_map/pallas_call | solution.py:388
  37.7 0.0 collective-permute-done.2.outer_ref
  37.7 0.0 collective-permute-done.3.inner_ref
  37.7 8.4 %shard_map.116 = (f32[16,8,128]{2,1,0:T(8,128)S(1)}, f32[8,2,8,128]{3,2,1,0:T(8,128)S(1)}) custom-call(f32[16,8,128]{2,1,0:T(8,128)S(1)} %copy-done.1, f32[16,1,128]{2,1,0:T(1,128)S(1)} %shard_map.115.rho_ref, f32[4,128]{1,0:T(4,128)S(1)} %collective-permute-done.2.outer_ref, f32[4,128]{1,0:T(4,128)S(1)} %collective-permute-done.3.inner_ref, ...), custom_call_target="tpu_custom_call" | custom-call | bytes 200000 | tf_op jit(solution)/shard_map/pallas_call | solution.py:416
  46.1 12.0 %all_to_all.5.arrived_ref = f32[8,2,8,128]{3,2,1,0:T(8,128)S(1)} all-to-all(f32[8,2,8,128]{3,2,1,0:T(8,128)S(1)} %get-tuple-element.48), channel_id=1, replica_groups=mesh['curve'=128,'group'=8] {'group'}, dimensions={0} | all-to-all | bytes 131072 | tf_op jit(solution)/shard_map/all_to_all | solution.py:424
  58.1 0.6 shard_map.117
  58.7 0.0 copy-start.3
  58.7 5.6 %collective-permute-start.4 = (f32[4,8,128]{2,1,0:T(8,128)S(1)}, f32[4,8,128]{2,1,0:T(8,128)S(1)}, u32[]{:S(2)}, u32[]{:S(2)}) collective-permute-start(f32[4,8,128]{2,1,0:T(8,128)S(1)} %get-tuple-element.53), channel_id=1, source_target_pairs={{8,16},{24,32},{40,48},{56,64},{72,80},{88,96},{104,112},{120,128}... | collective-permute-start | bytes 49160 | tf_op jit(solution)/shard_map/ppermute | solution.py:352
  64.3 1.9 %collective-permute-start.5 = (f32[4,8,128]{2,1,0:T(8,128)S(1)}, f32[4,8,128]{2,1,0:T(8,128)S(1)}, u32[]{:S(2)}, u32[]{:S(2)}) collective-permute-start(f32[4,8,128]{2,1,0:T(8,128)S(1)} %get-tuple-element.54), channel_id=1, source_target_pairs={{0,8},{16,24},{32,40},{48,56},{64,72},{80,88},{96,104},{112,120},{... | collective-permute-start | bytes 49160 | tf_op jit(solution)/shard_map/ppermute | solution.py:357
  66.2 0.6 shard_map.118
  66.9 1.9 %collective-permute-done.5.inner_ref = f32[4,8,128]{2,1,0:T(8,128)S(1)} collective-permute-done((f32[4,8,128]{2,1,0:T(8,128)S(1)}, f32[4,8,128]{2,1,0:T(8,128)S(1)}, u32[]{:S(2)}, u32[]{:S(2)}) %collective-permute-start.5) | collective-permute-done | bytes 16416 | tf_op jit(solution)/shard_map/ppermute | solution.py:357
  68.8 1.4 %shard_map.119 = (f32[4,128]{1,0:T(4,128)S(1)}, f32[4,128]{1,0:T(4,128)S(1)}, bf16[24,128,64]{2,1,0:T(8,128)(2,1)S(1)}, bf16[24,32,256]{2,1,0:T(8,128)(2,1)S(1)}) custom-call(f32[4,8,128]{2,1,0:T(8,128)S(1)} %collective-permute-done.4.outer_ref, f32[4,8,128]{2,1,0:T(8,128)S(1)} %collective-permute-done.5.inner_ref, ...), custom_call_target="tpu_custom_call" | custom-call | bytes 200000 | tf_op jit(solution)/shard_map/pallas_call | solution.py:381
  70.2 3.3 %collective-permute-start.6 = (f32[4,128]{1,0:T(4,128)S(1)}, f32[4,128]{1,0:T(4,128)S(1)}, u32[]{:S(2)}, u32[]{:S(2)}) collective-permute-start(f32[4,128]{1,0:T(4,128)S(1)} %get-tuple-element.59), channel_id=1, source_target_pairs={{8,16},{24,32},{40,48},{56,64},{72,80},{88,96},{104,112},{120,128}... | collective-permute-start | bytes 6152 | tf_op jit(solution)/shard_map/ppermute | solution.py:352
  73.5 1.9 %collective-permute-start.7 = (f32[4,128]{1,0:T(4,128)S(1)}, f32[4,128]{1,0:T(4,128)S(1)}, u32[]{:S(2)}, u32[]{:S(2)}) collective-permute-start(f32[4,128]{1,0:T(4,128)S(1)} %get-tuple-element.60), channel_id=1, source_target_pairs={{0,8},{16,24},{32,40},{48,56},{64,72},{80,88},{96,104},{112,120},{... | collective-permute-start | bytes 6152 | tf_op jit(solution)/shard_map/ppermute | solution.py:357
  75.5 2.7 %shard_map.120.rho_ref = f32[16,1,128]{2,1,0:T(1,128)S(1)} custom-call(s32[6,1,16]{2,1,0:T(1,128)S(1)} %get-tuple-element.51.near_ref, bf16[16,64,384]{2,1,0:T(8,128)(2,1)S(1)} %get-tuple-element.52.target_ref, bf16[24,128,64]{2,1,0:T(8,128)(2,1)S(1)} %get-tuple-element.58.source_ref), custom_call_target="tpu_custom_call" | custom-call | bytes 200000 | tf_op jit(solution)/shard_map/pallas_call | solution.py:388
  78.2 8.1 %shard_map.121 = (f32[3,16,128]{2,1,0:T(8,128)}, f32[3,16,128]{2,1,0:T(8,128)}, f32[16,128]{1,0:T(8,128)}) custom-call(f32[16,8,128]{2,1,0:T(8,128)S(1)} %get-tuple-element.50.table_ref, f32[16,1,128]{2,1,0:T(1,128)S(1)} %shard_map.120.rho_ref, f32[4,128]{1,0:T(4,128)S(1)} %collective-permute-done.6.outer_ref, ...), custom_call_target="tpu_custom_call" | custom-call | bytes 200000 | tf_op jit(solution)/shard_map/pallas_call | solution.py:432
  (9 shorter events, 0.0 us)
Async XLA Ops:
  2.1 23.4 %copy-start.2 = (s32[1,16,6]{1,0,2:T(1,128)S(1)}, s32[1,16,6]{1,0,2:T(1,128)}, u32[]{:S(2)}) copy-start(s32[1,16,6]{1,0,2:T(1,128)} %param.13) | copy-start | bytes 1156
  2.2 25.5 %collective-permute-start = (f32[4,8,128]{2,1,0:T(8,128)}, f32[4,8,128]{2,1,0:T(8,128)S(1)}, u32[]{:S(2)}, u32[]{:S(2)}) collective-permute-start(f32[4,8,128]{2,1,0:T(8,128)} %get-tuple-element.37), channel_id=1, source_target_pairs={{8,16},{24,32},{40,48},{56,64},{72,80},{88,96},{104,112},{120,128}... | collective-permute-start | bytes 49160 | tf_op jit(solution)/shard_map/ppermute | solution.py:352
  23.6 4.7 %collective-permute-start.1 = (f32[4,8,128]{2,1,0:T(8,128)}, f32[4,8,128]{2,1,0:T(8,128)S(1)}, u32[]{:S(2)}, u32[]{:S(2)}) collective-permute-start(f32[4,8,128]{2,1,0:T(8,128)} %get-tuple-element.38), channel_id=1, source_target_pairs={{0,8},{16,24},{32,40},{48,56},{64,72},{80,88},{96,104},{112,120},{... | collective-permute-start | bytes 49160 | tf_op jit(solution)/shard_map/ppermute | solution.py:357
  25.5 0.7 copy-start.4
  25.5 0.7 copy-start.5
  25.5 0.7 copy-start.6
  26.2 0.8 copy-start
  29.7 8.0 %collective-permute-start.2 = (f32[4,128]{1,0:T(4,128)S(1)}, f32[4,128]{1,0:T(4,128)S(1)}, u32[]{:S(2)}, u32[]{:S(2)}) collective-permute-start(f32[4,128]{1,0:T(4,128)S(1)} %get-tuple-element.43), channel_id=1, source_target_pairs={{8,16},{24,32},{40,48},{56,64},{72,80},{88,96},{104,112},{120,128}... | collective-permute-start | bytes 6152 | tf_op jit(solution)/shard_map/ppermute | solution.py:352
  33.0 4.7 %collective-permute-start.3 = (f32[4,128]{1,0:T(4,128)S(1)}, f32[4,128]{1,0:T(4,128)S(1)}, u32[]{:S(2)}, u32[]{:S(2)}) collective-permute-start(f32[4,128]{1,0:T(4,128)S(1)} %get-tuple-element.44), channel_id=1, source_target_pairs={{0,8},{16,24},{32,40},{48,56},{64,72},{80,88},{96,104},{112,120},{... | collective-permute-start | bytes 6152 | tf_op jit(solution)/shard_map/ppermute | solution.py:357
  35.0 2.8 %copy-start.1 = (f32[16,8,128]{2,1,0:T(8,128)S(1)}, f32[16,8,128]{2,1,0:T(8,128)}, u32[]{:S(2)}) copy-start(f32[16,8,128]{2,1,0:T(8,128)} %get-tuple-element.34.table_ref) | copy-start | bytes 196612
  58.7 7.5 %copy-start.3 = (s32[1,16,6]{1,0,2:T(1,128)S(1)}, s32[1,16,6]{1,0,2:T(1,128)}, u32[]{:S(2)}) copy-start(s32[1,16,6]{1,0,2:T(1,128)} %param.16) | copy-start | bytes 1156
  58.7 8.2 %collective-permute-start.4 = (f32[4,8,128]{2,1,0:T(8,128)S(1)}, f32[4,8,128]{2,1,0:T(8,128)S(1)}, u32[]{:S(2)}, u32[]{:S(2)}) collective-permute-start(f32[4,8,128]{2,1,0:T(8,128)S(1)} %get-tuple-element.53), channel_id=1, source_target_pairs={{8,16},{24,32},{40,48},{56,64},{72,80},{88,96},{104,112},{120,128}... | collective-permute-start | bytes 49160 | tf_op jit(solution)/shard_map/ppermute | solution.py:352
  64.3 4.5 %collective-permute-start.5 = (f32[4,8,128]{2,1,0:T(8,128)S(1)}, f32[4,8,128]{2,1,0:T(8,128)S(1)}, u32[]{:S(2)}, u32[]{:S(2)}) collective-permute-start(f32[4,8,128]{2,1,0:T(8,128)S(1)} %get-tuple-element.54), channel_id=1, source_target_pairs={{0,8},{16,24},{32,40},{48,56},{64,72},{80,88},{96,104},{112,120},{... | collective-permute-start | bytes 49160 | tf_op jit(solution)/shard_map/ppermute | solution.py:357
  70.2 8.0 %collective-permute-start.6 = (f32[4,128]{1,0:T(4,128)S(1)}, f32[4,128]{1,0:T(4,128)S(1)}, u32[]{:S(2)}, u32[]{:S(2)}) collective-permute-start(f32[4,128]{1,0:T(4,128)S(1)} %get-tuple-element.59), channel_id=1, source_target_pairs={{8,16},{24,32},{40,48},{56,64},{72,80},{88,96},{104,112},{120,128}... | collective-permute-start | bytes 6152 | tf_op jit(solution)/shard_map/ppermute | solution.py:352
  73.5 4.7 %collective-permute-start.7 = (f32[4,128]{1,0:T(4,128)S(1)}, f32[4,128]{1,0:T(4,128)S(1)}, u32[]{:S(2)}, u32[]{:S(2)}) collective-permute-start(f32[4,128]{1,0:T(4,128)S(1)} %get-tuple-element.60), channel_id=1, source_target_pairs={{0,8},{16,24},{32,40},{48,56},{64,72},{80,88},{96,104},{112,120},{... | collective-permute-start | bytes 6152 | tf_op jit(solution)/shard_map/ppermute | solution.py:357

commit v6 on v5

--- a/solution.py
+++ b/solution.py
@@ -201,7 +201,7 @@
         rho_ref[j] = density_of(j, target_ref, source_ref, near_ref)
         return carry
 
-    lax.fori_loop(0, BLOCKS, target, 0, unroll=2)
+    lax.fori_loop(0, BLOCKS, target, 0, unroll=16)
 
 
 def advance(
@@ -215,9 +215,8 @@
     above = jnp.where(even, inner, outer)
     flat = [rho_ref[b] for b in range(BLOCKS)] + [below, above, jnp.ones((8, LANES), F32)]
     flat = jnp.concatenate(flat, axis=0)
-    across = flat.T
     for s in range(CANDIDATES):
-        column = jnp.broadcast_to(across[:, s : s + 1], (LANES, LANES))
+        column = jnp.broadcast_to(flat[s : s + 1, :], (LANES, LANES)).T
         rho_of[s] = column
         inverse_of[s] = 1.0 / column
 
@@ -247,7 +246,7 @@
         done(j, jnp.where(rows < 3, kicked + TIME_STEP * drift, kicked))
         return carry
 
-    lax.fori_loop(0, BLOCKS, target, 0, unroll=2)
+    lax.fori_loop(0, BLOCKS, target, 0, unroll=16)
 
 
 def force_move_kernel(

time: 87.6 us -> 85 us (0.970)
  Pallas kernels: 28.1 us -> 23.7 us
  waiting for transfers between devices: 2.5 us -> 3.73 us
    pallas_call x2, Pallas kernels: 5.48 us -> 3.35 us  [half_step(): call(density_kernel, (shape(BLOCKS, 1, LANES),), [SMEM, VMEM, VMEM])]
    ppermute x4, waiting for transfers between devices: 0.01 us -> 1.2 us  [swap_outer(): lax.ppermute(item, 'curve', pairs + [(target, source) for source, target...]
    pallas_call x1, Pallas kernels: 8.11 us -> 6.94 us  [body(): call(force_out_kernel, (shape(3, BLOCKS, LANES), shape(3, BLOCKS, LANES),...]
    pallas_call x1, Pallas kernels: 8.37 us -> 7.21 us  [body(): call(force_move_kernel, (TABLE, shape(groups, MOVES, 8, LANES)), FORCE_SP...]
  transfers between devices with their start and end apart: 8 -> 8, of which waited for: 2 -> 4; matrix products, arithmetic and copies ran while one was open for 0% -> 0% of each run, Pallas kernels for 8% -> 6%
where the time goes in v6:
time: 85 us; the launch traced here: 83.7 us
  starting transfers between devices  41.5 us (49%)
  Pallas kernels  23.7 us (28%)
  blocking collectives  12.4 us (15%)
  waiting for transfers between devices  3.73 us (4%)
  local copies, waits for them, and re-layouts  1.51 us (2%)
  between operations  0.85 us (1%)
    ppermute x4, starting transfers between devices, swap_outer(): lax.ppermute(item, 'curve', pairs + [(target, source) for source, target...  33.6 us
    all_to_all x1, blocking collectives, body(): arrived = lax.all_to_all(send, 'group', 0, 0)  12.4 us
    ppermute x4, starting transfers between devices, swap_inner(): lax.ppermute(item, 'curve', pairs + [(target, source) for source, target...  7.86 us
    pallas_call x1, Pallas kernels, body(): call(force_move_kernel, (TABLE, shape(groups, MOVES, 8, LANES)), FORCE_SP...  7.21 us
    pallas_call x1, Pallas kernels, body(): call(force_out_kernel, (shape(3, BLOCKS, LANES), shape(3, BLOCKS, LANES),...  6.94 us
    pallas_call x2, Pallas kernels, half_step(): call(density_kernel, (shape(BLOCKS, 1, LANES),), [SMEM, VMEM, VMEM])  3.35 us
    pallas_call x2, Pallas kernels, half_step(): call(listed_density_kernel, (shape(HALO, LANES), shape(HALO, LANES)) + SO...  2.84 us
    ppermute x4, waiting for transfers between devices, swap_inner(): lax.ppermute(item, 'curve', pairs + [(target, source) for source, target...  2.53 us
  transfers between devices with their start and end apart: 8, of which 4 were waited for; matrix products, arithmetic and copies ran while one was open for 0% of the time, Pallas kernels for 6%

profile of v6, /device:TPU:1, one launch (start us, length us, event | category | flops | bytes accessed | tf_op | source)
XLA Modules:
  0.0 83.7 jit_solution(10479732335757821748)
XLA Ops:
  0.6 1.5 %shard_map.112 = (f32[16,8,128]{2,1,0:T(8,128)}, f32[4,8,128]{2,1,0:T(8,128)}, f32[4,8,128]{2,1,0:T(8,128)}) custom-call(f32[3,16,128]{2,1,0:T(8,128)} %bitcast.18, f32[3,16,128]{2,1,0:T(8,128)} %bitcast.19, f32[16,128]{1,0:T(8,128)} %bitcast.20, s32[1,16]{1,0:T(1,128)} %counts_hbm.1, s32[1,8]{1,0:T(1,128)} %refs_1_.1), custom_call_target="tpu_custom_call" | custom-call | bytes 200000 | tf_op jit(solution)/shard_map/pallas_call | solution.py:399
  2.1 0.0 copy-start.2
  2.2 21.4 %collective-permute-start = (f32[4,8,128]{2,1,0:T(8,128)}, f32[4,8,128]{2,1,0:T(8,128)S(1)}, u32[]{:S(2)}, u32[]{:S(2)}) collective-permute-start(f32[4,8,128]{2,1,0:T(8,128)} %get-tuple-element.37), channel_id=1, source_target_pairs={{8,16},{24,32},{40,48},{56,64},{72,80},{88,96},{104,112},{120,128}... | collective-permute-start | bytes 49160 | tf_op jit(solution)/shard_map/ppermute | solution.py:351
  23.6 1.9 %collective-permute-start.1 = (f32[4,8,128]{2,1,0:T(8,128)}, f32[4,8,128]{2,1,0:T(8,128)S(1)}, u32[]{:S(2)}, u32[]{:S(2)}) collective-permute-start(f32[4,8,128]{2,1,0:T(8,128)} %get-tuple-element.38), channel_id=1, source_target_pairs={{0,8},{16,24},{32,40},{48,56},{64,72},{80,88},{96,104},{112,120},{... | collective-permute-start | bytes 49160 | tf_op jit(solution)/shard_map/ppermute | solution.py:356
  25.5 0.0 copy-start.4
  25.5 0.0 copy-start.6
  25.6 0.6 copy-done.4
  26.2 0.0 copy-done.5
  26.2 0.0 copy-done.6
  26.2 0.8 %copy-done = f32[16,8,128]{2,1,0:T(8,128)S(1)} copy-done((f32[16,8,128]{2,1,0:T(8,128)S(1)}, f32[16,8,128]{2,1,0:T(8,128)}, u32[]{:S(2)}) %copy-start) | copy-done | bytes 65560
  27.0 0.6 shard_map.113
  27.7 0.6 collective-permute-done.1.inner_ref
  28.3 1.4 %shard_map.114 = (f32[4,128]{1,0:T(4,128)S(1)}, f32[4,128]{1,0:T(4,128)S(1)}, bf16[24,128,64]{2,1,0:T(8,128)(2,1)S(1)}, bf16[24,32,256]{2,1,0:T(8,128)(2,1)S(1)}) custom-call(f32[4,8,128]{2,1,0:T(8,128)S(1)} %collective-permute-done.outer_ref, f32[4,8,128]{2,1,0:T(8,128)S(1)} %collective-permute-done.1.inner_ref, ...), custom_call_target="tpu_custom_call" | custom-call | bytes 200000 | tf_op jit(solution)/shard_map/pallas_call | solution.py:380
  29.7 3.3 %collective-permute-start.2 = (f32[4,128]{1,0:T(4,128)S(1)}, f32[4,128]{1,0:T(4,128)S(1)}, u32[]{:S(2)}, u32[]{:S(2)}) collective-permute-start(f32[4,128]{1,0:T(4,128)S(1)} %get-tuple-element.43), channel_id=1, source_target_pairs={{8,16},{24,32},{40,48},{56,64},{72,80},{88,96},{104,112},{120,128}... | collective-permute-start | bytes 6152 | tf_op jit(solution)/shard_map/ppermute | solution.py:351
  33.0 1.9 %collective-permute-start.3 = (f32[4,128]{1,0:T(4,128)S(1)}, f32[4,128]{1,0:T(4,128)S(1)}, u32[]{:S(2)}, u32[]{:S(2)}) collective-permute-start(f32[4,128]{1,0:T(4,128)S(1)} %get-tuple-element.44), channel_id=1, source_target_pairs={{0,8},{16,24},{32,40},{48,56},{64,72},{80,88},{96,104},{112,120},{... | collective-permute-start | bytes 6152 | tf_op jit(solution)/shard_map/ppermute | solution.py:356
  35.0 1.7 %shard_map.115.rho_ref = f32[16,1,128]{2,1,0:T(1,128)S(1)} custom-call(s32[6,1,16]{2,1,0:T(1,128)S(1)} %get-tuple-element.35.near_ref, bf16[16,64,384]{2,1,0:T(8,128)(2,1)S(1)} %get-tuple-element.36.target_ref, bf16[24,128,64]{2,1,0:T(8,128)(2,1)S(1)} %get-tuple-element.42.source_ref), custom_call_target="tpu_custom_call" | custom-call | bytes 200000 | tf_op jit(solution)/shard_map/pallas_call | solution.py:387
  36.6 0.7 collective-permute-done.2.outer_ref
  37.4 7.2 %shard_map.116 = (f32[16,8,128]{2,1,0:T(8,128)S(1)}, f32[8,2,8,128]{3,2,1,0:T(8,128)S(1)}) custom-call(f32[16,8,128]{2,1,0:T(8,128)S(1)} %copy-done.1, f32[16,1,128]{2,1,0:T(1,128)S(1)} %shard_map.115.rho_ref, f32[4,128]{1,0:T(4,128)S(1)} %collective-permute-done.2.outer_ref, f32[4,128]{1,0:T(4,128)S(1)} %collective-permute-done.3.inner_ref, ...), custom_call_target="tpu_custom_call" | custom-call | bytes 200000 | tf_op jit(solution)/shard_map/pallas_call | solution.py:415
  44.6 12.4 %all_to_all.5.arrived_ref = f32[8,2,8,128]{3,2,1,0:T(8,128)S(1)} all-to-all(f32[8,2,8,128]{3,2,1,0:T(8,128)S(1)} %get-tuple-element.48), channel_id=1, replica_groups=mesh['curve'=128,'group'=8] {'group'}, dimensions={0} | all-to-all | bytes 131072 | tf_op jit(solution)/shard_map/all_to_all | solution.py:423
  57.0 0.6 shard_map.117
  57.5 0.0 copy-start.3
  57.6 5.5 %collective-permute-start.4 = (f32[4,8,128]{2,1,0:T(8,128)S(1)}, f32[4,8,128]{2,1,0:T(8,128)S(1)}, u32[]{:S(2)}, u32[]{:S(2)}) collective-permute-start(f32[4,8,128]{2,1,0:T(8,128)S(1)} %get-tuple-element.53), channel_id=1, source_target_pairs={{8,16},{24,32},{40,48},{56,64},{72,80},{88,96},{104,112},{120,128}... | collective-permute-start | bytes 49160 | tf_op jit(solution)/shard_map/ppermute | solution.py:351
  63.1 1.9 %collective-permute-start.5 = (f32[4,8,128]{2,1,0:T(8,128)S(1)}, f32[4,8,128]{2,1,0:T(8,128)S(1)}, u32[]{:S(2)}, u32[]{:S(2)}) collective-permute-start(f32[4,8,128]{2,1,0:T(8,128)S(1)} %get-tuple-element.54), channel_id=1, source_target_pairs={{0,8},{16,24},{32,40},{48,56},{64,72},{80,88},{96,104},{112,120},{... | collective-permute-start | bytes 49160 | tf_op jit(solution)/shard_map/ppermute | solution.py:356
  65.0 0.6 shard_map.118
  65.7 1.9 %collective-permute-done.5.inner_ref = f32[4,8,128]{2,1,0:T(8,128)S(1)} collective-permute-done((f32[4,8,128]{2,1,0:T(8,128)S(1)}, f32[4,8,128]{2,1,0:T(8,128)S(1)}, u32[]{:S(2)}, u32[]{:S(2)}) %collective-permute-start.5) | collective-permute-done | bytes 16416 | tf_op jit(solution)/shard_map/ppermute | solution.py:356
  67.6 1.4 %shard_map.119 = (f32[4,128]{1,0:T(4,128)S(1)}, f32[4,128]{1,0:T(4,128)S(1)}, bf16[24,128,64]{2,1,0:T(8,128)(2,1)S(1)}, bf16[24,32,256]{2,1,0:T(8,128)(2,1)S(1)}) custom-call(f32[4,8,128]{2,1,0:T(8,128)S(1)} %collective-permute-done.4.outer_ref, f32[4,8,128]{2,1,0:T(8,128)S(1)} %collective-permute-done.5.inner_ref, ...), custom_call_target="tpu_custom_call" | custom-call | bytes 200000 | tf_op jit(solution)/shard_map/pallas_call | solution.py:380
  69.0 3.4 %collective-permute-start.6 = (f32[4,128]{1,0:T(4,128)S(1)}, f32[4,128]{1,0:T(4,128)S(1)}, u32[]{:S(2)}, u32[]{:S(2)}) collective-permute-start(f32[4,128]{1,0:T(4,128)S(1)} %get-tuple-element.59), channel_id=1, source_target_pairs={{8,16},{24,32},{40,48},{56,64},{72,80},{88,96},{104,112},{120,128}... | collective-permute-start | bytes 6152 | tf_op jit(solution)/shard_map/ppermute | solution.py:351
  72.4 2.1 %collective-permute-start.7 = (f32[4,128]{1,0:T(4,128)S(1)}, f32[4,128]{1,0:T(4,128)S(1)}, u32[]{:S(2)}, u32[]{:S(2)}) collective-permute-start(f32[4,128]{1,0:T(4,128)S(1)} %get-tuple-element.60), channel_id=1, source_target_pairs={{0,8},{16,24},{32,40},{48,56},{64,72},{80,88},{96,104},{112,120},{... | collective-permute-start | bytes 6152 | tf_op jit(solution)/shard_map/ppermute | solution.py:356
  74.5 1.7 %shard_map.120.rho_ref = f32[16,1,128]{2,1,0:T(1,128)S(1)} custom-call(s32[6,1,16]{2,1,0:T(1,128)S(1)} %get-tuple-element.51.near_ref, bf16[16,64,384]{2,1,0:T(8,128)(2,1)S(1)} %get-tuple-element.52.target_ref, bf16[24,128,64]{2,1,0:T(8,128)(2,1)S(1)} %get-tuple-element.58.source_ref), custom_call_target="tpu_custom_call" | custom-call | bytes 200000 | tf_op jit(solution)/shard_map/pallas_call | solution.py:387
  76.2 0.5 collective-permute-done.6.outer_ref
  76.7 0.0 collective-permute-done.7.inner_ref
  76.7 6.9 %shard_map.121 = (f32[3,16,128]{2,1,0:T(8,128)}, f32[3,16,128]{2,1,0:T(8,128)}, f32[16,128]{1,0:T(8,128)}) custom-call(f32[16,8,128]{2,1,0:T(8,128)S(1)} %get-tuple-element.50.table_ref, f32[16,1,128]{2,1,0:T(1,128)S(1)} %shard_map.120.rho_ref, f32[4,128]{1,0:T(4,128)S(1)} %collective-permute-done.6.outer_ref, ...), custom_call_target="tpu_custom_call" | custom-call | bytes 200000 | tf_op jit(solution)/shard_map/pallas_call | solution.py:431
  (9 shorter events, 0.0 us)
Async XLA Ops:
  2.1 23.4 %copy-start.2 = (s32[1,16,6]{1,0,2:T(1,128)S(1)}, s32[1,16,6]{1,0,2:T(1,128)}, u32[]{:S(2)}) copy-start(s32[1,16,6]{1,0,2:T(1,128)} %param.13) | copy-start | bytes 1156
  2.2 25.5 %collective-permute-start = (f32[4,8,128]{2,1,0:T(8,128)}, f32[4,8,128]{2,1,0:T(8,128)S(1)}, u32[]{:S(2)}, u32[]{:S(2)}) collective-permute-start(f32[4,8,128]{2,1,0:T(8,128)} %get-tuple-element.37), channel_id=1, source_target_pairs={{8,16},{24,32},{40,48},{56,64},{72,80},{88,96},{104,112},{120,128}... | collective-permute-start | bytes 49160 | tf_op jit(solution)/shard_map/ppermute | solution.py:351
  23.6 4.7 %collective-permute-start.1 = (f32[4,8,128]{2,1,0:T(8,128)}, f32[4,8,128]{2,1,0:T(8,128)S(1)}, u32[]{:S(2)}, u32[]{:S(2)}) collective-permute-start(f32[4,8,128]{2,1,0:T(8,128)} %get-tuple-element.38), channel_id=1, source_target_pairs={{0,8},{16,24},{32,40},{48,56},{64,72},{80,88},{96,104},{112,120},{... | collective-permute-start | bytes 49160 | tf_op jit(solution)/shard_map/ppermute | solution.py:356
  25.5 0.7 copy-start.4
  25.5 0.7 copy-start.5
  25.5 0.7 copy-start.6
  26.2 0.8 %copy-start = (f32[16,8,128]{2,1,0:T(8,128)S(1)}, f32[16,8,128]{2,1,0:T(8,128)}, u32[]{:S(2)}) copy-start(f32[16,8,128]{2,1,0:T(8,128)} %get-tuple-element.34.table_ref) | copy-start | bytes 196612
  29.7 7.6 %collective-permute-start.2 = (f32[4,128]{1,0:T(4,128)S(1)}, f32[4,128]{1,0:T(4,128)S(1)}, u32[]{:S(2)}, u32[]{:S(2)}) collective-permute-start(f32[4,128]{1,0:T(4,128)S(1)} %get-tuple-element.43), channel_id=1, source_target_pairs={{8,16},{24,32},{40,48},{56,64},{72,80},{88,96},{104,112},{120,128}... | collective-permute-start | bytes 6152 | tf_op jit(solution)/shard_map/ppermute | solution.py:351
  33.0 4.3 %collective-permute-start.3 = (f32[4,128]{1,0:T(4,128)S(1)}, f32[4,128]{1,0:T(4,128)S(1)}, u32[]{:S(2)}, u32[]{:S(2)}) collective-permute-start(f32[4,128]{1,0:T(4,128)S(1)} %get-tuple-element.44), channel_id=1, source_target_pairs={{0,8},{16,24},{32,40},{48,56},{64,72},{80,88},{96,104},{112,120},{... | collective-permute-start | bytes 6152 | tf_op jit(solution)/shard_map/ppermute | solution.py:356
  35.0 2.4 %copy-start.1 = (f32[16,8,128]{2,1,0:T(8,128)S(1)}, f32[16,8,128]{2,1,0:T(8,128)}, u32[]{:S(2)}) copy-start(f32[16,8,128]{2,1,0:T(8,128)} %get-tuple-element.34.table_ref) | copy-start | bytes 196612
  57.5 7.5 %copy-start.3 = (s32[1,16,6]{1,0,2:T(1,128)S(1)}, s32[1,16,6]{1,0,2:T(1,128)}, u32[]{:S(2)}) copy-start(s32[1,16,6]{1,0,2:T(1,128)} %param.16) | copy-start | bytes 1156
  57.6 8.1 %collective-permute-start.4 = (f32[4,8,128]{2,1,0:T(8,128)S(1)}, f32[4,8,128]{2,1,0:T(8,128)S(1)}, u32[]{:S(2)}, u32[]{:S(2)}) collective-permute-start(f32[4,8,128]{2,1,0:T(8,128)S(1)} %get-tuple-element.53), channel_id=1, source_target_pairs={{8,16},{24,32},{40,48},{56,64},{72,80},{88,96},{104,112},{120,128}... | collective-permute-start | bytes 49160 | tf_op jit(solution)/shard_map/ppermute | solution.py:351
  63.1 4.5 %collective-permute-start.5 = (f32[4,8,128]{2,1,0:T(8,128)S(1)}, f32[4,8,128]{2,1,0:T(8,128)S(1)}, u32[]{:S(2)}, u32[]{:S(2)}) collective-permute-start(f32[4,8,128]{2,1,0:T(8,128)S(1)} %get-tuple-element.54), channel_id=1, source_target_pairs={{0,8},{16,24},{32,40},{48,56},{64,72},{80,88},{96,104},{112,120},{... | collective-permute-start | bytes 49160 | tf_op jit(solution)/shard_map/ppermute | solution.py:356
  69.0 7.6 %collective-permute-start.6 = (f32[4,128]{1,0:T(4,128)S(1)}, f32[4,128]{1,0:T(4,128)S(1)}, u32[]{:S(2)}, u32[]{:S(2)}) collective-permute-start(f32[4,128]{1,0:T(4,128)S(1)} %get-tuple-element.59), channel_id=1, source_target_pairs={{8,16},{24,32},{40,48},{56,64},{72,80},{88,96},{104,112},{120,128}... | collective-permute-start | bytes 6152 | tf_op jit(solution)/shard_map/ppermute | solution.py:351
  72.4 4.3 %collective-permute-start.7 = (f32[4,128]{1,0:T(4,128)S(1)}, f32[4,128]{1,0:T(4,128)S(1)}, u32[]{:S(2)}, u32[]{:S(2)}) collective-permute-start(f32[4,128]{1,0:T(4,128)S(1)} %get-tuple-element.60), channel_id=1, source_target_pairs={{0,8},{16,24},{32,40},{48,56},{64,72},{80,88},{96,104},{112,120},{... | collective-permute-start | bytes 6152 | tf_op jit(solution)/shard_map/ppermute | solution.py:356

commit v7 on v6

--- a/solution.py
+++ b/solution.py
@@ -106,7 +106,7 @@
     stacked = jnp.concatenate([high, high, high, middle, middle, low, quadratic, ones], axis=0)
     weights = split((mass * FORCE_SCALE) * jnp.where(rows < 3, local, jnp.where(rows == 3, 1.0, 0.0)))
     summed = jnp.concatenate([weights[0], weights[1], weights[2], jnp.zeros_like(local)], axis=0).astype(BF16)
-    return stacked.T.astype(BF16), jnp.concatenate([summed, summed], axis=1)
+    return stacked.T.astype(BF16), summed
 
 
 def base_of_segment():
@@ -234,9 +234,10 @@
             factor = jnp.exp2(distance) * (closing + (mine_inverse + inverse_of[s]))
             high = factor.astype(BF16)
             low = (factor - high.astype(F32)).astype(BF16)
-            wholes += [high, low]
+            wholes.append(jnp.concatenate([high, low], axis=1))
             lefts.append(sum_ref[s])
         total = jnp.dot(jnp.concatenate(lefts, axis=1), jnp.concatenate(wholes, axis=0), preferred_element_type=F32)
+        total = total[:, 0:LANES] + total[:, LANES : 2 * LANES]
         sums = total[0:8] + total[8:16] + total[16:24]
         tile = table_ref[j]
         local = local_tile(tile, base, rows)
@@ -358,11 +359,11 @@
 
 SOURCES = (
     shape(CANDIDATES, LANES, FEATURES, dtype=BF16),
-    shape(CANDIDATES, 32, 2 * LANES, dtype=BF16),
+    shape(CANDIDATES, 32, LANES, dtype=BF16),
 )
 OWN_SOURCES = (
     shape(BLOCKS, LANES, FEATURES, dtype=BF16),
-    shape(BLOCKS, 32, 2 * LANES, dtype=BF16),
+    shape(BLOCKS, 32, LANES, dtype=BF16),
 )
 
 

time: 85 us -> 82.6 us (0.972)
  Pallas kernels: 23.7 us -> 21.3 us
    pallas_call x1, Pallas kernels: 6.94 us -> 5.73 us  [body(): call(force_out_kernel, (shape(3, BLOCKS, LANES), shape(3, BLOCKS, LANES),...]
    pallas_call x1, Pallas kernels: 7.21 us -> 6.02 us  [body(): call(force_move_kernel, (TABLE, shape(groups, MOVES, 8, LANES)), FORCE_SP...]
where the time goes in v7:
time: 82.6 us; the launch traced here: 81.3 us
  starting transfers between devices  41.5 us (50%)
  Pallas kernels  21.3 us (26%)
  blocking collectives  12.4 us (15%)
  waiting for transfers between devices  3.73 us (5%)
  local copies, waits for them, and re-layouts  1.51 us (2%)
  between operations  0.85 us (1%)
    ppermute x4, starting transfers between devices, swap_outer(): lax.ppermute(item, 'curve', pairs + [(target, source) for source, target...  33.6 us
    all_to_all x1, blocking collectives, body(): arrived = lax.all_to_all(send, 'group', 0, 0)  12.4 us
    ppermute x4, starting transfers between devices, swap_inner(): lax.ppermute(item, 'curve', pairs + [(target, source) for source, target...  7.86 us
    pallas_call x1, Pallas kernels, body(): call(force_move_kernel, (TABLE, shape(groups, MOVES, 8, LANES)), FORCE_SP...  6.02 us
    pallas_call x1, Pallas kernels, body(): call(force_out_kernel, (shape(3, BLOCKS, LANES), shape(3, BLOCKS, LANES),...  5.73 us
    pallas_call x2, Pallas kernels, half_step(): call(density_kernel, (shape(BLOCKS, 1, LANES),), [SMEM, VMEM, VMEM])  3.35 us
    pallas_call x2, Pallas kernels, half_step(): call(listed_density_kernel, (shape(HALO, LANES), shape(HALO, LANES)) + SO...  2.84 us
    ppermute x4, waiting for transfers between devices, swap_inner(): lax.ppermute(item, 'curve', pairs + [(target, source) for source, target...  2.52 us
  transfers between devices with their start and end apart: 8, of which 4 were waited for; matrix products, arithmetic and copies ran while one was open for 0% of the time, Pallas kernels for 6%

profile of v7, /device:TPU:1, one launch (start us, length us, event | category | flops | bytes accessed | tf_op | source)
XLA Modules:
  0.0 81.3 jit_solution(7017213547037404399)
XLA Ops:
  0.6 1.5 %shard_map.112 = (f32[16,8,128]{2,1,0:T(8,128)}, f32[4,8,128]{2,1,0:T(8,128)}, f32[4,8,128]{2,1,0:T(8,128)}) custom-call(f32[3,16,128]{2,1,0:T(8,128)} %bitcast.18, f32[3,16,128]{2,1,0:T(8,128)} %bitcast.19, f32[16,128]{1,0:T(8,128)} %bitcast.20, s32[1,16]{1,0:T(1,128)} %counts_hbm.1, s32[1,8]{1,0:T(1,128)} %refs_1_.1), custom_call_target="tpu_custom_call" | custom-call | bytes 200000 | tf_op jit(solution)/shard_map/pallas_call | solution.py:400
  2.1 0.0 copy-start.2
  2.2 21.4 %collective-permute-start = (f32[4,8,128]{2,1,0:T(8,128)}, f32[4,8,128]{2,1,0:T(8,128)S(1)}, u32[]{:S(2)}, u32[]{:S(2)}) collective-permute-start(f32[4,8,128]{2,1,0:T(8,128)} %get-tuple-element.37), channel_id=1, source_target_pairs={{8,16},{24,32},{40,48},{56,64},{72,80},{88,96},{104,112},{120,128}... | collective-permute-start | bytes 49160 | tf_op jit(solution)/shard_map/ppermute | solution.py:352
  23.6 1.9 %collective-permute-start.1 = (f32[4,8,128]{2,1,0:T(8,128)}, f32[4,8,128]{2,1,0:T(8,128)S(1)}, u32[]{:S(2)}, u32[]{:S(2)}) collective-permute-start(f32[4,8,128]{2,1,0:T(8,128)} %get-tuple-element.38), channel_id=1, source_target_pairs={{0,8},{16,24},{32,40},{48,56},{64,72},{80,88},{96,104},{112,120},{... | collective-permute-start | bytes 49160 | tf_op jit(solution)/shard_map/ppermute | solution.py:357
  25.5 0.0 copy-start.6
  25.6 0.6 copy-done.4
  26.2 0.0 copy-done.5
  26.2 0.0 copy-done.6
  26.2 0.8 %copy-done = f32[16,8,128]{2,1,0:T(8,128)S(1)} copy-done((f32[16,8,128]{2,1,0:T(8,128)S(1)}, f32[16,8,128]{2,1,0:T(8,128)}, u32[]{:S(2)}) %copy-start) | copy-done | bytes 65560
  27.0 0.6 shard_map.113
  27.7 0.6 collective-permute-done.1.inner_ref
  28.3 1.4 %shard_map.114 = (f32[4,128]{1,0:T(4,128)S(1)}, f32[4,128]{1,0:T(4,128)S(1)}, bf16[24,128,64]{2,1,0:T(8,128)(2,1)S(1)}, bf16[24,32,128]{2,1,0:T(8,128)(2,1)S(1)}) custom-call(f32[4,8,128]{2,1,0:T(8,128)S(1)} %collective-permute-done.outer_ref, f32[4,8,128]{2,1,0:T(8,128)S(1)} %collective-permute-done.1.inner_ref, ...), custom_call_target="tpu_custom_call" | custom-call | bytes 200000 | tf_op jit(solution)/shard_map/pallas_call | solution.py:381
  29.7 3.3 %collective-permute-start.2 = (f32[4,128]{1,0:T(4,128)S(1)}, f32[4,128]{1,0:T(4,128)S(1)}, u32[]{:S(2)}, u32[]{:S(2)}) collective-permute-start(f32[4,128]{1,0:T(4,128)S(1)} %get-tuple-element.43), channel_id=1, source_target_pairs={{8,16},{24,32},{40,48},{56,64},{72,80},{88,96},{104,112},{120,128}... | collective-permute-start | bytes 6152 | tf_op jit(solution)/shard_map/ppermute | solution.py:352
  33.0 1.9 %collective-permute-start.3 = (f32[4,128]{1,0:T(4,128)S(1)}, f32[4,128]{1,0:T(4,128)S(1)}, u32[]{:S(2)}, u32[]{:S(2)}) collective-permute-start(f32[4,128]{1,0:T(4,128)S(1)} %get-tuple-element.44), channel_id=1, source_target_pairs={{0,8},{16,24},{32,40},{48,56},{64,72},{80,88},{96,104},{112,120},{... | collective-permute-start | bytes 6152 | tf_op jit(solution)/shard_map/ppermute | solution.py:357
  35.0 1.7 %shard_map.115.rho_ref = f32[16,1,128]{2,1,0:T(1,128)S(1)} custom-call(s32[6,1,16]{2,1,0:T(1,128)S(1)} %get-tuple-element.35.near_ref, bf16[16,64,384]{2,1,0:T(8,128)(2,1)S(1)} %get-tuple-element.36.target_ref, bf16[24,128,64]{2,1,0:T(8,128)(2,1)S(1)} %get-tuple-element.42.source_ref), custom_call_target="tpu_custom_call" | custom-call | bytes 200000 | tf_op jit(solution)/shard_map/pallas_call | solution.py:388
  36.7 0.7 collective-permute-done.2.outer_ref
  37.4 0.0 collective-permute-done.3.inner_ref
  37.4 6.0 %shard_map.116 = (f32[16,8,128]{2,1,0:T(8,128)S(1)}, f32[8,2,8,128]{3,2,1,0:T(8,128)S(1)}) custom-call(f32[16,8,128]{2,1,0:T(8,128)S(1)} %copy-done.1, f32[16,1,128]{2,1,0:T(1,128)S(1)} %shard_map.115.rho_ref, f32[4,128]{1,0:T(4,128)S(1)} %collective-permute-done.2.outer_ref, f32[4,128]{1,0:T(4,128)S(1)} %collective-permute-done.3.inner_ref, ...), custom_call_target="tpu_custom_call" | custom-call | bytes 200000 | tf_op jit(solution)/shard_map/pallas_call | solution.py:416
  43.4 12.4 %all_to_all.5.arrived_ref = f32[8,2,8,128]{3,2,1,0:T(8,128)S(1)} all-to-all(f32[8,2,8,128]{3,2,1,0:T(8,128)S(1)} %get-tuple-element.48), channel_id=1, replica_groups=mesh['curve'=128,'group'=8] {'group'}, dimensions={0} | all-to-all | bytes 131072 | tf_op jit(solution)/shard_map/all_to_all | solution.py:424
  55.8 0.6 shard_map.117
  56.4 0.0 copy-start.3
  56.4 5.6 %collective-permute-start.4 = (f32[4,8,128]{2,1,0:T(8,128)S(1)}, f32[4,8,128]{2,1,0:T(8,128)S(1)}, u32[]{:S(2)}, u32[]{:S(2)}) collective-permute-start(f32[4,8,128]{2,1,0:T(8,128)S(1)} %get-tuple-element.53), channel_id=1, source_target_pairs={{8,16},{24,32},{40,48},{56,64},{72,80},{88,96},{104,112},{120,128}... | collective-permute-start | bytes 49160 | tf_op jit(solution)/shard_map/ppermute | solution.py:352
  61.9 1.9 %collective-permute-start.5 = (f32[4,8,128]{2,1,0:T(8,128)S(1)}, f32[4,8,128]{2,1,0:T(8,128)S(1)}, u32[]{:S(2)}, u32[]{:S(2)}) collective-permute-start(f32[4,8,128]{2,1,0:T(8,128)S(1)} %get-tuple-element.54), channel_id=1, source_target_pairs={{0,8},{16,24},{32,40},{48,56},{64,72},{80,88},{96,104},{112,120},{... | collective-permute-start | bytes 49160 | tf_op jit(solution)/shard_map/ppermute | solution.py:357
  63.9 0.6 shard_map.118
  64.5 1.9 %collective-permute-done.5.inner_ref = f32[4,8,128]{2,1,0:T(8,128)S(1)} collective-permute-done((f32[4,8,128]{2,1,0:T(8,128)S(1)}, f32[4,8,128]{2,1,0:T(8,128)S(1)}, u32[]{:S(2)}, u32[]{:S(2)}) %collective-permute-start.5) | collective-permute-done | bytes 16416 | tf_op jit(solution)/shard_map/ppermute | solution.py:357
  66.4 1.4 %shard_map.119 = (f32[4,128]{1,0:T(4,128)S(1)}, f32[4,128]{1,0:T(4,128)S(1)}, bf16[24,128,64]{2,1,0:T(8,128)(2,1)S(1)}, bf16[24,32,128]{2,1,0:T(8,128)(2,1)S(1)}) custom-call(f32[4,8,128]{2,1,0:T(8,128)S(1)} %collective-permute-done.4.outer_ref, f32[4,8,128]{2,1,0:T(8,128)S(1)} %collective-permute-done.5.inner_ref, ...), custom_call_target="tpu_custom_call" | custom-call | bytes 200000 | tf_op jit(solution)/shard_map/pallas_call | solution.py:381
  67.8 3.3 %collective-permute-start.6 = (f32[4,128]{1,0:T(4,128)S(1)}, f32[4,128]{1,0:T(4,128)S(1)}, u32[]{:S(2)}, u32[]{:S(2)}) collective-permute-start(f32[4,128]{1,0:T(4,128)S(1)} %get-tuple-element.59), channel_id=1, source_target_pairs={{8,16},{24,32},{40,48},{56,64},{72,80},{88,96},{104,112},{120,128}... | collective-permute-start | bytes 6152 | tf_op jit(solution)/shard_map/ppermute | solution.py:352
  71.2 2.1 %collective-permute-start.7 = (f32[4,128]{1,0:T(4,128)S(1)}, f32[4,128]{1,0:T(4,128)S(1)}, u32[]{:S(2)}, u32[]{:S(2)}) collective-permute-start(f32[4,128]{1,0:T(4,128)S(1)} %get-tuple-element.60), channel_id=1, source_target_pairs={{0,8},{16,24},{32,40},{48,56},{64,72},{80,88},{96,104},{112,120},{... | collective-permute-start | bytes 6152 | tf_op jit(solution)/shard_map/ppermute | solution.py:357
  73.3 1.7 %shard_map.120.rho_ref = f32[16,1,128]{2,1,0:T(1,128)S(1)} custom-call(s32[6,1,16]{2,1,0:T(1,128)S(1)} %get-tuple-element.51.near_ref, bf16[16,64,384]{2,1,0:T(8,128)(2,1)S(1)} %get-tuple-element.52.target_ref, bf16[24,128,64]{2,1,0:T(8,128)(2,1)S(1)} %get-tuple-element.58.source_ref), custom_call_target="tpu_custom_call" | custom-call | bytes 200000 | tf_op jit(solution)/shard_map/pallas_call | solution.py:388
  75.0 0.5 collective-permute-done.6.outer_ref
  75.5 0.0 collective-permute-done.7.inner_ref
  75.5 5.7 %shard_map.121 = (f32[3,16,128]{2,1,0:T(8,128)}, f32[3,16,128]{2,1,0:T(8,128)}, f32[16,128]{1,0:T(8,128)}) custom-call(f32[16,8,128]{2,1,0:T(8,128)S(1)} %get-tuple-element.50.table_ref, f32[16,1,128]{2,1,0:T(1,128)S(1)} %shard_map.120.rho_ref, f32[4,128]{1,0:T(4,128)S(1)} %collective-permute-done.6.outer_ref, ...), custom_call_target="tpu_custom_call" | custom-call | bytes 200000 | tf_op jit(solution)/shard_map/pallas_call | solution.py:432
  (9 shorter events, 0.0 us)
Async XLA Ops:
  2.1 23.4 %copy-start.2 = (s32[1,16,6]{1,0,2:T(1,128)S(1)}, s32[1,16,6]{1,0,2:T(1,128)}, u32[]{:S(2)}) copy-start(s32[1,16,6]{1,0,2:T(1,128)} %param.13) | copy-start | bytes 1156
  2.2 25.5 %collective-permute-start = (f32[4,8,128]{2,1,0:T(8,128)}, f32[4,8,128]{2,1,0:T(8,128)S(1)}, u32[]{:S(2)}, u32[]{:S(2)}) collective-permute-start(f32[4,8,128]{2,1,0:T(8,128)} %get-tuple-element.37), channel_id=1, source_target_pairs={{8,16},{24,32},{40,48},{56,64},{72,80},{88,96},{104,112},{120,128}... | collective-permute-start | bytes 49160 | tf_op jit(solution)/shard_map/ppermute | solution.py:352
  23.6 4.7 %collective-permute-start.1 = (f32[4,8,128]{2,1,0:T(8,128)}, f32[4,8,128]{2,1,0:T(8,128)S(1)}, u32[]{:S(2)}, u32[]{:S(2)}) collective-permute-start(f32[4,8,128]{2,1,0:T(8,128)} %get-tuple-element.38), channel_id=1, source_target_pairs={{0,8},{16,24},{32,40},{48,56},{64,72},{80,88},{96,104},{112,120},{... | collective-permute-start | bytes 49160 | tf_op jit(solution)/shard_map/ppermute | solution.py:357
  25.5 0.7 copy-start.4
  25.5 0.7 copy-start.5
  25.5 0.7 copy-start.6
  26.2 0.8 %copy-start = (f32[16,8,128]{2,1,0:T(8,128)S(1)}, f32[16,8,128]{2,1,0:T(8,128)}, u32[]{:S(2)}) copy-start(f32[16,8,128]{2,1,0:T(8,128)} %get-tuple-element.34.table_ref) | copy-start | bytes 196612
  29.7 7.6 %collective-permute-start.2 = (f32[4,128]{1,0:T(4,128)S(1)}, f32[4,128]{1,0:T(4,128)S(1)}, u32[]{:S(2)}, u32[]{:S(2)}) collective-permute-start(f32[4,128]{1,0:T(4,128)S(1)} %get-tuple-element.43), channel_id=1, source_target_pairs={{8,16},{24,32},{40,48},{56,64},{72,80},{88,96},{104,112},{120,128}... | collective-permute-start | bytes 6152 | tf_op jit(solution)/shard_map/ppermute | solution.py:352
  33.0 4.3 %collective-permute-start.3 = (f32[4,128]{1,0:T(4,128)S(1)}, f32[4,128]{1,0:T(4,128)S(1)}, u32[]{:S(2)}, u32[]{:S(2)}) collective-permute-start(f32[4,128]{1,0:T(4,128)S(1)} %get-tuple-element.44), channel_id=1, source_target_pairs={{0,8},{16,24},{32,40},{48,56},{64,72},{80,88},{96,104},{112,120},{... | collective-permute-start | bytes 6152 | tf_op jit(solution)/shard_map/ppermute | solution.py:357
  35.0 2.4 %copy-start.1 = (f32[16,8,128]{2,1,0:T(8,128)S(1)}, f32[16,8,128]{2,1,0:T(8,128)}, u32[]{:S(2)}) copy-start(f32[16,8,128]{2,1,0:T(8,128)} %get-tuple-element.34.table_ref) | copy-start | bytes 196612
  56.4 7.5 %copy-start.3 = (s32[1,16,6]{1,0,2:T(1,128)S(1)}, s32[1,16,6]{1,0,2:T(1,128)}, u32[]{:S(2)}) copy-start(s32[1,16,6]{1,0,2:T(1,128)} %param.16) | copy-start | bytes 1156
  56.4 8.1 %collective-permute-start.4 = (f32[4,8,128]{2,1,0:T(8,128)S(1)}, f32[4,8,128]{2,1,0:T(8,128)S(1)}, u32[]{:S(2)}, u32[]{:S(2)}) collective-permute-start(f32[4,8,128]{2,1,0:T(8,128)S(1)} %get-tuple-element.53), channel_id=1, source_target_pairs={{8,16},{24,32},{40,48},{56,64},{72,80},{88,96},{104,112},{120,128}... | collective-permute-start | bytes 49160 | tf_op jit(solution)/shard_map/ppermute | solution.py:352
  61.9 4.5 %collective-permute-start.5 = (f32[4,8,128]{2,1,0:T(8,128)S(1)}, f32[4,8,128]{2,1,0:T(8,128)S(1)}, u32[]{:S(2)}, u32[]{:S(2)}) collective-permute-start(f32[4,8,128]{2,1,0:T(8,128)S(1)} %get-tuple-element.54), channel_id=1, source_target_pairs={{0,8},{16,24},{32,40},{48,56},{64,72},{80,88},{96,104},{112,120},{... | collective-permute-start | bytes 49160 | tf_op jit(solution)/shard_map/ppermute | solution.py:357
  67.8 7.6 %collective-permute-start.6 = (f32[4,128]{1,0:T(4,128)S(1)}, f32[4,128]{1,0:T(4,128)S(1)}, u32[]{:S(2)}, u32[]{:S(2)}) collective-permute-start(f32[4,128]{1,0:T(4,128)S(1)} %get-tuple-element.59), channel_id=1, source_target_pairs={{8,16},{24,32},{40,48},{56,64},{72,80},{88,96},{104,112},{120,128}... | collective-permute-start | bytes 6152 | tf_op jit(solution)/shard_map/ppermute | solution.py:352
  71.2 4.3 %collective-permute-start.7 = (f32[4,128]{1,0:T(4,128)S(1)}, f32[4,128]{1,0:T(4,128)S(1)}, u32[]{:S(2)}, u32[]{:S(2)}) collective-permute-start(f32[4,128]{1,0:T(4,128)S(1)} %get-tuple-element.60), channel_id=1, source_target_pairs={{0,8},{16,24},{32,40},{48,56},{64,72},{80,88},{96,104},{112,120},{... | collective-permute-start | bytes 6152 | tf_op jit(solution)/shard_map/ppermute | solution.py:357
